TPU v7x, 32 devices: a whole 2x2x4 slice. The times are simulated.
32 devices in a mesh: group: 2 (over y), seq: 4 (over z), fsdp: 4 (over x, core).
Axes of the slice: x: 2, y: 2, z: 4, core: 2. Of those that a mesh axis runs over, the one named last changes fastest.
Arguments:
- tile_patches: bfloat16 [64, 256, 1536], P(('group', 'seq', 'fsdp')), parts along dimension 0, may hold values from -6 to 6
- vit_gain: float32 [1536], replicated, may hold values from 0.25 to 1.75
- w_query: bfloat16 [1536, 768], P('fsdp'), may hold values from -0.15625 to 0.15625
- w_key: bfloat16 [1536, 768], P('fsdp'), may hold values from -0.15625 to 0.15625
- w_value: bfloat16 [1536, 768], P('fsdp'), may hold values from -0.15625 to 0.15625
- w_out: bfloat16 [768, 1536], P('fsdp'), may hold values from -0.21875 to 0.21875
- w_proj: bfloat16 [1536, 768], P('fsdp'), may hold values from -0.15625 to 0.15625
- long_gain: float32 [768], replicated, may hold values from 0.25 to 1.75
- long_query: bfloat16 [768, 768], P(None, 'fsdp'), may hold values from -0.21875 to 0.21875
- long_key: bfloat16 [768, 768], P(None, 'fsdp'), may hold values from -0.21875 to 0.21875
- long_value: bfloat16 [768, 768], P(None, 'fsdp'), may hold values from -0.21875 to 0.21875
- long_out: bfloat16 [768, 768], P('fsdp'), may hold values from -0.21875 to 0.21875
- seq_order: int32 [64], P(('group', 'seq', 'fsdp')), parts along dimension 0, may hold values from 0 to 31, each once
- counts: int32 [32], P(('group', 'seq', 'fsdp')), parts along dimension 0, may hold values from 1 to 2
Outputs:
- encoded: bfloat16 [64, 768], P(('group', 'seq'), 'fsdp'), parts along dimension 0
There are 2 independent parts, one for each index of `group`. A program takes and returns all parts, laid end to end along the dimension named above; an argument that names none is the same for every part. Nothing has to cross between parts.
Inputs may be any that keep to these rules, and one draw needn't show every extreme that they name: `seq_order`: each of the 32 sequence positions belongs to exactly one tile. In each block of 2 consecutive tiles the first counts tiles are tissue.
All inputs are finite; a program needn't handle non-finite values.
Results may differ from a plain program's by a relative error of at most 0.013.
Values may be sent and summed in bfloat16 or wider, within the bound.
No kernel may reach another device: no remote copies, remote signals or barrier semaphores. Data moves between devices by JAX's collectives and lax.ppermute only.
A program may use at most 64 MiB of HBM per device.

v0:
```python
import functools
import math

import jax
import jax.numpy as jnp
from jax import lax
from jax.experimental import pallas as pl
from jax.experimental.pallas import tpu as pltpu
from jax.sharding import PartitionSpec as P


VHD = 64
HEADS = 16
DILATION_STEP = 4
EPSILON = 1e-06
LANES = 128


BF16 = jnp.bfloat16
F32 = jnp.float32


def other(index, step, size):
    return index ^ step if size & (size - 1) == 0 else (index + step) % size


def source(index, step, size):
    return index ^ step if size & (size - 1) == 0 else (index + size - step) % size


def swap(array, axis, step):
    size = lax.axis_size(axis)
    return lax.ppermute(array, axis, [(i, other(i, step, size)) for i in range(size)])


def spread(array, axis):
    return [array] + [swap(array, axis, step) for step in range(1, lax.axis_size(axis))]


def deal(arrays, axis):
    return [arrays[0]] + [swap(arrays[step], axis, step) for step in range(1, len(arrays))]


def normalise(rows, gain):
    average = jnp.mean(rows, axis=-1, keepdims=True)
    centred = rows - average
    variance = jnp.mean(centred * centred, axis=-1, keepdims=True)
    return (centred * lax.rsqrt(variance + EPSILON) * gain).astype(BF16)


def contract(left, right, left_axis, right_axis):
    return lax.dot_general(
        left, right, (((left_axis,), (right_axis,)), ((), ())), preferred_element_type=F32
    )


def in_hbm(array):
    return pltpu.with_memory_space_constraint(array, pltpu.HBM)


def call(body, outs, scratch=(), limit=1 << 23, specs=()):
    smem, vmem = pl.BlockSpec(memory_space=pltpu.SMEM), pl.BlockSpec(memory_space=pltpu.VMEM)

    def run(place, *arrays):
        last = len(arrays) - len(specs)
        return pl.pallas_call(
            body,
            out_shape=outs,
            in_specs=[smem] + [vmem] * last + [pl.BlockSpec(memory_space=m) for m in specs],
            out_specs=jax.tree.map(lambda _: vmem, outs),
            scratch_shapes=list(scratch),
            compiler_params=pltpu.CompilerParams(vmem_limit_bytes=limit),
        )(place, *arrays)

    return run


def head_kernel(tokens, out):
    for tile in range(tokens.shape[0]):
        out[tile : tile + 1, :] = tokens[tile, 0:1, :]


def notes_kernel(size, place, order, counts, after, out, rows):
    me = place[0] % size
    tiles = order.shape[0]
    lane = lax.broadcasted_iota(jnp.int32, (1, LANES), 1)
    rows[...] = jnp.zeros_like(rows)
    for tile in range(tiles):
        spot = order[tile]
        present = (counts[0] > tile).astype(jnp.int32)
        high = jnp.where(lane == 0, spot // 256, 0)
        low = jnp.where(lane == 1, spot % 256, 0)
        notes = high + low + jnp.where(lane == 2, present, 0)
        rows[me, tile : tile + 1, :] = notes.astype(F32)
    out[...] = rows[...].reshape(size * tiles, LANES).astype(BF16)


def query_kernel(size, place, *refs):
    heads_in, (gain, weight, out, first, rows, blocks) = refs[:size], refs[size:]
    me = place[0] % size
    tiles, width = heads_in[0].shape
    mine = weight.shape[0]
    for step in range(size):
        rows[source(me, step, size)] = heads_in[step][...].astype(F32)
    full = rows[...].reshape(size * tiles, width)
    for block in range(size):
        blocks[block] = full[:, block * mine : (block + 1) * mine]
    first[...] = blocks[me]
    normed = normalise(full, gain[...]).astype(F32)
    for block in range(size):
        blocks[block] = normed[:, block * mine : (block + 1) * mine]
    out[...] = contract(blocks[me].astype(BF16), weight[...], 1, 0).astype(BF16)


def grouped(shape, axis, span):
    return lax.broadcasted_iota(jnp.int32, shape, axis) // span


def own_head(shape, heads):
    row = lax.broadcasted_iota(jnp.int32, shape, 0) % heads
    return row == grouped(shape, 1, VHD)


def fold_kernel(size, heads, place, *refs):
    parts, weight, outs, folded = refs[:size], refs[size], refs[size + 1 : -1], refs[-1]
    me = place[0] % size
    total = parts[0][...].astype(F32)
    for step in range(1, size):
        total = total + parts[step][...].astype(F32)
    count, _ = total.shape
    spots = (count * heads, count)
    repeat = grouped(spots, 0, heads) == lax.broadcasted_iota(jnp.int32, spots, 1)
    repeated = contract(repeat.astype(F32).astype(BF16), total.astype(BF16), 1, 0)
    blocked = jnp.where(own_head(repeated.shape, heads), repeated, 0.0).astype(BF16)
    folded[...] = contract(blocked, weight[...], 1, 1).astype(BF16).reshape(folded.shape)
    for step in range(size):
        outs[step][...] = folded[other(me, step, size)]


def cut_kernel(size, place, weight, after, *refs):
    outs, blocks = refs[:-1], refs[-1]
    me = place[0] % size
    mine = weight.shape[1] // size
    for block in range(size):
        blocks[block] = weight[:, block * mine : (block + 1) * mine]
    for step in range(size):
        outs[step][...] = blocks[other(me, step, size)]


def token_kernel(size, heads, place, *refs):
    parts, normed, outs, (blocks, folded) = (
        refs[:size],
        refs[size],
        refs[size + 1 : -2],
        refs[-2:],
    )
    me = place[0] % size
    rows = parts[0].shape[1]
    for step in range(size):
        blocks[source(me, step, size)] = parts[step][...]
    for block in range(size):
        folded[:, block * rows : (block + 1) * rows] = blocks[block]
    tiles, patches, width = normed.shape
    tokens = normed[...].reshape(tiles * patches, width)
    scores = contract(folded[...], tokens, 1, 1) / math.sqrt(VHD)
    same = grouped(scores.shape, 0, heads) == grouped(scores.shape, 1, patches)
    lifted = jnp.where(same, jnp.exp(scores), 0.0)
    probs = (lifted / jnp.sum(lifted, axis=-1, keepdims=True)).astype(BF16)
    mixed = contract(probs, tokens, 1, 0).astype(BF16)
    for block in range(size):
        blocks[block] = mixed[:, block * rows : (block + 1) * rows]
    for step in range(size):
        outs[step][...] = blocks[other(me, step, size)]


def value_kernel(size, heads, place, *refs):
    parts, (weight, out, mixed) = refs[:size], refs[size:]
    me = place[0] % size
    for step in range(size):
        mixed[source(me, step, size)] = parts[step][...]
    rows = mixed[...].reshape(size * parts[0].shape[0], parts[0].shape[1])
    product = contract(rows, weight[...], 1, 0)
    kept = jnp.where(own_head(product.shape, heads), product, 0.0).astype(BF16)
    spots = (out.shape[0], product.shape[0])
    collect = lax.broadcasted_iota(jnp.int32, spots, 0) == grouped(spots, 1, heads)
    out[...] = contract(collect.astype(F32).astype(BF16), kept, 1, 0).astype(BF16)


def embed_kernel(size, place, *refs):
    parts, blocks, (first, project, notes, out, weight) = (
        refs[:size],
        refs[size : 2 * size],
        refs[2 * size :],
    )
    me = place[0] % size
    total = parts[0][...].astype(F32)
    for step in range(1, size):
        total = total + parts[step][...].astype(F32)
    pooled = total.astype(BF16)
    depth = blocks[0].shape[0]
    for step in range(size):
        start = pl.multiple_of(source(me, step, size) * depth, 16)
        weight[pl.ds(start, depth), :] = blocks[step][...]
    class_row = (first[...] + contract(pooled, weight[...], 1, 0)).astype(BF16)
    width = project.shape[1]
    out[:, :width] = contract(class_row, project[...], 1, 0).astype(BF16)
    out[:, width:] = notes[...]


def gather_kernel(*refs):
    parts, out = refs[1:-1], refs[-1]
    total = parts[0][...].astype(F32)
    for part in parts[1:]:
        total = total + part[...].astype(F32)
    width = total.shape[1] - LANES
    there = total[:, width + 2 : width + 3] > 0
    out[:, :width] = jnp.where(there, total[:, :width], 0.0).astype(BF16)
    out[:, width:] = total[:, width:].astype(BF16)


def along_lanes(column):
    shape = (column.shape[0], column.shape[0])
    here = lax.broadcasted_iota(jnp.int32, shape, 0) == lax.broadcasted_iota(jnp.int32, shape, 1)
    return jnp.sum(jnp.where(here, column, 0.0), axis=0, keepdims=True)


def slide_kernel(size, seq_size, place, *refs):
    parts = refs[:seq_size]
    gain, w_query, w_key, w_value = refs[seq_size : seq_size + 4]
    w_out, outs = refs[seq_size + 4 : seq_size + 4 + size], refs[seq_size + 4 + size :]
    me, seq = place[0] % size, place[0] // size
    rows = parts[0].shape[0]
    model = gain.shape[1]
    width = w_query.shape[0]
    total = rows * seq_size
    segment = total // 4
    tiles = jnp.concatenate([part[...].astype(F32) for part in parts], axis=0)
    notes = tiles[:, model:]
    position = along_lanes(notes[:, 0:1] * 256.0 + notes[:, 1:2]).astype(jnp.int32)
    here = along_lanes(notes[:, 2:3])
    normed = normalise(tiles[:, :model], gain[...])
    keys = contract(normed, w_key[...], 1, 1).astype(BF16)
    values = contract(normed, w_value[...], 1, 1).astype(BF16)
    asked = seq * rows + lax.broadcasted_iota(jnp.int32, (rows, total), 0)
    picker = jnp.where(asked == position, 1.0, 0.0).astype(BF16)
    mine = contract(picker, normed, 1, 0).astype(BF16)
    queries = contract(mine, w_query[...], 1, 1).astype(BF16).astype(F32)
    head_size = model // HEADS
    count = width // head_size
    shape = (count, rows, width)
    own = grouped(shape, 2, head_size) == lax.broadcasted_iota(jnp.int32, shape, 0)
    blocked = jnp.where(own, jnp.broadcast_to(queries[None], shape), 0.0)
    blocked = blocked.reshape(count * rows, width).astype(BF16)
    scores = contract(blocked, keys, 1, 1) / math.sqrt(head_size)
    line = lax.broadcasted_iota(jnp.int32, (count * rows, total), 0)
    asking = seq * rows + line % rows
    shift = (me * count + line // rows) % DILATION_STEP
    allowed = (here > 0) | (asking == position)
    near = (asking // segment == position // segment) & allowed
    far = (asking % DILATION_STEP == shift) & (position % DILATION_STEP == shift) & allowed
    times = jnp.where(near, 1.0, 0.0) + jnp.where(far, 1.0, 0.0)
    lifted = jnp.where(times > 0, jnp.exp(scores), 0.0)
    bottom = jnp.sum(lifted * times, axis=-1, keepdims=True)
    weights = (lifted.astype(BF16).astype(F32) * times).astype(BF16)
    mixed = (contract(weights, values, 1, 0) / bottom).reshape(shape)
    attended = jnp.sum(jnp.where(own, mixed, 0.0), axis=0).astype(BF16)
    for step in range(size):
        outs[step][...] = contract(attended, w_out[step][...], 1, 0).astype(BF16)


def residual_kernel(size, seq_size, place, *refs):
    parts, (after, out, blocks) = refs[:seq_size], refs[seq_size:]
    me, seq = place[0] % size, place[0] // size
    rows, width = out.shape
    total = rows * seq_size
    tiles = jnp.concatenate([part[...].astype(F32) for part in parts], axis=0)
    notes = tiles[:, size * width :]
    position = along_lanes(notes[:, 0:1] * 256.0 + notes[:, 1:2]).astype(jnp.int32)
    asked = seq * rows + lax.broadcasted_iota(jnp.int32, (rows, total), 0)
    picker = jnp.where(asked == position, 1.0, 0.0).astype(BF16)
    mine = contract(picker, tiles[:, : size * width].astype(BF16), 1, 0)
    for block in range(size):
        blocks[block] = mine[:, block * width : (block + 1) * width]
    out[...] = blocks[me]


def local(
    tile_patches,
    vit_gain,
    w_query,
    w_key,
    w_value,
    w_out,
    w_proj,
    long_gain,
    long_query,
    long_key,
    long_value,
    long_out,
    seq_order,
    counts,
):
    size = lax.axis_size("fsdp")
    seq_size = lax.axis_size("seq")
    me = lax.axis_index("fsdp")
    place = (lax.axis_index("seq") * size + me).astype(jnp.int32).reshape(1)
    tiles, _, width = tile_patches.shape
    vit_width = w_key.shape[1]
    heads = vit_width // VHD
    rows = w_key.shape[0]
    model = w_proj.shape[1]
    count = tiles * size

    head_row = pl.pallas_call(
        head_kernel,
        out_shape=jax.ShapeDtypeStruct((tiles, width), BF16),
        grid=(1,),
        in_specs=[pl.BlockSpec((tiles, 8, width), lambda i: (0, 0, 0))],
        out_specs=pl.BlockSpec(memory_space=pltpu.VMEM),
        compiler_params=pltpu.CompilerParams(vmem_limit_bytes=1 << 20),
        name="head",
    )(in_hbm(tile_patches))
    head_rows = spread(head_row, "fsdp")
    notes = call(
        functools.partial(notes_kernel, size),
        jax.ShapeDtypeStruct((count, LANES), BF16),
        [pltpu.VMEM((size, tiles, LANES), F32)],
        specs=[pltpu.SMEM, pltpu.SMEM, pl.ANY],
    )(place, seq_order, counts, head_row)

    def cut(weight, after):
        shape = (weight.shape[0], weight.shape[1] // size)
        return call(
            functools.partial(cut_kernel, size),
            [jax.ShapeDtypeStruct(shape, BF16)] * size,
            [pltpu.VMEM((size, *shape), BF16)],
            specs=[pl.ANY],
        )(place, weight, after)

    out_blocks = deal(cut(w_out, head_row), "fsdp")

    normed = normalise(tile_patches.astype(F32), vit_gain)

    gain_row = vit_gain[None, :]
    query_part, first = call(
        functools.partial(query_kernel, size),
        [
            jax.ShapeDtypeStruct((count, vit_width), BF16),
            jax.ShapeDtypeStruct((count, rows), F32),
        ],
        [pltpu.VMEM((size, tiles, width), F32), pltpu.VMEM((size, count, rows), F32)],
    )(place, *head_rows, gain_row, w_query)
    query_parts = spread(query_part, "fsdp")

    block = jax.ShapeDtypeStruct((tiles * heads, rows), BF16)
    folded = call(
        functools.partial(fold_kernel, size, heads),
        [block] * size,
        [pltpu.VMEM((size, tiles * heads, rows), BF16)],
    )(place, *query_parts, w_key)
    folded = deal(folded, "fsdp")

    mixed = call(
        functools.partial(token_kernel, size, heads),
        [block] * size,
        [pltpu.VMEM((size, tiles * heads, rows), BF16), pltpu.VMEM((tiles * heads, width), BF16)],
    )(place, *folded, normed)
    mixed = deal(mixed, "fsdp")

    pooled_part = call(
        functools.partial(value_kernel, size, heads),
        jax.ShapeDtypeStruct((count, vit_width), BF16),
        [pltpu.VMEM((size, tiles * heads, rows), BF16)],
    )(place, *mixed, w_value)
    pooled_parts = spread(pooled_part, "fsdp")

    embed_part = call(
        functools.partial(embed_kernel, size),
        jax.ShapeDtypeStruct((count, model + LANES), BF16),
        [pltpu.VMEM((vit_width, width // size), BF16)],
    )(place, *pooled_parts, *out_blocks, first, w_proj, notes)
    embed_parts = spread(embed_part, "fsdp")

    group_tiles = call(
        gather_kernel, jax.ShapeDtypeStruct((count, model + LANES), BF16)
    )(place, *embed_parts)
    all_tiles = spread(group_tiles, "seq")

    head_width = long_query.shape[1]
    long_blocks = cut(long_out, pooled_part)
    block = jax.ShapeDtypeStruct((count, head_width), BF16)
    terms = call(functools.partial(slide_kernel, size, seq_size), [block] * size)(
        place,
        *all_tiles,
        long_gain[None, :],
        jnp.transpose(long_query),
        jnp.transpose(long_key),
        jnp.transpose(long_value),
        *long_blocks,
    )
    residual = call(
        functools.partial(residual_kernel, size, seq_size),
        jax.ShapeDtypeStruct((count, head_width), F32),
        [pltpu.VMEM((size, count, head_width), F32)],
        specs=[pl.ANY],
    )(place, *all_tiles, terms[0])
    terms = deal(terms, "fsdp")
    summed = terms[0].astype(F32)
    for step in range(1, size):
        summed = summed + terms[step].astype(F32)
    return (residual + summed).astype(BF16)


def solution(mesh):
    return jax.shard_map(
        local,
        mesh=mesh,
        in_specs=(
            P(("group", "seq", "fsdp"), None, None),
            P(),
            P("fsdp", None),
            P("fsdp", None),
            P("fsdp", None),
            P("fsdp", None),
            P("fsdp", None),
            P(),
            P(None, "fsdp"),
            P(None, "fsdp"),
            P(None, "fsdp"),
            P("fsdp", None),
            P(("group", "seq", "fsdp")),
            P(("group", "seq", "fsdp")),
        ),
        out_specs=P(("group", "seq"), "fsdp"),
        check_vma=False,
    )
```

profile of v0, /device:TPU:0, one launch (start us, length us, event | category | flops | bytes accessed | tf_op | source)
XLA Modules:
  0.0 48.0 jit_solution(3998885516126355870)
XLA Ops:
  0.0 1.0 %head.1.refs_0_.after = bf16[2,1536]{1,0:T(2,128)(2,1)S(1)} custom-call(bf16[2,256,1536]{2,1,0:T(8,128)(2,1)} %tokens.1), custom_call_target="tpu_custom_call" | custom-call | tf_op jit(solution)/shard_map/head/pallas_call | solution.py:314
  1.0 0.6 %collective-permute-start = (bf16[2,1536]{1,0:T(2,128)(2,1)S(1)}, bf16[2,1536]{1,0:T(2,128)(2,1)S(1)}, u32[]{:S(2)}, u32[]{:S(2)}) collective-permute-start(bf16[2,1536]{1,0:T(2,128)(2,1)S(1)} %head.1.refs_0_.after), channel_id=1, source_target_pairs={{0,1},{1,0},{2,3},{3,2},{4,5},{5,4},{6,7},{7,6},{8,9},{9,8},{10,11... | collective-permute-start | bytes 18440 | tf_op jit(solution)/shard_map/ppermute | solution.py:33
  1.5 2.6 %collective-permute-start.1 = (bf16[2,1536]{1,0:T(2,128)(2,1)S(1)}, bf16[2,1536]{1,0:T(2,128)(2,1)S(1)}, u32[]{:S(2)}, u32[]{:S(2)}) collective-permute-start(bf16[2,1536]{1,0:T(2,128)(2,1)S(1)} %head.1.refs_0_.after), channel_id=1, source_target_pairs={{0,2},{1,3},{2,0},{3,1},{4,6},{5,7},{6,4},{7,5},{8,10},{9,11},{10,... | collective-permute-start | bytes 18440 | tf_op jit(solution)/shard_map/ppermute | solution.py:33
  4.1 0.0 collective-permute-start.2
  4.1 0.1 shard_map.140
  4.3 0.2 collective-permute-start.15
  4.5 1.9 %collective-permute-start.16 = (bf16[192,384]{1,0:T(8,128)(2,1)S(1)}, bf16[192,384]{1,0:T(8,128)(2,1)S(1)}, u32[]{:S(2)}, u32[]{:S(2)}) collective-permute-start(bf16[192,384]{1,0:T(8,128)(2,1)S(1)} %get-tuple-element.38), channel_id=1, source_target_pairs={{0,2},{1,3},{2,0},{3,1},{4,6},{5,7},{6,4},{7,5},{8,10},{9,11},{10,... | collective-permute-start | bytes 442376 | tf_op jit(solution)/shard_map/ppermute | solution.py:33
  6.4 0.3 convert_reduce_fusion
  6.8 0.4 collective-permute-done.2.refs_3_
  7.2 0.4 shard_map.136
  7.5 0.2 collective-permute-start.3
  7.8 0.5 collective-permute-start.4
  8.2 1.2 %collective-permute-start.5 = (bf16[8,768]{1,0:T(8,128)(2,1)S(1)}, bf16[8,768]{1,0:T(8,128)(2,1)S(1)}, u32[]{:S(2)}, u32[]{:S(2)}) collective-permute-start(bf16[8,768]{1,0:T(8,128)(2,1)S(1)} %get-tuple-element.27.refs_0_), channel_id=1, source_target_pairs={{0,3},{1,2},{2,1},{3,0},{4,7},{5,6},{6,5},{7,4},{8,11},{9,10},{10,... | collective-permute-start | bytes 36872 | tf_op jit(solution)/shard_map/ppermute | solution.py:33
  9.4 0.5 %fusion.2 = f32[2,256]{1,0:T(2,128)S(1)} fusion(bf16[2,256,1536]{2,1,0:T(8,128)(2,1)S(1)} %copy-done.10, f32[2,256]{1,0:T(2,128)S(1)} %broadcast_multiply_fusion), kind=kLoop, calls=%fused_computation.4 | loop fusion | flops 3145216 | bytes 1576960 | tf_op jit(solution)/shard_map/reduce_sum | solution.py:47
  10.0 0.6 %collective-permute-start.17 = (bf16[192,384]{1,0:T(8,128)(2,1)S(1)}, bf16[192,384]{1,0:T(8,128)(2,1)S(1)}, u32[]{:S(2)}, u32[]{:S(2)}) collective-permute-start(bf16[192,384]{1,0:T(8,128)(2,1)S(1)} %get-tuple-element.39), channel_id=1, source_target_pairs={{0,3},{1,2},{2,1},{3,0},{4,7},{5,6},{6,5},{7,4},{8,11},{9,10},{10,... | collective-permute-start | bytes 442376 | tf_op jit(solution)/shard_map/ppermute | solution.py:33
  10.6 0.9 %collective-permute-done.4.refs_2_ = bf16[8,768]{1,0:T(8,128)(2,1)S(1)} collective-permute-done((bf16[8,768]{1,0:T(8,128)(2,1)S(1)}, bf16[8,768]{1,0:T(8,128)(2,1)S(1)}, u32[]{:S(2)}, u32[]{:S(2)}) %collective-permute-start.4) | collective-permute-done | bytes 12320 | tf_op jit(solution)/shard_map/ppermute | solution.py:33
  11.5 0.4 shard_map.137
  11.9 0.2 collective-permute-start.6
  12.1 1.4 %collective-permute-start.7 = (bf16[24,384]{1,0:T(8,128)(2,1)S(1)}, bf16[24,384]{1,0:T(8,128)(2,1)S(1)}, u32[]{:S(2)}, u32[]{:S(2)}) collective-permute-start(bf16[24,384]{1,0:T(8,128)(2,1)S(1)} %get-tuple-element.30), channel_id=1, source_target_pairs={{0,2},{1,3},{2,0},{3,1},{4,6},{5,7},{6,4},{7,5},{8,10},{9,11},{10,... | collective-permute-start | bytes 55304 | tf_op jit(solution)/shard_map/ppermute | solution.py:33
  13.5 0.8 %collective-permute-start.8 = (bf16[24,384]{1,0:T(8,128)(2,1)S(1)}, bf16[24,384]{1,0:T(8,128)(2,1)S(1)}, u32[]{:S(2)}, u32[]{:S(2)}) collective-permute-start(bf16[24,384]{1,0:T(8,128)(2,1)S(1)} %get-tuple-element.31), channel_id=1, source_target_pairs={{0,3},{1,2},{2,1},{3,0},{4,7},{5,6},{6,5},{7,4},{8,11},{9,10},{10,... | collective-permute-start | bytes 55304 | tf_op jit(solution)/shard_map/ppermute | solution.py:33
  14.3 0.5 %fusion.4.refs_4_ = bf16[2,256,1536]{2,1,0:T(8,128)(2,1)S(1)} fusion(bf16[2,256,1536]{2,1,0:T(8,128)(2,1)S(1)} %copy-done.10, f32[1536]{0:T(1024)S(1)} %copy-done.11, f32[2,256]{1,0:T(2,128)S(1)} %add_rsqrt_fusion, f32[2,256]{1,0:T(2,128)S(1)} %broadcast_multiply_fusion), kind=kLoop, calls=%fused_computation.6 | loop fusion | flops 3932160 | bytes 3155968 | tf_op jit(solution)/shard_map/convert_element_type | solution.py:48
  14.9 0.0 copy-start.3
  14.9 0.0 copy-start.9
  14.9 0.0 copy-start.4
  14.9 1.8 %collective-permute-done.7.refs_2_ = bf16[24,384]{1,0:T(8,128)(2,1)S(1)} collective-permute-done((bf16[24,384]{1,0:T(8,128)(2,1)S(1)}, bf16[24,384]{1,0:T(8,128)(2,1)S(1)}, u32[]{:S(2)}, u32[]{:S(2)}) %collective-permute-start.7) | collective-permute-done | bytes 18464 | tf_op jit(solution)/shard_map/ppermute | solution.py:33
  16.7 0.1 collective-permute-done.8.refs_3_
  16.8 1.0 %shard_map.138 = (bf16[24,384]{1,0:T(8,128)(2,1)S(1)}, bf16[24,384]{1,0:T(8,128)(2,1)S(1)}, bf16[24,384]{1,0:T(8,128)(2,1)S(1)}, bf16[24,384]{1,0:T(8,128)(2,1)S(1)}) custom-call(s32[1]{0:T(128)} %bitcast.place.refs_0_, bf16[24,384]{1,0:T(8,128)(2,1)S(1)} %get-tuple-element.28.refs_0_, bf16[24,384]{1,0:T(8,128)(2,1)S(1)} %collective-permute-done.6.refs_1_, ...), custom_call_target="tpu_custom_call" | custom-call | tf_op jit(solution)/shard_map/pallas_call | solution.py:66
  17.8 0.0 copy-start.6
  17.8 0.0 copy-start.7
  17.8 0.0 copy-start.8
  17.8 1.0 %collective-permute-start.10 = (bf16[24,384]{1,0:T(8,128)(2,1)S(1)}, bf16[24,384]{1,0:T(8,128)(2,1)S(1)}, u32[]{:S(2)}, u32[]{:S(2)}) collective-permute-start(bf16[24,384]{1,0:T(8,128)(2,1)S(1)} %get-tuple-element.34), channel_id=1, source_target_pairs={{0,2},{1,3},{2,0},{3,1},{4,6},{5,7},{6,4},{7,5},{8,10},{9,11},{10,... | collective-permute-start | bytes 55304 | tf_op jit(solution)/shard_map/ppermute | solution.py:33
  18.9 0.5 %collective-permute-start.11 = (bf16[24,384]{1,0:T(8,128)(2,1)S(1)}, bf16[24,384]{1,0:T(8,128)(2,1)S(1)}, u32[]{:S(2)}, u32[]{:S(2)}) collective-permute-start(bf16[24,384]{1,0:T(8,128)(2,1)S(1)} %get-tuple-element.35), channel_id=1, source_target_pairs={{0,3},{1,2},{2,1},{3,0},{4,7},{5,6},{6,5},{7,4},{8,11},{9,10},{10,... | collective-permute-start | bytes 55304 | tf_op jit(solution)/shard_map/ppermute | solution.py:33
  19.4 2.3 %collective-permute-done.10.refs_2_ = bf16[24,384]{1,0:T(8,128)(2,1)S(1)} collective-permute-done((bf16[24,384]{1,0:T(8,128)(2,1)S(1)}, bf16[24,384]{1,0:T(8,128)(2,1)S(1)}, u32[]{:S(2)}, u32[]{:S(2)}) %collective-permute-start.10) | collective-permute-done | bytes 18464 | tf_op jit(solution)/shard_map/ppermute | solution.py:33
  21.7 0.5 %collective-permute-done.11.refs_3_ = bf16[24,384]{1,0:T(8,128)(2,1)S(1)} collective-permute-done((bf16[24,384]{1,0:T(8,128)(2,1)S(1)}, bf16[24,384]{1,0:T(8,128)(2,1)S(1)}, u32[]{:S(2)}, u32[]{:S(2)}) %collective-permute-start.11) | collective-permute-done | bytes 18464 | tf_op jit(solution)/shard_map/ppermute | solution.py:33
  22.2 0.7 %collective-permute-done.9.refs_1_ = bf16[24,384]{1,0:T(8,128)(2,1)S(1)} collective-permute-done((bf16[24,384]{1,0:T(8,128)(2,1)S(1)}, bf16[24,384]{1,0:T(8,128)(2,1)S(1)}, u32[]{:S(2)}, u32[]{:S(2)}) %collective-permute-start.9) | collective-permute-done | bytes 18464 | tf_op jit(solution)/shard_map/ppermute | solution.py:33
  22.9 0.3 shard_map.139.refs_0_.after
  23.2 0.2 collective-permute-start.12
  23.4 1.0 %collective-permute-start.13 = (bf16[8,768]{1,0:T(8,128)(2,1)S(1)}, bf16[8,768]{1,0:T(8,128)(2,1)S(1)}, u32[]{:S(2)}, u32[]{:S(2)}) collective-permute-start(bf16[8,768]{1,0:T(8,128)(2,1)S(1)} %shard_map.139.refs_0_.after), channel_id=1, source_target_pairs={{0,2},{1,3},{2,0},{3,1},{4,6},{5,7},{6,4},{7,5},{8,10},{9,11},{10,... | collective-permute-start | bytes 36872 | tf_op jit(solution)/shard_map/ppermute | solution.py:33
  24.4 0.0 collective-permute-done.12.refs_1_
  24.4 0.7 %collective-permute-start.14 = (bf16[8,768]{1,0:T(8,128)(2,1)S(1)}, bf16[8,768]{1,0:T(8,128)(2,1)S(1)}, u32[]{:S(2)}, u32[]{:S(2)}) collective-permute-start(bf16[8,768]{1,0:T(8,128)(2,1)S(1)} %shard_map.139.refs_0_.after), channel_id=1, source_target_pairs={{0,3},{1,2},{2,1},{3,0},{4,7},{5,6},{6,5},{7,4},{8,11},{9,10},{10,... | collective-permute-start | bytes 36872 | tf_op jit(solution)/shard_map/ppermute | solution.py:33
  25.8 0.6 %shard_map.141.refs_10_ = bf16[8,128]{1,0:T(8,128)(2,1)S(1)} custom-call(s32[1]{0:T(128)} %bitcast.place.refs_0_, s32[2]{0:T(128)S(1)} %copy-done.9, s32[1]{0:T(128)S(6)} %copy.15.counts, bf16[2,1536]{1,0:T(2,128)(2,1)S(1)} %head.1.refs_0_.after), custom_call_target="tpu_custom_call" | custom-call | tf_op jit(solution)/shard_map/pallas_call | solution.py:66
  26.4 0.7 %collective-permute-done.13.refs_2_ = bf16[8,768]{1,0:T(8,128)(2,1)S(1)} collective-permute-done((bf16[8,768]{1,0:T(8,128)(2,1)S(1)}, bf16[8,768]{1,0:T(8,128)(2,1)S(1)}, u32[]{:S(2)}, u32[]{:S(2)}) %collective-permute-start.13) | collective-permute-done | bytes 12320 | tf_op jit(solution)/shard_map/ppermute | solution.py:33
  27.1 0.4 collective-permute-done.14.refs_3_
  27.5 0.4 shard_map.142.refs_1_
  28.0 0.2 collective-permute-start.18
  28.2 1.0 %collective-permute-start.19 = (bf16[8,896]{1,0:T(8,128)(2,1)S(1)}, bf16[8,896]{1,0:T(8,128)(2,1)S(1)}, u32[]{:S(2)}, u32[]{:S(2)}) collective-permute-start(bf16[8,896]{1,0:T(8,128)(2,1)S(1)} %shard_map.142.refs_1_), channel_id=1, source_target_pairs={{0,2},{1,3},{2,0},{3,1},{4,6},{5,7},{6,4},{7,5},{8,10},{9,11},{10,... | collective-permute-start | bytes 43016 | tf_op jit(solution)/shard_map/ppermute | solution.py:33
  29.1 0.7 %collective-permute-start.20 = (bf16[8,896]{1,0:T(8,128)(2,1)S(1)}, bf16[8,896]{1,0:T(8,128)(2,1)S(1)}, u32[]{:S(2)}, u32[]{:S(2)}) collective-permute-start(bf16[8,896]{1,0:T(8,128)(2,1)S(1)} %shard_map.142.refs_1_), channel_id=1, source_target_pairs={{0,3},{1,2},{2,1},{3,0},{4,7},{5,6},{6,5},{7,4},{8,11},{9,10},{10,... | collective-permute-start | bytes 43016 | tf_op jit(solution)/shard_map/ppermute | solution.py:33
  29.9 2.0 %collective-permute-done.19.refs_3_ = bf16[8,896]{1,0:T(8,128)(2,1)S(1)} collective-permute-done((bf16[8,896]{1,0:T(8,128)(2,1)S(1)}, bf16[8,896]{1,0:T(8,128)(2,1)S(1)}, u32[]{:S(2)}, u32[]{:S(2)}) %collective-permute-start.19) | collective-permute-done | bytes 14368 | tf_op jit(solution)/shard_map/ppermute | solution.py:33
  31.9 0.4 collective-permute-done.20.refs_4_
  32.3 0.1 shard_map.143.refs_0_
  32.3 1.6 %collective-permute-start.21 = (bf16[8,896]{1,0:T(8,128)(2,1)S(1)}, bf16[8,896]{1,0:T(8,128)(2,1)S(1)}, u32[]{:S(2)}, u32[]{:S(2)}) collective-permute-start(bf16[8,896]{1,0:T(8,128)(2,1)S(1)} %shard_map.143.refs_0_), channel_id=1, source_target_pairs={{0,4},{4,0},{8,12},{12,8},{1,5},{5,1},{9,13},{13,9},{2,6},{6,2},{1... | collective-permute-start | bytes 43016 | tf_op jit(solution)/shard_map/ppermute | solution.py:33
  34.0 2.6 %collective-permute-start.22 = (bf16[8,896]{1,0:T(8,128)(2,1)S(1)}, bf16[8,896]{1,0:T(8,128)(2,1)S(1)}, u32[]{:S(2)}, u32[]{:S(2)}) collective-permute-start(bf16[8,896]{1,0:T(8,128)(2,1)S(1)} %shard_map.143.refs_0_), channel_id=1, source_target_pairs={{0,8},{4,12},{8,0},{12,4},{1,9},{5,13},{9,1},{13,5},{2,10},{6,14},... | collective-permute-start | bytes 43016 | tf_op jit(solution)/shard_map/ppermute | solution.py:33
  36.6 0.2 collective-permute-start.23
  36.7 0.1 shard_map.144
  36.9 1.7 %collective-permute-done.22.refs_2_ = bf16[8,896]{1,0:T(8,128)(2,1)S(1)} collective-permute-done((bf16[8,896]{1,0:T(8,128)(2,1)S(1)}, bf16[8,896]{1,0:T(8,128)(2,1)S(1)}, u32[]{:S(2)}, u32[]{:S(2)}) %collective-permute-start.22) | collective-permute-done | bytes 14368 | tf_op jit(solution)/shard_map/ppermute | solution.py:33
  38.6 3.5 %collective-permute-done.23.refs_3_ = bf16[8,896]{1,0:T(8,128)(2,1)S(1)} collective-permute-done((bf16[8,896]{1,0:T(8,128)(2,1)S(1)}, bf16[8,896]{1,0:T(8,128)(2,1)S(1)}, u32[]{:S(2)}, u32[]{:S(2)}) %collective-permute-start.23) | collective-permute-done | bytes 14368 | tf_op jit(solution)/shard_map/ppermute | solution.py:33
  42.1 1.1 %shard_map.145 = (bf16[8,192]{1,0:T(8,128)(2,1)S(1)}, bf16[8,192]{1,0:T(8,128)(2,1)S(1)}, bf16[8,192]{1,0:T(8,128)(2,1)S(1)}, bf16[8,192]{1,0:T(8,128)(2,1)S(1)}) custom-call(s32[1]{0:T(128)} %bitcast.place.refs_0_, bf16[8,896]{1,0:T(8,128)(2,1)S(1)} %shard_map.143.refs_0_, bf16[8,896]{1,0:T(8,128)(2,1)S(1)} %collective-permute-done.21.refs_1_, ...), custom_call_target="tpu_custom_call" | custom-call | tf_op jit(solution)/shard_map/pallas_call | solution.py:66
  43.2 0.0 collective-permute-start.24
  43.2 1.1 %collective-permute-start.25 = (bf16[8,192]{1,0:T(8,128)(2,1)S(1)}, bf16[8,192]{1,0:T(8,128)(2,1)S(1)}, u32[]{:S(2)}, u32[]{:S(2)}) collective-permute-start(bf16[8,192]{1,0:T(8,128)(2,1)S(1)} %get-tuple-element.47), channel_id=1, source_target_pairs={{0,2},{1,3},{2,0},{3,1},{4,6},{5,7},{6,4},{7,5},{8,10},{9,11},{10,... | collective-permute-start | bytes 9224 | tf_op jit(solution)/shard_map/ppermute | solution.py:33
  44.4 0.7 %collective-permute-start.26 = (bf16[8,192]{1,0:T(8,128)(2,1)S(1)}, bf16[8,192]{1,0:T(8,128)(2,1)S(1)}, u32[]{:S(2)}, u32[]{:S(2)}) collective-permute-start(bf16[8,192]{1,0:T(8,128)(2,1)S(1)} %get-tuple-element.48), channel_id=1, source_target_pairs={{0,3},{1,2},{2,1},{3,0},{4,7},{5,6},{6,5},{7,4},{8,11},{9,10},{10,... | collective-permute-start | bytes 9224 | tf_op jit(solution)/shard_map/ppermute | solution.py:33
  45.1 0.3 shard_map.146
  45.4 1.5 %collective-permute-done.25 = bf16[8,192]{1,0:T(8,128)(2,1)S(1)} collective-permute-done((bf16[8,192]{1,0:T(8,128)(2,1)S(1)}, bf16[8,192]{1,0:T(8,128)(2,1)S(1)}, u32[]{:S(2)}, u32[]{:S(2)}) %collective-permute-start.25) | collective-permute-done | bytes 3104 | tf_op jit(solution)/shard_map/ppermute | solution.py:33
  46.9 0.5 %collective-permute-done.26 = bf16[8,192]{1,0:T(8,128)(2,1)S(1)} collective-permute-done((bf16[8,192]{1,0:T(8,128)(2,1)S(1)}, bf16[8,192]{1,0:T(8,128)(2,1)S(1)}, u32[]{:S(2)}, u32[]{:S(2)}) %collective-permute-start.26) | collective-permute-done | bytes 3104 | tf_op jit(solution)/shard_map/ppermute | solution.py:33
  47.4 0.6 %add_convert_fusion = bf16[8,192]{1,0:T(8,128)(2,1)} fusion(f32[8,192]{1,0:T(8,128)S(1)} %shard_map.146, bf16[8,192]{1,0:T(8,128)(2,1)S(1)} %collective-permute-done.26, bf16[8,192]{1,0:T(8,128)(2,1)S(1)} %collective-permute-done.25, bf16[8,192]{1,0:T(8,128)(2,1)S(1)} %collective-permute-done.24, bf16[8,192]{1,0:T(8,128)(2,1)S(1)} %get-tuple-element.45.refs_4_), kind=kLoop, calls=%fused_computation.7 | loop fusion | flops 13824 | bytes 21504 | tf_op jit(solution)/shard_map/convert_element_type | solution.py:411
  (36 shorter events, 0.1 us)
Async XLA Ops:
  0.0 4.1 %copy-start = (bf16[192,1536]{1,0:T(8,128)(2,1)S(1)}, bf16[192,1536]{1,0:T(8,128)(2,1)}, u32[]{:S(2)}) copy-start(bf16[192,1536]{1,0:T(8,128)(2,1)} %weight.2) | copy-start | bytes 1769476
  0.0 6.4 %copy-start.10 = (bf16[2,256,1536]{2,1,0:T(8,128)(2,1)S(1)}, bf16[2,256,1536]{2,1,0:T(8,128)(2,1)}, u32[]{:S(2)}) copy-start(bf16[2,256,1536]{2,1,0:T(8,128)(2,1)} %tokens.1) | copy-start | bytes 4718596
  0.0 6.7 %copy-start.11 = (f32[1536]{0:T(1024)S(1)}, f32[1536]{0:T(1024)}, u32[]{:S(2)}) copy-start(f32[1536]{0:T(1024)} %param.15) | copy-start | bytes 18436
  0.0 7.2 %copy-start.1 = (bf16[384,768]{1,0:T(8,128)(2,1)S(1)}, bf16[384,768]{1,0:T(8,128)(2,1)}, u32[]{:S(2)}) copy-start(bf16[384,768]{1,0:T(8,128)(2,1)} %refs_5_.1) | copy-start | bytes 1769476
  1.0 5.8 %collective-permute-start = (bf16[2,1536]{1,0:T(2,128)(2,1)S(1)}, bf16[2,1536]{1,0:T(2,128)(2,1)S(1)}, u32[]{:S(2)}, u32[]{:S(2)}) collective-permute-start(bf16[2,1536]{1,0:T(2,128)(2,1)S(1)} %head.1.refs_0_.after), channel_id=1, source_target_pairs={{0,1},{1,0},{2,3},{3,2},{4,5},{5,4},{6,7},{7,6},{8,9},{9,8},{10,11... | collective-permute-start | bytes 18440 | tf_op jit(solution)/shard_map/ppermute | solution.py:33
  1.5 5.2 %collective-permute-start.1 = (bf16[2,1536]{1,0:T(2,128)(2,1)S(1)}, bf16[2,1536]{1,0:T(2,128)(2,1)S(1)}, u32[]{:S(2)}, u32[]{:S(2)}) collective-permute-start(bf16[2,1536]{1,0:T(2,128)(2,1)S(1)} %head.1.refs_0_.after), channel_id=1, source_target_pairs={{0,2},{1,3},{2,0},{3,1},{4,6},{5,7},{6,4},{7,5},{8,10},{9,11},{10,... | collective-permute-start | bytes 18440 | tf_op jit(solution)/shard_map/ppermute | solution.py:33
  4.1 3.1 %collective-permute-start.2 = (bf16[2,1536]{1,0:T(2,128)(2,1)S(1)}, bf16[2,1536]{1,0:T(2,128)(2,1)S(1)}, u32[]{:S(2)}, u32[]{:S(2)}) collective-permute-start(bf16[2,1536]{1,0:T(2,128)(2,1)S(1)} %head.1.refs_0_.after), channel_id=1, source_target_pairs={{0,3},{1,2},{2,1},{3,0},{4,7},{5,6},{6,5},{7,4},{8,11},{9,10},{10,... | collective-permute-start | bytes 18440 | tf_op jit(solution)/shard_map/ppermute | solution.py:33
  4.3 23.3 %collective-permute-start.15 = (bf16[192,384]{1,0:T(8,128)(2,1)S(1)}, bf16[192,384]{1,0:T(8,128)(2,1)S(1)}, u32[]{:S(2)}, u32[]{:S(2)}) collective-permute-start(bf16[192,384]{1,0:T(8,128)(2,1)S(1)} %get-tuple-element.37), channel_id=1, source_target_pairs={{0,1},{1,0},{2,3},{3,2},{4,5},{5,4},{6,7},{7,6},{8,9},{9,8},{10,11... | collective-permute-start | bytes 442376 | tf_op jit(solution)/shard_map/ppermute | solution.py:33
  4.5 7.0 %copy-start.2 = (bf16[384,768]{1,0:T(8,128)(2,1)S(1)}, bf16[384,768]{1,0:T(8,128)(2,1)}, u32[]{:S(2)}) copy-start(bf16[384,768]{1,0:T(8,128)(2,1)} %refs_4_.2) | copy-start | bytes 1769476
  4.5 23.0 %collective-permute-start.16 = (bf16[192,384]{1,0:T(8,128)(2,1)S(1)}, bf16[192,384]{1,0:T(8,128)(2,1)S(1)}, u32[]{:S(2)}, u32[]{:S(2)}) collective-permute-start(bf16[192,384]{1,0:T(8,128)(2,1)S(1)} %get-tuple-element.38), channel_id=1, source_target_pairs={{0,2},{1,3},{2,0},{3,1},{4,6},{5,7},{6,4},{7,5},{8,10},{9,11},{10,... | collective-permute-start | bytes 442376 | tf_op jit(solution)/shard_map/ppermute | solution.py:33
  7.5 2.4 %collective-permute-start.3 = (bf16[8,768]{1,0:T(8,128)(2,1)S(1)}, bf16[8,768]{1,0:T(8,128)(2,1)S(1)}, u32[]{:S(2)}, u32[]{:S(2)}) collective-permute-start(bf16[8,768]{1,0:T(8,128)(2,1)S(1)} %get-tuple-element.27.refs_0_), channel_id=1, source_target_pairs={{0,1},{1,0},{2,3},{3,2},{4,5},{5,4},{6,7},{7,6},{8,9},{9,8},{10,11... | collective-permute-start | bytes 36872 | tf_op jit(solution)/shard_map/ppermute | solution.py:33
  7.8 3.7 %collective-permute-start.4 = (bf16[8,768]{1,0:T(8,128)(2,1)S(1)}, bf16[8,768]{1,0:T(8,128)(2,1)S(1)}, u32[]{:S(2)}, u32[]{:S(2)}) collective-permute-start(bf16[8,768]{1,0:T(8,128)(2,1)S(1)} %get-tuple-element.27.refs_0_), channel_id=1, source_target_pairs={{0,2},{1,3},{2,0},{3,1},{4,6},{5,7},{6,4},{7,5},{8,10},{9,11},{10,... | collective-permute-start | bytes 36872 | tf_op jit(solution)/shard_map/ppermute | solution.py:33
  8.2 3.3 %collective-permute-start.5 = (bf16[8,768]{1,0:T(8,128)(2,1)S(1)}, bf16[8,768]{1,0:T(8,128)(2,1)S(1)}, u32[]{:S(2)}, u32[]{:S(2)}) collective-permute-start(bf16[8,768]{1,0:T(8,128)(2,1)S(1)} %get-tuple-element.27.refs_0_), channel_id=1, source_target_pairs={{0,3},{1,2},{2,1},{3,0},{4,7},{5,6},{6,5},{7,4},{8,11},{9,10},{10,... | collective-permute-start | bytes 36872 | tf_op jit(solution)/shard_map/ppermute | solution.py:33
  10.0 17.5 %collective-permute-start.17 = (bf16[192,384]{1,0:T(8,128)(2,1)S(1)}, bf16[192,384]{1,0:T(8,128)(2,1)S(1)}, u32[]{:S(2)}, u32[]{:S(2)}) collective-permute-start(bf16[192,384]{1,0:T(8,128)(2,1)S(1)} %get-tuple-element.39), channel_id=1, source_target_pairs={{0,3},{1,2},{2,1},{3,0},{4,7},{5,6},{6,5},{7,4},{8,11},{9,10},{10,... | collective-permute-start | bytes 442376 | tf_op jit(solution)/shard_map/ppermute | solution.py:33
  11.9 1.6 %collective-permute-start.6 = (bf16[24,384]{1,0:T(8,128)(2,1)S(1)}, bf16[24,384]{1,0:T(8,128)(2,1)S(1)}, u32[]{:S(2)}, u32[]{:S(2)}) collective-permute-start(bf16[24,384]{1,0:T(8,128)(2,1)S(1)} %get-tuple-element.29), channel_id=1, source_target_pairs={{0,1},{1,0},{2,3},{3,2},{4,5},{5,4},{6,7},{7,6},{8,9},{9,8},{10,11... | collective-permute-start | bytes 55304 | tf_op jit(solution)/shard_map/ppermute | solution.py:33
  12.1 4.6 %collective-permute-start.7 = (bf16[24,384]{1,0:T(8,128)(2,1)S(1)}, bf16[24,384]{1,0:T(8,128)(2,1)S(1)}, u32[]{:S(2)}, u32[]{:S(2)}) collective-permute-start(bf16[24,384]{1,0:T(8,128)(2,1)S(1)} %get-tuple-element.30), channel_id=1, source_target_pairs={{0,2},{1,3},{2,0},{3,1},{4,6},{5,7},{6,4},{7,5},{8,10},{9,11},{10,... | collective-permute-start | bytes 55304 | tf_op jit(solution)/shard_map/ppermute | solution.py:33
  13.5 3.3 %collective-permute-start.8 = (bf16[24,384]{1,0:T(8,128)(2,1)S(1)}, bf16[24,384]{1,0:T(8,128)(2,1)S(1)}, u32[]{:S(2)}, u32[]{:S(2)}) collective-permute-start(bf16[24,384]{1,0:T(8,128)(2,1)S(1)} %get-tuple-element.31), channel_id=1, source_target_pairs={{0,3},{1,2},{2,1},{3,0},{4,7},{5,6},{6,5},{7,4},{8,11},{9,10},{10,... | collective-permute-start | bytes 55304 | tf_op jit(solution)/shard_map/ppermute | solution.py:33
  14.9 8.0 %copy-start.3 = (bf16[384,768]{1,0:T(8,128)(2,1)S(1)}, bf16[384,768]{1,0:T(8,128)(2,1)}, u32[]{:S(2)}) copy-start(bf16[384,768]{1,0:T(8,128)(2,1)} %refs_4_.3) | copy-start | bytes 1769476
  14.9 10.9 %copy-start.9 = (s32[2]{0:T(128)S(1)}, s32[2]{0:T(128)}, u32[]{:S(2)}) copy-start(s32[2]{0:T(128)} %order.1) | copy-start | bytes 28
  14.9 12.6 %copy-start.4 = (bf16[384,768]{1,0:T(8,128)(2,1)S(1)}, bf16[384,768]{1,0:T(8,128)(2,1)}, u32[]{:S(2)}) copy-start(bf16[384,768]{1,0:T(8,128)(2,1)} %refs_9_.1) | copy-start | bytes 1769476
  16.8 20.0 %copy-start.12 = (f32[768]{0:T(1024)S(1)}, f32[768]{0:T(1024)}, u32[]{:S(2)}) copy-start(f32[768]{0:T(1024)} %param.21) | copy-start | bytes 9220
  16.8 20.0 %copy-start.5 = (bf16[192,768]{1,0:T(8,128)(2,1)S(1)}, bf16[192,768]{1,0:T(8,128)(2,1)}, u32[]{:S(2)}) copy-start(bf16[192,768]{1,0:T(8,128)(2,1)} %weight.3) | copy-start | bytes 884740
  17.8 24.3 %copy-start.6 = (bf16[768,192]{0,1:T(8,128)(2,1)S(1)}, bf16[768,192]{0,1:T(8,128)(2,1)}, u32[]{:S(2)}) copy-start(bf16[768,192]{0,1:T(8,128)(2,1)} %param.22) | copy-start | bytes 884740
  17.8 24.3 %copy-start.7 = (bf16[768,192]{0,1:T(8,128)(2,1)S(1)}, bf16[768,192]{0,1:T(8,128)(2,1)}, u32[]{:S(2)}) copy-start(bf16[768,192]{0,1:T(8,128)(2,1)} %param.23) | copy-start | bytes 884740
  17.8 24.3 %copy-start.8 = (bf16[768,192]{0,1:T(8,128)(2,1)S(1)}, bf16[768,192]{0,1:T(8,128)(2,1)}, u32[]{:S(2)}) copy-start(bf16[768,192]{0,1:T(8,128)(2,1)} %param.24) | copy-start | bytes 884740
  17.8 3.8 %collective-permute-start.10 = (bf16[24,384]{1,0:T(8,128)(2,1)S(1)}, bf16[24,384]{1,0:T(8,128)(2,1)S(1)}, u32[]{:S(2)}, u32[]{:S(2)}) collective-permute-start(bf16[24,384]{1,0:T(8,128)(2,1)S(1)} %get-tuple-element.34), channel_id=1, source_target_pairs={{0,2},{1,3},{2,0},{3,1},{4,6},{5,7},{6,4},{7,5},{8,10},{9,11},{10,... | collective-permute-start | bytes 55304 | tf_op jit(solution)/shard_map/ppermute | solution.py:33
  18.9 3.3 %collective-permute-start.11 = (bf16[24,384]{1,0:T(8,128)(2,1)S(1)}, bf16[24,384]{1,0:T(8,128)(2,1)S(1)}, u32[]{:S(2)}, u32[]{:S(2)}) collective-permute-start(bf16[24,384]{1,0:T(8,128)(2,1)S(1)} %get-tuple-element.35), channel_id=1, source_target_pairs={{0,3},{1,2},{2,1},{3,0},{4,7},{5,6},{6,5},{7,4},{8,11},{9,10},{10,... | collective-permute-start | bytes 55304 | tf_op jit(solution)/shard_map/ppermute | solution.py:33
  21.7 1.2 %collective-permute-start.9 = (bf16[24,384]{1,0:T(8,128)(2,1)S(1)}, bf16[24,384]{1,0:T(8,128)(2,1)S(1)}, u32[]{:S(2)}, u32[]{:S(2)}) collective-permute-start(bf16[24,384]{1,0:T(8,128)(2,1)S(1)} %get-tuple-element.33), channel_id=1, source_target_pairs={{0,1},{1,0},{2,3},{3,2},{4,5},{5,4},{6,7},{7,6},{8,9},{9,8},{10,11... | collective-permute-start | bytes 55304 | tf_op jit(solution)/shard_map/ppermute | solution.py:33
  23.2 1.2 %collective-permute-start.12 = (bf16[8,768]{1,0:T(8,128)(2,1)S(1)}, bf16[8,768]{1,0:T(8,128)(2,1)S(1)}, u32[]{:S(2)}, u32[]{:S(2)}) collective-permute-start(bf16[8,768]{1,0:T(8,128)(2,1)S(1)} %shard_map.139.refs_0_.after), channel_id=1, source_target_pairs={{0,1},{1,0},{2,3},{3,2},{4,5},{5,4},{6,7},{7,6},{8,9},{9,8},{10,11... | collective-permute-start | bytes 36872 | tf_op jit(solution)/shard_map/ppermute | solution.py:33
  23.4 3.7 %collective-permute-start.13 = (bf16[8,768]{1,0:T(8,128)(2,1)S(1)}, bf16[8,768]{1,0:T(8,128)(2,1)S(1)}, u32[]{:S(2)}, u32[]{:S(2)}) collective-permute-start(bf16[8,768]{1,0:T(8,128)(2,1)S(1)} %shard_map.139.refs_0_.after), channel_id=1, source_target_pairs={{0,2},{1,3},{2,0},{3,1},{4,6},{5,7},{6,4},{7,5},{8,10},{9,11},{10,... | collective-permute-start | bytes 36872 | tf_op jit(solution)/shard_map/ppermute | solution.py:33
  24.4 3.1 %collective-permute-start.14 = (bf16[8,768]{1,0:T(8,128)(2,1)S(1)}, bf16[8,768]{1,0:T(8,128)(2,1)S(1)}, u32[]{:S(2)}, u32[]{:S(2)}) collective-permute-start(bf16[8,768]{1,0:T(8,128)(2,1)S(1)} %shard_map.139.refs_0_.after), channel_id=1, source_target_pairs={{0,3},{1,2},{2,1},{3,0},{4,7},{5,6},{6,5},{7,4},{8,11},{9,10},{10,... | collective-permute-start | bytes 36872 | tf_op jit(solution)/shard_map/ppermute | solution.py:33
  28.0 1.9 %collective-permute-start.18 = (bf16[8,896]{1,0:T(8,128)(2,1)S(1)}, bf16[8,896]{1,0:T(8,128)(2,1)S(1)}, u32[]{:S(2)}, u32[]{:S(2)}) collective-permute-start(bf16[8,896]{1,0:T(8,128)(2,1)S(1)} %shard_map.142.refs_1_), channel_id=1, source_target_pairs={{0,1},{1,0},{2,3},{3,2},{4,5},{5,4},{6,7},{7,6},{8,9},{9,8},{10,11... | collective-permute-start | bytes 43016 | tf_op jit(solution)/shard_map/ppermute | solution.py:33
  28.2 3.7 %collective-permute-start.19 = (bf16[8,896]{1,0:T(8,128)(2,1)S(1)}, bf16[8,896]{1,0:T(8,128)(2,1)S(1)}, u32[]{:S(2)}, u32[]{:S(2)}) collective-permute-start(bf16[8,896]{1,0:T(8,128)(2,1)S(1)} %shard_map.142.refs_1_), channel_id=1, source_target_pairs={{0,2},{1,3},{2,0},{3,1},{4,6},{5,7},{6,4},{7,5},{8,10},{9,11},{10,... | collective-permute-start | bytes 43016 | tf_op jit(solution)/shard_map/ppermute | solution.py:33
  29.1 3.1 %collective-permute-start.20 = (bf16[8,896]{1,0:T(8,128)(2,1)S(1)}, bf16[8,896]{1,0:T(8,128)(2,1)S(1)}, u32[]{:S(2)}, u32[]{:S(2)}) collective-permute-start(bf16[8,896]{1,0:T(8,128)(2,1)S(1)} %shard_map.142.refs_1_), channel_id=1, source_target_pairs={{0,3},{1,2},{2,1},{3,0},{4,7},{5,6},{6,5},{7,4},{8,11},{9,10},{10,... | collective-permute-start | bytes 43016 | tf_op jit(solution)/shard_map/ppermute | solution.py:33
  32.3 4.6 %collective-permute-start.21 = (bf16[8,896]{1,0:T(8,128)(2,1)S(1)}, bf16[8,896]{1,0:T(8,128)(2,1)S(1)}, u32[]{:S(2)}, u32[]{:S(2)}) collective-permute-start(bf16[8,896]{1,0:T(8,128)(2,1)S(1)} %shard_map.143.refs_0_), channel_id=1, source_target_pairs={{0,4},{4,0},{8,12},{12,8},{1,5},{5,1},{9,13},{13,9},{2,6},{6,2},{1... | collective-permute-start | bytes 43016 | tf_op jit(solution)/shard_map/ppermute | solution.py:33
  34.0 4.6 %collective-permute-start.22 = (bf16[8,896]{1,0:T(8,128)(2,1)S(1)}, bf16[8,896]{1,0:T(8,128)(2,1)S(1)}, u32[]{:S(2)}, u32[]{:S(2)}) collective-permute-start(bf16[8,896]{1,0:T(8,128)(2,1)S(1)} %shard_map.143.refs_0_), channel_id=1, source_target_pairs={{0,8},{4,12},{8,0},{12,4},{1,9},{5,13},{9,1},{13,5},{2,10},{6,14},... | collective-permute-start | bytes 43016 | tf_op jit(solution)/shard_map/ppermute | solution.py:33
  36.6 5.5 %collective-permute-start.23 = (bf16[8,896]{1,0:T(8,128)(2,1)S(1)}, bf16[8,896]{1,0:T(8,128)(2,1)S(1)}, u32[]{:S(2)}, u32[]{:S(2)}) collective-permute-start(bf16[8,896]{1,0:T(8,128)(2,1)S(1)} %shard_map.143.refs_0_), channel_id=1, source_target_pairs={{0,12},{4,8},{8,4},{12,0},{1,13},{5,9},{9,5},{13,1},{2,14},{6,10},... | collective-permute-start | bytes 43016 | tf_op jit(solution)/shard_map/ppermute | solution.py:33
  43.2 2.2 %collective-permute-start.24 = (bf16[8,192]{1,0:T(8,128)(2,1)S(1)}, bf16[8,192]{1,0:T(8,128)(2,1)S(1)}, u32[]{:S(2)}, u32[]{:S(2)}) collective-permute-start(bf16[8,192]{1,0:T(8,128)(2,1)S(1)} %get-tuple-element.46), channel_id=1, source_target_pairs={{0,1},{1,0},{2,3},{3,2},{4,5},{5,4},{6,7},{7,6},{8,9},{9,8},{10,11... | collective-permute-start | bytes 9224 | tf_op jit(solution)/shard_map/ppermute | solution.py:33
  43.2 3.7 %collective-permute-start.25 = (bf16[8,192]{1,0:T(8,128)(2,1)S(1)}, bf16[8,192]{1,0:T(8,128)(2,1)S(1)}, u32[]{:S(2)}, u32[]{:S(2)}) collective-permute-start(bf16[8,192]{1,0:T(8,128)(2,1)S(1)} %get-tuple-element.47), channel_id=1, source_target_pairs={{0,2},{1,3},{2,0},{3,1},{4,6},{5,7},{6,4},{7,5},{8,10},{9,11},{10,... | collective-permute-start | bytes 9224 | tf_op jit(solution)/shard_map/ppermute | solution.py:33
  44.4 3.0 %collective-permute-start.26 = (bf16[8,192]{1,0:T(8,128)(2,1)S(1)}, bf16[8,192]{1,0:T(8,128)(2,1)S(1)}, u32[]{:S(2)}, u32[]{:S(2)}) collective-permute-start(bf16[8,192]{1,0:T(8,128)(2,1)S(1)} %get-tuple-element.48), channel_id=1, source_target_pairs={{0,3},{1,2},{2,1},{3,0},{4,7},{5,6},{6,5},{7,4},{8,11},{9,10},{10,... | collective-permute-start | bytes 9224 | tf_op jit(solution)/shard_map/ppermute | solution.py:33
where the time goes:
time: 48.1 us; the launch traced here: 48 us
  starting transfers between devices  21.8 us (45%)
  waiting for transfers between devices  17.4 us (36%)
  Pallas kernels  5.88 us (12%)
  other arithmetic  1.97 us (4%)
  between operations  0.86 us (2%)
    ppermute x27, starting transfers between devices, swap(): lax.ppermute(array, axis, [(i, other(i, step, size)) for i in range(size)])  21.8 us
    ppermute x27, waiting for transfers between devices, swap(): lax.ppermute(array, axis, [(i, other(i, step, size)) for i in range(size)])  17.4 us
    pallas_call x11, Pallas kernels, run(): pl.pallas_call(body, out_shape=outs, in_specs=[smem] + [vmem] * last + [p...  4.92 us
    pallas_call x1, Pallas kernels, local(): pl.pallas_call(head_kernel, out_shape=jax.ShapeDtypeStruct((tiles, width)...  0.97 us
  transfers between devices with their start and end apart: 27, of which 15 were waited for; matrix products, arithmetic and copies ran while one was open for 3% of the time, Pallas kernels for 7%

commit v1 on v0

--- a/solution.py
+++ b/solution.py
@@ -35,6 +35,20 @@
 
 def spread(array, axis):
     return [array] + [swap(array, axis, step) for step in range(1, lax.axis_size(axis))]
+
+
+def rows_of_all(array):
+    size, seq_size = lax.axis_size("fsdp"), lax.axis_size("seq")
+    if size % 2 or seq_size & (seq_size - 1) or seq_size < 4:
+        return spread(array, "seq")
+    direct = [swap(array, "seq", step) for step in range(3, seq_size)]
+    pairs = [
+        (row * size + place, (row ^ (1 + place % 2)) * size + place)
+        for row in range(seq_size)
+        for place in range(size)
+    ]
+    near = lax.ppermute(array, ("seq", "fsdp"), pairs)
+    return [array, near, swap(near, "fsdp", 1), *direct]
 
 
 def deal(arrays, axis):
@@ -384,7 +398,7 @@
     group_tiles = call(
         gather_kernel, jax.ShapeDtypeStruct((count, model + LANES), BF16)
     )(place, *embed_parts)
-    all_tiles = spread(group_tiles, "seq")
+    all_tiles = rows_of_all(group_tiles)
 
     head_width = long_query.shape[1]
     long_blocks = cut(long_out, pooled_part)

time: 48.1 us -> 45.6 us (0.948)
  waiting for transfers between devices: 17.4 us -> 15.1 us
    ppermute x27 -> x26, waiting for transfers between devices: 17.4 us -> 15.1 us  [swap(): lax.ppermute(array, axis, [(i, other(i, step, size)) for i in range(size)])]
    ppermute x27 -> x26, starting transfers between devices: 21.8 us -> 19.9 us  [swap(): lax.ppermute(array, axis, [(i, other(i, step, size)) for i in range(size)])]
    ppermute x0 -> x1, starting transfers between devices: none -> 1.62 us  [rows_of_all(): near = lax.ppermute(array, ('seq', 'fsdp'), pairs)]
  transfers between devices with their start and end apart: 27 -> 27, of which waited for: 15 -> 14; matrix products, arithmetic and copies ran while one was open for 3% -> 3% of each run, Pallas kernels for 7% -> 7%
where the time goes in v1:
time: 45.6 us; the launch traced here: 45.4 us
  starting transfers between devices  21.5 us (47%)
  waiting for transfers between devices  15.1 us (33%)
  Pallas kernels  5.88 us (13%)
  other arithmetic  1.97 us (4%)
  between operations  0.87 us (2%)
    ppermute x26, starting transfers between devices, swap(): lax.ppermute(array, axis, [(i, other(i, step, size)) for i in range(size)])  19.9 us
    ppermute x26, waiting for transfers between devices, swap(): lax.ppermute(array, axis, [(i, other(i, step, size)) for i in range(size)])  15.1 us
    pallas_call x11, Pallas kernels, run(): pl.pallas_call(body, out_shape=outs, in_specs=[smem] + [vmem] * last + [p...  4.92 us
    ppermute x1, starting transfers between devices, rows_of_all(): near = lax.ppermute(array, ('seq', 'fsdp'), pairs)  1.62 us
    pallas_call x1, Pallas kernels, local(): pl.pallas_call(head_kernel, out_shape=jax.ShapeDtypeStruct((tiles, width)...  0.97 us
  transfers between devices with their start and end apart: 27, of which 14 were waited for; matrix products, arithmetic and copies ran while one was open for 3% of the time, Pallas kernels for 7%

profile of v1, /device:TPU:0, one launch (start us, length us, event | category | flops | bytes accessed | tf_op | source)
XLA Modules:
  0.0 45.4 jit_solution(6189353471994035243)
XLA Ops:
  0.0 1.0 %head.1.refs_0_.after = bf16[2,1536]{1,0:T(2,128)(2,1)S(1)} custom-call(bf16[2,256,1536]{2,1,0:T(8,128)(2,1)} %tokens.1), custom_call_target="tpu_custom_call" | custom-call | tf_op jit(solution)/shard_map/head/pallas_call | solution.py:328
  1.0 0.6 %collective-permute-start = (bf16[2,1536]{1,0:T(2,128)(2,1)S(1)}, bf16[2,1536]{1,0:T(2,128)(2,1)S(1)}, u32[]{:S(2)}, u32[]{:S(2)}) collective-permute-start(bf16[2,1536]{1,0:T(2,128)(2,1)S(1)} %head.1.refs_0_.after), channel_id=1, source_target_pairs={{0,1},{1,0},{2,3},{3,2},{4,5},{5,4},{6,7},{7,6},{8,9},{9,8},{10,11... | collective-permute-start | bytes 18440 | tf_op jit(solution)/shard_map/ppermute | solution.py:33
  1.5 2.6 %collective-permute-start.1 = (bf16[2,1536]{1,0:T(2,128)(2,1)S(1)}, bf16[2,1536]{1,0:T(2,128)(2,1)S(1)}, u32[]{:S(2)}, u32[]{:S(2)}) collective-permute-start(bf16[2,1536]{1,0:T(2,128)(2,1)S(1)} %head.1.refs_0_.after), channel_id=1, source_target_pairs={{0,2},{1,3},{2,0},{3,1},{4,6},{5,7},{6,4},{7,5},{8,10},{9,11},{10,... | collective-permute-start | bytes 18440 | tf_op jit(solution)/shard_map/ppermute | solution.py:33
  4.1 0.0 collective-permute-start.2
  4.1 0.1 shard_map.140
  4.3 0.2 collective-permute-start.15
  4.5 1.9 %collective-permute-start.16 = (bf16[192,384]{1,0:T(8,128)(2,1)S(1)}, bf16[192,384]{1,0:T(8,128)(2,1)S(1)}, u32[]{:S(2)}, u32[]{:S(2)}) collective-permute-start(bf16[192,384]{1,0:T(8,128)(2,1)S(1)} %get-tuple-element.38), channel_id=1, source_target_pairs={{0,2},{1,3},{2,0},{3,1},{4,6},{5,7},{6,4},{7,5},{8,10},{9,11},{10,... | collective-permute-start | bytes 442376 | tf_op jit(solution)/shard_map/ppermute | solution.py:33
  6.4 0.3 convert_reduce_fusion
  6.8 0.0 collective-permute-done.1.refs_2_
  6.8 0.4 collective-permute-done.2.refs_3_
  7.2 0.4 shard_map.136
  7.5 0.2 collective-permute-start.3
  7.8 0.5 %collective-permute-start.4 = (bf16[8,768]{1,0:T(8,128)(2,1)S(1)}, bf16[8,768]{1,0:T(8,128)(2,1)S(1)}, u32[]{:S(2)}, u32[]{:S(2)}) collective-permute-start(bf16[8,768]{1,0:T(8,128)(2,1)S(1)} %get-tuple-element.27.refs_0_), channel_id=1, source_target_pairs={{0,2},{1,3},{2,0},{3,1},{4,6},{5,7},{6,4},{7,5},{8,10},{9,11},{10,... | collective-permute-start | bytes 36872 | tf_op jit(solution)/shard_map/ppermute | solution.py:33
  8.2 1.2 %collective-permute-start.5 = (bf16[8,768]{1,0:T(8,128)(2,1)S(1)}, bf16[8,768]{1,0:T(8,128)(2,1)S(1)}, u32[]{:S(2)}, u32[]{:S(2)}) collective-permute-start(bf16[8,768]{1,0:T(8,128)(2,1)S(1)} %get-tuple-element.27.refs_0_), channel_id=1, source_target_pairs={{0,3},{1,2},{2,1},{3,0},{4,7},{5,6},{6,5},{7,4},{8,11},{9,10},{10,... | collective-permute-start | bytes 36872 | tf_op jit(solution)/shard_map/ppermute | solution.py:33
  9.4 0.5 %fusion.2 = f32[2,256]{1,0:T(2,128)S(1)} fusion(bf16[2,256,1536]{2,1,0:T(8,128)(2,1)S(1)} %copy-done.10, f32[2,256]{1,0:T(2,128)S(1)} %broadcast_multiply_fusion), kind=kLoop, calls=%fused_computation.4 | loop fusion | flops 3145216 | bytes 1576960 | tf_op jit(solution)/shard_map/reduce_sum | solution.py:61
  10.0 0.0 collective-permute-done.3.refs_1_
  10.0 0.6 %collective-permute-start.17 = (bf16[192,384]{1,0:T(8,128)(2,1)S(1)}, bf16[192,384]{1,0:T(8,128)(2,1)S(1)}, u32[]{:S(2)}, u32[]{:S(2)}) collective-permute-start(bf16[192,384]{1,0:T(8,128)(2,1)S(1)} %get-tuple-element.39), channel_id=1, source_target_pairs={{0,3},{1,2},{2,1},{3,0},{4,7},{5,6},{6,5},{7,4},{8,11},{9,10},{10,... | collective-permute-start | bytes 442376 | tf_op jit(solution)/shard_map/ppermute | solution.py:33
  10.6 0.9 %collective-permute-done.4.refs_2_ = bf16[8,768]{1,0:T(8,128)(2,1)S(1)} collective-permute-done((bf16[8,768]{1,0:T(8,128)(2,1)S(1)}, bf16[8,768]{1,0:T(8,128)(2,1)S(1)}, u32[]{:S(2)}, u32[]{:S(2)}) %collective-permute-start.4) | collective-permute-done | bytes 12320 | tf_op jit(solution)/shard_map/ppermute | solution.py:33
  11.5 0.4 shard_map.137
  11.9 0.2 collective-permute-start.6
  12.1 1.4 %collective-permute-start.7 = (bf16[24,384]{1,0:T(8,128)(2,1)S(1)}, bf16[24,384]{1,0:T(8,128)(2,1)S(1)}, u32[]{:S(2)}, u32[]{:S(2)}) collective-permute-start(bf16[24,384]{1,0:T(8,128)(2,1)S(1)} %get-tuple-element.30), channel_id=1, source_target_pairs={{0,2},{1,3},{2,0},{3,1},{4,6},{5,7},{6,4},{7,5},{8,10},{9,11},{10,... | collective-permute-start | bytes 55304 | tf_op jit(solution)/shard_map/ppermute | solution.py:33
  13.5 0.8 %collective-permute-start.8 = (bf16[24,384]{1,0:T(8,128)(2,1)S(1)}, bf16[24,384]{1,0:T(8,128)(2,1)S(1)}, u32[]{:S(2)}, u32[]{:S(2)}) collective-permute-start(bf16[24,384]{1,0:T(8,128)(2,1)S(1)} %get-tuple-element.31), channel_id=1, source_target_pairs={{0,3},{1,2},{2,1},{3,0},{4,7},{5,6},{6,5},{7,4},{8,11},{9,10},{10,... | collective-permute-start | bytes 55304 | tf_op jit(solution)/shard_map/ppermute | solution.py:33
  14.3 0.5 %fusion.4.refs_4_ = bf16[2,256,1536]{2,1,0:T(8,128)(2,1)S(1)} fusion(bf16[2,256,1536]{2,1,0:T(8,128)(2,1)S(1)} %copy-done.10, f32[1536]{0:T(1024)S(1)} %copy-done.11, f32[2,256]{1,0:T(2,128)S(1)} %add_rsqrt_fusion, f32[2,256]{1,0:T(2,128)S(1)} %broadcast_multiply_fusion), kind=kLoop, calls=%fused_computation.6 | loop fusion | flops 3932160 | bytes 3155968 | tf_op jit(solution)/shard_map/convert_element_type | solution.py:62
  14.9 0.0 copy-start.3
  14.9 0.0 copy-start.9
  14.9 0.0 copy-start.4
  14.9 1.8 %collective-permute-done.7.refs_2_ = bf16[24,384]{1,0:T(8,128)(2,1)S(1)} collective-permute-done((bf16[24,384]{1,0:T(8,128)(2,1)S(1)}, bf16[24,384]{1,0:T(8,128)(2,1)S(1)}, u32[]{:S(2)}, u32[]{:S(2)}) %collective-permute-start.7) | collective-permute-done | bytes 18464 | tf_op jit(solution)/shard_map/ppermute | solution.py:33
  16.7 0.1 collective-permute-done.8.refs_3_
  16.8 1.0 %shard_map.138 = (bf16[24,384]{1,0:T(8,128)(2,1)S(1)}, bf16[24,384]{1,0:T(8,128)(2,1)S(1)}, bf16[24,384]{1,0:T(8,128)(2,1)S(1)}, bf16[24,384]{1,0:T(8,128)(2,1)S(1)}) custom-call(s32[1]{0:T(128)} %bitcast.place.refs_0_, bf16[24,384]{1,0:T(8,128)(2,1)S(1)} %get-tuple-element.28.refs_0_, bf16[24,384]{1,0:T(8,128)(2,1)S(1)} %collective-permute-done.6.refs_1_, ...), custom_call_target="tpu_custom_call" | custom-call | tf_op jit(solution)/shard_map/pallas_call | solution.py:80
  17.8 0.0 copy-start.6
  17.8 0.0 copy-start.7
  17.8 0.0 copy-start.8
  17.8 1.0 %collective-permute-start.10 = (bf16[24,384]{1,0:T(8,128)(2,1)S(1)}, bf16[24,384]{1,0:T(8,128)(2,1)S(1)}, u32[]{:S(2)}, u32[]{:S(2)}) collective-permute-start(bf16[24,384]{1,0:T(8,128)(2,1)S(1)} %get-tuple-element.34), channel_id=1, source_target_pairs={{0,2},{1,3},{2,0},{3,1},{4,6},{5,7},{6,4},{7,5},{8,10},{9,11},{10,... | collective-permute-start | bytes 55304 | tf_op jit(solution)/shard_map/ppermute | solution.py:33
  18.9 0.5 %collective-permute-start.11 = (bf16[24,384]{1,0:T(8,128)(2,1)S(1)}, bf16[24,384]{1,0:T(8,128)(2,1)S(1)}, u32[]{:S(2)}, u32[]{:S(2)}) collective-permute-start(bf16[24,384]{1,0:T(8,128)(2,1)S(1)} %get-tuple-element.35), channel_id=1, source_target_pairs={{0,3},{1,2},{2,1},{3,0},{4,7},{5,6},{6,5},{7,4},{8,11},{9,10},{10,... | collective-permute-start | bytes 55304 | tf_op jit(solution)/shard_map/ppermute | solution.py:33
  19.4 2.3 %collective-permute-done.10.refs_2_ = bf16[24,384]{1,0:T(8,128)(2,1)S(1)} collective-permute-done((bf16[24,384]{1,0:T(8,128)(2,1)S(1)}, bf16[24,384]{1,0:T(8,128)(2,1)S(1)}, u32[]{:S(2)}, u32[]{:S(2)}) %collective-permute-start.10) | collective-permute-done | bytes 18464 | tf_op jit(solution)/shard_map/ppermute | solution.py:33
  21.7 0.5 %collective-permute-done.11.refs_3_ = bf16[24,384]{1,0:T(8,128)(2,1)S(1)} collective-permute-done((bf16[24,384]{1,0:T(8,128)(2,1)S(1)}, bf16[24,384]{1,0:T(8,128)(2,1)S(1)}, u32[]{:S(2)}, u32[]{:S(2)}) %collective-permute-start.11) | collective-permute-done | bytes 18464 | tf_op jit(solution)/shard_map/ppermute | solution.py:33
  22.2 0.7 %collective-permute-done.9.refs_1_ = bf16[24,384]{1,0:T(8,128)(2,1)S(1)} collective-permute-done((bf16[24,384]{1,0:T(8,128)(2,1)S(1)}, bf16[24,384]{1,0:T(8,128)(2,1)S(1)}, u32[]{:S(2)}, u32[]{:S(2)}) %collective-permute-start.9) | collective-permute-done | bytes 18464 | tf_op jit(solution)/shard_map/ppermute | solution.py:33
  22.9 0.3 shard_map.139.refs_0_.after
  23.2 0.2 collective-permute-start.12
  23.4 1.0 %collective-permute-start.13 = (bf16[8,768]{1,0:T(8,128)(2,1)S(1)}, bf16[8,768]{1,0:T(8,128)(2,1)S(1)}, u32[]{:S(2)}, u32[]{:S(2)}) collective-permute-start(bf16[8,768]{1,0:T(8,128)(2,1)S(1)} %shard_map.139.refs_0_.after), channel_id=1, source_target_pairs={{0,2},{1,3},{2,0},{3,1},{4,6},{5,7},{6,4},{7,5},{8,10},{9,11},{10,... | collective-permute-start | bytes 36872 | tf_op jit(solution)/shard_map/ppermute | solution.py:33
  24.4 0.0 collective-permute-done.12.refs_1_
  24.4 0.7 %collective-permute-start.14 = (bf16[8,768]{1,0:T(8,128)(2,1)S(1)}, bf16[8,768]{1,0:T(8,128)(2,1)S(1)}, u32[]{:S(2)}, u32[]{:S(2)}) collective-permute-start(bf16[8,768]{1,0:T(8,128)(2,1)S(1)} %shard_map.139.refs_0_.after), channel_id=1, source_target_pairs={{0,3},{1,2},{2,1},{3,0},{4,7},{5,6},{6,5},{7,4},{8,11},{9,10},{10,... | collective-permute-start | bytes 36872 | tf_op jit(solution)/shard_map/ppermute | solution.py:33
  25.8 0.6 %shard_map.141.refs_10_ = bf16[8,128]{1,0:T(8,128)(2,1)S(1)} custom-call(s32[1]{0:T(128)} %bitcast.place.refs_0_, s32[2]{0:T(128)S(1)} %copy-done.9, s32[1]{0:T(128)S(6)} %copy.15.counts, bf16[2,1536]{1,0:T(2,128)(2,1)S(1)} %head.1.refs_0_.after), custom_call_target="tpu_custom_call" | custom-call | tf_op jit(solution)/shard_map/pallas_call | solution.py:80
  26.4 0.7 %collective-permute-done.13.refs_2_ = bf16[8,768]{1,0:T(8,128)(2,1)S(1)} collective-permute-done((bf16[8,768]{1,0:T(8,128)(2,1)S(1)}, bf16[8,768]{1,0:T(8,128)(2,1)S(1)}, u32[]{:S(2)}, u32[]{:S(2)}) %collective-permute-start.13) | collective-permute-done | bytes 12320 | tf_op jit(solution)/shard_map/ppermute | solution.py:33
  27.1 0.4 collective-permute-done.14.refs_3_
  27.5 0.4 shard_map.142.refs_1_
  28.0 0.2 collective-permute-start.18
  28.2 1.0 %collective-permute-start.19 = (bf16[8,896]{1,0:T(8,128)(2,1)S(1)}, bf16[8,896]{1,0:T(8,128)(2,1)S(1)}, u32[]{:S(2)}, u32[]{:S(2)}) collective-permute-start(bf16[8,896]{1,0:T(8,128)(2,1)S(1)} %shard_map.142.refs_1_), channel_id=1, source_target_pairs={{0,2},{1,3},{2,0},{3,1},{4,6},{5,7},{6,4},{7,5},{8,10},{9,11},{10,... | collective-permute-start | bytes 43016 | tf_op jit(solution)/shard_map/ppermute | solution.py:33
  29.1 0.7 %collective-permute-start.20 = (bf16[8,896]{1,0:T(8,128)(2,1)S(1)}, bf16[8,896]{1,0:T(8,128)(2,1)S(1)}, u32[]{:S(2)}, u32[]{:S(2)}) collective-permute-start(bf16[8,896]{1,0:T(8,128)(2,1)S(1)} %shard_map.142.refs_1_), channel_id=1, source_target_pairs={{0,3},{1,2},{2,1},{3,0},{4,7},{5,6},{6,5},{7,4},{8,11},{9,10},{10,... | collective-permute-start | bytes 43016 | tf_op jit(solution)/shard_map/ppermute | solution.py:33
  29.9 2.0 %collective-permute-done.19.refs_3_ = bf16[8,896]{1,0:T(8,128)(2,1)S(1)} collective-permute-done((bf16[8,896]{1,0:T(8,128)(2,1)S(1)}, bf16[8,896]{1,0:T(8,128)(2,1)S(1)}, u32[]{:S(2)}, u32[]{:S(2)}) %collective-permute-start.19) | collective-permute-done | bytes 14368 | tf_op jit(solution)/shard_map/ppermute | solution.py:33
  31.9 0.4 collective-permute-done.20.refs_4_
  32.3 0.1 shard_map.143.refs_0_
  32.3 1.6 %collective-permute-start.21 = (bf16[8,896]{1,0:T(8,128)(2,1)S(1)}, bf16[8,896]{1,0:T(8,128)(2,1)S(1)}, u32[]{:S(2)}, u32[]{:S(2)}) collective-permute-start(bf16[8,896]{1,0:T(8,128)(2,1)S(1)} %shard_map.143.refs_0_), channel_id=1, source_target_pairs={{0,4},{1,9},{2,6},{3,11},{4,0},{5,13},{6,2},{7,15},{8,12},{9,1},{1... | collective-permute-start | bytes 43016 | tf_op jit(solution)/shard_map/ppermute | solution.py:50
  34.0 2.5 %collective-permute-start.23 = (bf16[8,896]{1,0:T(8,128)(2,1)S(1)}, bf16[8,896]{1,0:T(8,128)(2,1)S(1)}, u32[]{:S(2)}, u32[]{:S(2)}) collective-permute-start(bf16[8,896]{1,0:T(8,128)(2,1)S(1)} %shard_map.143.refs_0_), channel_id=1, source_target_pairs={{0,12},{4,8},{8,4},{12,0},{1,13},{5,9},{9,5},{13,1},{2,14},{6,10},... | collective-permute-start | bytes 43016 | tf_op jit(solution)/shard_map/ppermute | solution.py:33
  36.5 0.1 shard_map.144
  36.6 2.9 %collective-permute-done.23.refs_3_ = bf16[8,896]{1,0:T(8,128)(2,1)S(1)} collective-permute-done((bf16[8,896]{1,0:T(8,128)(2,1)S(1)}, bf16[8,896]{1,0:T(8,128)(2,1)S(1)}, u32[]{:S(2)}, u32[]{:S(2)}) %collective-permute-start.23) | collective-permute-done | bytes 14368 | tf_op jit(solution)/shard_map/ppermute | solution.py:33
  39.5 1.1 %shard_map.145 = (bf16[8,192]{1,0:T(8,128)(2,1)S(1)}, bf16[8,192]{1,0:T(8,128)(2,1)S(1)}, bf16[8,192]{1,0:T(8,128)(2,1)S(1)}, bf16[8,192]{1,0:T(8,128)(2,1)S(1)}) custom-call(s32[1]{0:T(128)} %bitcast.place.refs_0_, bf16[8,896]{1,0:T(8,128)(2,1)S(1)} %shard_map.143.refs_0_, bf16[8,896]{1,0:T(8,128)(2,1)S(1)} %collective-permute-done.21.refs_1_, ...), custom_call_target="tpu_custom_call" | custom-call | tf_op jit(solution)/shard_map/pallas_call | solution.py:80
  40.6 0.0 collective-permute-start.24
  40.7 1.1 %collective-permute-start.25 = (bf16[8,192]{1,0:T(8,128)(2,1)S(1)}, bf16[8,192]{1,0:T(8,128)(2,1)S(1)}, u32[]{:S(2)}, u32[]{:S(2)}) collective-permute-start(bf16[8,192]{1,0:T(8,128)(2,1)S(1)} %get-tuple-element.47), channel_id=1, source_target_pairs={{0,2},{1,3},{2,0},{3,1},{4,6},{5,7},{6,4},{7,5},{8,10},{9,11},{10,... | collective-permute-start | bytes 9224 | tf_op jit(solution)/shard_map/ppermute | solution.py:33
  41.8 0.7 %collective-permute-start.26 = (bf16[8,192]{1,0:T(8,128)(2,1)S(1)}, bf16[8,192]{1,0:T(8,128)(2,1)S(1)}, u32[]{:S(2)}, u32[]{:S(2)}) collective-permute-start(bf16[8,192]{1,0:T(8,128)(2,1)S(1)} %get-tuple-element.48), channel_id=1, source_target_pairs={{0,3},{1,2},{2,1},{3,0},{4,7},{5,6},{6,5},{7,4},{8,11},{9,10},{10,... | collective-permute-start | bytes 9224 | tf_op jit(solution)/shard_map/ppermute | solution.py:33
  42.5 0.3 shard_map.146
  42.9 1.5 %collective-permute-done.25 = bf16[8,192]{1,0:T(8,128)(2,1)S(1)} collective-permute-done((bf16[8,192]{1,0:T(8,128)(2,1)S(1)}, bf16[8,192]{1,0:T(8,128)(2,1)S(1)}, u32[]{:S(2)}, u32[]{:S(2)}) %collective-permute-start.25) | collective-permute-done | bytes 3104 | tf_op jit(solution)/shard_map/ppermute | solution.py:33
  44.4 0.5 %collective-permute-done.26 = bf16[8,192]{1,0:T(8,128)(2,1)S(1)} collective-permute-done((bf16[8,192]{1,0:T(8,128)(2,1)S(1)}, bf16[8,192]{1,0:T(8,128)(2,1)S(1)}, u32[]{:S(2)}, u32[]{:S(2)}) %collective-permute-start.26) | collective-permute-done | bytes 3104 | tf_op jit(solution)/shard_map/ppermute | solution.py:33
  44.8 0.6 %add_convert_fusion = bf16[8,192]{1,0:T(8,128)(2,1)} fusion(f32[8,192]{1,0:T(8,128)S(1)} %shard_map.146, bf16[8,192]{1,0:T(8,128)(2,1)S(1)} %collective-permute-done.26, bf16[8,192]{1,0:T(8,128)(2,1)S(1)} %collective-permute-done.25, bf16[8,192]{1,0:T(8,128)(2,1)S(1)} %collective-permute-done.24, bf16[8,192]{1,0:T(8,128)(2,1)S(1)} %get-tuple-element.45.refs_4_), kind=kLoop, calls=%fused_computation.7 | loop fusion | flops 13824 | bytes 21504 | tf_op jit(solution)/shard_map/convert_element_type | solution.py:425
  (36 shorter events, 0.1 us)
Async XLA Ops:
  0.0 4.1 %copy-start = (bf16[192,1536]{1,0:T(8,128)(2,1)S(1)}, bf16[192,1536]{1,0:T(8,128)(2,1)}, u32[]{:S(2)}) copy-start(bf16[192,1536]{1,0:T(8,128)(2,1)} %weight.2) | copy-start | bytes 1769476
  0.0 6.4 %copy-start.10 = (bf16[2,256,1536]{2,1,0:T(8,128)(2,1)S(1)}, bf16[2,256,1536]{2,1,0:T(8,128)(2,1)}, u32[]{:S(2)}) copy-start(bf16[2,256,1536]{2,1,0:T(8,128)(2,1)} %tokens.1) | copy-start | bytes 4718596
  0.0 6.7 %copy-start.11 = (f32[1536]{0:T(1024)S(1)}, f32[1536]{0:T(1024)}, u32[]{:S(2)}) copy-start(f32[1536]{0:T(1024)} %param.15) | copy-start | bytes 18436
  0.0 7.2 %copy-start.1 = (bf16[384,768]{1,0:T(8,128)(2,1)S(1)}, bf16[384,768]{1,0:T(8,128)(2,1)}, u32[]{:S(2)}) copy-start(bf16[384,768]{1,0:T(8,128)(2,1)} %refs_5_.1) | copy-start | bytes 1769476
  1.0 5.8 %collective-permute-start = (bf16[2,1536]{1,0:T(2,128)(2,1)S(1)}, bf16[2,1536]{1,0:T(2,128)(2,1)S(1)}, u32[]{:S(2)}, u32[]{:S(2)}) collective-permute-start(bf16[2,1536]{1,0:T(2,128)(2,1)S(1)} %head.1.refs_0_.after), channel_id=1, source_target_pairs={{0,1},{1,0},{2,3},{3,2},{4,5},{5,4},{6,7},{7,6},{8,9},{9,8},{10,11... | collective-permute-start | bytes 18440 | tf_op jit(solution)/shard_map/ppermute | solution.py:33
  1.5 5.2 %collective-permute-start.1 = (bf16[2,1536]{1,0:T(2,128)(2,1)S(1)}, bf16[2,1536]{1,0:T(2,128)(2,1)S(1)}, u32[]{:S(2)}, u32[]{:S(2)}) collective-permute-start(bf16[2,1536]{1,0:T(2,128)(2,1)S(1)} %head.1.refs_0_.after), channel_id=1, source_target_pairs={{0,2},{1,3},{2,0},{3,1},{4,6},{5,7},{6,4},{7,5},{8,10},{9,11},{10,... | collective-permute-start | bytes 18440 | tf_op jit(solution)/shard_map/ppermute | solution.py:33
  4.1 3.1 %collective-permute-start.2 = (bf16[2,1536]{1,0:T(2,128)(2,1)S(1)}, bf16[2,1536]{1,0:T(2,128)(2,1)S(1)}, u32[]{:S(2)}, u32[]{:S(2)}) collective-permute-start(bf16[2,1536]{1,0:T(2,128)(2,1)S(1)} %head.1.refs_0_.after), channel_id=1, source_target_pairs={{0,3},{1,2},{2,1},{3,0},{4,7},{5,6},{6,5},{7,4},{8,11},{9,10},{10,... | collective-permute-start | bytes 18440 | tf_op jit(solution)/shard_map/ppermute | solution.py:33
  4.3 23.3 %collective-permute-start.15 = (bf16[192,384]{1,0:T(8,128)(2,1)S(1)}, bf16[192,384]{1,0:T(8,128)(2,1)S(1)}, u32[]{:S(2)}, u32[]{:S(2)}) collective-permute-start(bf16[192,384]{1,0:T(8,128)(2,1)S(1)} %get-tuple-element.37), channel_id=1, source_target_pairs={{0,1},{1,0},{2,3},{3,2},{4,5},{5,4},{6,7},{7,6},{8,9},{9,8},{10,11... | collective-permute-start | bytes 442376 | tf_op jit(solution)/shard_map/ppermute | solution.py:33
  4.5 7.0 %copy-start.2 = (bf16[384,768]{1,0:T(8,128)(2,1)S(1)}, bf16[384,768]{1,0:T(8,128)(2,1)}, u32[]{:S(2)}) copy-start(bf16[384,768]{1,0:T(8,128)(2,1)} %refs_4_.2) | copy-start | bytes 1769476
  4.5 23.0 %collective-permute-start.16 = (bf16[192,384]{1,0:T(8,128)(2,1)S(1)}, bf16[192,384]{1,0:T(8,128)(2,1)S(1)}, u32[]{:S(2)}, u32[]{:S(2)}) collective-permute-start(bf16[192,384]{1,0:T(8,128)(2,1)S(1)} %get-tuple-element.38), channel_id=1, source_target_pairs={{0,2},{1,3},{2,0},{3,1},{4,6},{5,7},{6,4},{7,5},{8,10},{9,11},{10,... | collective-permute-start | bytes 442376 | tf_op jit(solution)/shard_map/ppermute | solution.py:33
  7.5 2.4 %collective-permute-start.3 = (bf16[8,768]{1,0:T(8,128)(2,1)S(1)}, bf16[8,768]{1,0:T(8,128)(2,1)S(1)}, u32[]{:S(2)}, u32[]{:S(2)}) collective-permute-start(bf16[8,768]{1,0:T(8,128)(2,1)S(1)} %get-tuple-element.27.refs_0_), channel_id=1, source_target_pairs={{0,1},{1,0},{2,3},{3,2},{4,5},{5,4},{6,7},{7,6},{8,9},{9,8},{10,11... | collective-permute-start | bytes 36872 | tf_op jit(solution)/shard_map/ppermute | solution.py:33
  7.8 3.7 %collective-permute-start.4 = (bf16[8,768]{1,0:T(8,128)(2,1)S(1)}, bf16[8,768]{1,0:T(8,128)(2,1)S(1)}, u32[]{:S(2)}, u32[]{:S(2)}) collective-permute-start(bf16[8,768]{1,0:T(8,128)(2,1)S(1)} %get-tuple-element.27.refs_0_), channel_id=1, source_target_pairs={{0,2},{1,3},{2,0},{3,1},{4,6},{5,7},{6,4},{7,5},{8,10},{9,11},{10,... | collective-permute-start | bytes 36872 | tf_op jit(solution)/shard_map/ppermute | solution.py:33
  8.2 3.3 %collective-permute-start.5 = (bf16[8,768]{1,0:T(8,128)(2,1)S(1)}, bf16[8,768]{1,0:T(8,128)(2,1)S(1)}, u32[]{:S(2)}, u32[]{:S(2)}) collective-permute-start(bf16[8,768]{1,0:T(8,128)(2,1)S(1)} %get-tuple-element.27.refs_0_), channel_id=1, source_target_pairs={{0,3},{1,2},{2,1},{3,0},{4,7},{5,6},{6,5},{7,4},{8,11},{9,10},{10,... | collective-permute-start | bytes 36872 | tf_op jit(solution)/shard_map/ppermute | solution.py:33
  10.0 17.5 %collective-permute-start.17 = (bf16[192,384]{1,0:T(8,128)(2,1)S(1)}, bf16[192,384]{1,0:T(8,128)(2,1)S(1)}, u32[]{:S(2)}, u32[]{:S(2)}) collective-permute-start(bf16[192,384]{1,0:T(8,128)(2,1)S(1)} %get-tuple-element.39), channel_id=1, source_target_pairs={{0,3},{1,2},{2,1},{3,0},{4,7},{5,6},{6,5},{7,4},{8,11},{9,10},{10,... | collective-permute-start | bytes 442376 | tf_op jit(solution)/shard_map/ppermute | solution.py:33
  11.9 1.6 %collective-permute-start.6 = (bf16[24,384]{1,0:T(8,128)(2,1)S(1)}, bf16[24,384]{1,0:T(8,128)(2,1)S(1)}, u32[]{:S(2)}, u32[]{:S(2)}) collective-permute-start(bf16[24,384]{1,0:T(8,128)(2,1)S(1)} %get-tuple-element.29), channel_id=1, source_target_pairs={{0,1},{1,0},{2,3},{3,2},{4,5},{5,4},{6,7},{7,6},{8,9},{9,8},{10,11... | collective-permute-start | bytes 55304 | tf_op jit(solution)/shard_map/ppermute | solution.py:33
  12.1 4.6 %collective-permute-start.7 = (bf16[24,384]{1,0:T(8,128)(2,1)S(1)}, bf16[24,384]{1,0:T(8,128)(2,1)S(1)}, u32[]{:S(2)}, u32[]{:S(2)}) collective-permute-start(bf16[24,384]{1,0:T(8,128)(2,1)S(1)} %get-tuple-element.30), channel_id=1, source_target_pairs={{0,2},{1,3},{2,0},{3,1},{4,6},{5,7},{6,4},{7,5},{8,10},{9,11},{10,... | collective-permute-start | bytes 55304 | tf_op jit(solution)/shard_map/ppermute | solution.py:33
  13.5 3.3 %collective-permute-start.8 = (bf16[24,384]{1,0:T(8,128)(2,1)S(1)}, bf16[24,384]{1,0:T(8,128)(2,1)S(1)}, u32[]{:S(2)}, u32[]{:S(2)}) collective-permute-start(bf16[24,384]{1,0:T(8,128)(2,1)S(1)} %get-tuple-element.31), channel_id=1, source_target_pairs={{0,3},{1,2},{2,1},{3,0},{4,7},{5,6},{6,5},{7,4},{8,11},{9,10},{10,... | collective-permute-start | bytes 55304 | tf_op jit(solution)/shard_map/ppermute | solution.py:33
  14.9 8.0 %copy-start.3 = (bf16[384,768]{1,0:T(8,128)(2,1)S(1)}, bf16[384,768]{1,0:T(8,128)(2,1)}, u32[]{:S(2)}) copy-start(bf16[384,768]{1,0:T(8,128)(2,1)} %refs_4_.3) | copy-start | bytes 1769476
  14.9 10.9 %copy-start.9 = (s32[2]{0:T(128)S(1)}, s32[2]{0:T(128)}, u32[]{:S(2)}) copy-start(s32[2]{0:T(128)} %order.1) | copy-start | bytes 28
  14.9 12.6 %copy-start.4 = (bf16[384,768]{1,0:T(8,128)(2,1)S(1)}, bf16[384,768]{1,0:T(8,128)(2,1)}, u32[]{:S(2)}) copy-start(bf16[384,768]{1,0:T(8,128)(2,1)} %refs_9_.1) | copy-start | bytes 1769476
  16.8 19.7 %copy-start.12 = (f32[768]{0:T(1024)S(1)}, f32[768]{0:T(1024)}, u32[]{:S(2)}) copy-start(f32[768]{0:T(1024)} %param.21) | copy-start | bytes 9220
  16.8 19.7 %copy-start.5 = (bf16[192,768]{1,0:T(8,128)(2,1)S(1)}, bf16[192,768]{1,0:T(8,128)(2,1)}, u32[]{:S(2)}) copy-start(bf16[192,768]{1,0:T(8,128)(2,1)} %weight.3) | copy-start | bytes 884740
  17.8 21.7 %copy-start.6 = (bf16[768,192]{0,1:T(8,128)(2,1)S(1)}, bf16[768,192]{0,1:T(8,128)(2,1)}, u32[]{:S(2)}) copy-start(bf16[768,192]{0,1:T(8,128)(2,1)} %param.22) | copy-start | bytes 884740
  17.8 21.7 %copy-start.7 = (bf16[768,192]{0,1:T(8,128)(2,1)S(1)}, bf16[768,192]{0,1:T(8,128)(2,1)}, u32[]{:S(2)}) copy-start(bf16[768,192]{0,1:T(8,128)(2,1)} %param.23) | copy-start | bytes 884740
  17.8 21.7 %copy-start.8 = (bf16[768,192]{0,1:T(8,128)(2,1)S(1)}, bf16[768,192]{0,1:T(8,128)(2,1)}, u32[]{:S(2)}) copy-start(bf16[768,192]{0,1:T(8,128)(2,1)} %param.24) | copy-start | bytes 884740
  17.8 3.8 %collective-permute-start.10 = (bf16[24,384]{1,0:T(8,128)(2,1)S(1)}, bf16[24,384]{1,0:T(8,128)(2,1)S(1)}, u32[]{:S(2)}, u32[]{:S(2)}) collective-permute-start(bf16[24,384]{1,0:T(8,128)(2,1)S(1)} %get-tuple-element.34), channel_id=1, source_target_pairs={{0,2},{1,3},{2,0},{3,1},{4,6},{5,7},{6,4},{7,5},{8,10},{9,11},{10,... | collective-permute-start | bytes 55304 | tf_op jit(solution)/shard_map/ppermute | solution.py:33
  18.9 3.3 %collective-permute-start.11 = (bf16[24,384]{1,0:T(8,128)(2,1)S(1)}, bf16[24,384]{1,0:T(8,128)(2,1)S(1)}, u32[]{:S(2)}, u32[]{:S(2)}) collective-permute-start(bf16[24,384]{1,0:T(8,128)(2,1)S(1)} %get-tuple-element.35), channel_id=1, source_target_pairs={{0,3},{1,2},{2,1},{3,0},{4,7},{5,6},{6,5},{7,4},{8,11},{9,10},{10,... | collective-permute-start | bytes 55304 | tf_op jit(solution)/shard_map/ppermute | solution.py:33
  21.7 1.2 %collective-permute-start.9 = (bf16[24,384]{1,0:T(8,128)(2,1)S(1)}, bf16[24,384]{1,0:T(8,128)(2,1)S(1)}, u32[]{:S(2)}, u32[]{:S(2)}) collective-permute-start(bf16[24,384]{1,0:T(8,128)(2,1)S(1)} %get-tuple-element.33), channel_id=1, source_target_pairs={{0,1},{1,0},{2,3},{3,2},{4,5},{5,4},{6,7},{7,6},{8,9},{9,8},{10,11... | collective-permute-start | bytes 55304 | tf_op jit(solution)/shard_map/ppermute | solution.py:33
  23.2 1.2 %collective-permute-start.12 = (bf16[8,768]{1,0:T(8,128)(2,1)S(1)}, bf16[8,768]{1,0:T(8,128)(2,1)S(1)}, u32[]{:S(2)}, u32[]{:S(2)}) collective-permute-start(bf16[8,768]{1,0:T(8,128)(2,1)S(1)} %shard_map.139.refs_0_.after), channel_id=1, source_target_pairs={{0,1},{1,0},{2,3},{3,2},{4,5},{5,4},{6,7},{7,6},{8,9},{9,8},{10,11... | collective-permute-start | bytes 36872 | tf_op jit(solution)/shard_map/ppermute | solution.py:33
  23.4 3.7 %collective-permute-start.13 = (bf16[8,768]{1,0:T(8,128)(2,1)S(1)}, bf16[8,768]{1,0:T(8,128)(2,1)S(1)}, u32[]{:S(2)}, u32[]{:S(2)}) collective-permute-start(bf16[8,768]{1,0:T(8,128)(2,1)S(1)} %shard_map.139.refs_0_.after), channel_id=1, source_target_pairs={{0,2},{1,3},{2,0},{3,1},{4,6},{5,7},{6,4},{7,5},{8,10},{9,11},{10,... | collective-permute-start | bytes 36872 | tf_op jit(solution)/shard_map/ppermute | solution.py:33
  24.4 3.1 %collective-permute-start.14 = (bf16[8,768]{1,0:T(8,128)(2,1)S(1)}, bf16[8,768]{1,0:T(8,128)(2,1)S(1)}, u32[]{:S(2)}, u32[]{:S(2)}) collective-permute-start(bf16[8,768]{1,0:T(8,128)(2,1)S(1)} %shard_map.139.refs_0_.after), channel_id=1, source_target_pairs={{0,3},{1,2},{2,1},{3,0},{4,7},{5,6},{6,5},{7,4},{8,11},{9,10},{10,... | collective-permute-start | bytes 36872 | tf_op jit(solution)/shard_map/ppermute | solution.py:33
  28.0 1.9 %collective-permute-start.18 = (bf16[8,896]{1,0:T(8,128)(2,1)S(1)}, bf16[8,896]{1,0:T(8,128)(2,1)S(1)}, u32[]{:S(2)}, u32[]{:S(2)}) collective-permute-start(bf16[8,896]{1,0:T(8,128)(2,1)S(1)} %shard_map.142.refs_1_), channel_id=1, source_target_pairs={{0,1},{1,0},{2,3},{3,2},{4,5},{5,4},{6,7},{7,6},{8,9},{9,8},{10,11... | collective-permute-start | bytes 43016 | tf_op jit(solution)/shard_map/ppermute | solution.py:33
  28.2 3.7 %collective-permute-start.19 = (bf16[8,896]{1,0:T(8,128)(2,1)S(1)}, bf16[8,896]{1,0:T(8,128)(2,1)S(1)}, u32[]{:S(2)}, u32[]{:S(2)}) collective-permute-start(bf16[8,896]{1,0:T(8,128)(2,1)S(1)} %shard_map.142.refs_1_), channel_id=1, source_target_pairs={{0,2},{1,3},{2,0},{3,1},{4,6},{5,7},{6,4},{7,5},{8,10},{9,11},{10,... | collective-permute-start | bytes 43016 | tf_op jit(solution)/shard_map/ppermute | solution.py:33
  29.1 3.1 %collective-permute-start.20 = (bf16[8,896]{1,0:T(8,128)(2,1)S(1)}, bf16[8,896]{1,0:T(8,128)(2,1)S(1)}, u32[]{:S(2)}, u32[]{:S(2)}) collective-permute-start(bf16[8,896]{1,0:T(8,128)(2,1)S(1)} %shard_map.142.refs_1_), channel_id=1, source_target_pairs={{0,3},{1,2},{2,1},{3,0},{4,7},{5,6},{6,5},{7,4},{8,11},{9,10},{10,... | collective-permute-start | bytes 43016 | tf_op jit(solution)/shard_map/ppermute | solution.py:33
  32.3 4.1 %collective-permute-start.21 = (bf16[8,896]{1,0:T(8,128)(2,1)S(1)}, bf16[8,896]{1,0:T(8,128)(2,1)S(1)}, u32[]{:S(2)}, u32[]{:S(2)}) collective-permute-start(bf16[8,896]{1,0:T(8,128)(2,1)S(1)} %shard_map.143.refs_0_), channel_id=1, source_target_pairs={{0,4},{1,9},{2,6},{3,11},{4,0},{5,13},{6,2},{7,15},{8,12},{9,1},{1... | collective-permute-start | bytes 43016 | tf_op jit(solution)/shard_map/ppermute | solution.py:50
  34.0 5.5 %collective-permute-start.23 = (bf16[8,896]{1,0:T(8,128)(2,1)S(1)}, bf16[8,896]{1,0:T(8,128)(2,1)S(1)}, u32[]{:S(2)}, u32[]{:S(2)}) collective-permute-start(bf16[8,896]{1,0:T(8,128)(2,1)S(1)} %shard_map.143.refs_0_), channel_id=1, source_target_pairs={{0,12},{4,8},{8,4},{12,0},{1,13},{5,9},{9,5},{13,1},{2,14},{6,10},... | collective-permute-start | bytes 43016 | tf_op jit(solution)/shard_map/ppermute | solution.py:33
  36.4 3.1 %collective-permute-start.22 = (bf16[8,896]{1,0:T(8,128)(2,1)S(1)}, bf16[8,896]{1,0:T(8,128)(2,1)S(1)}, u32[]{:S(2)}, u32[]{:S(2)}) collective-permute-start(bf16[8,896]{1,0:T(8,128)(2,1)S(1)} %collective-permute-done.21.refs_1_), channel_id=1, source_target_pairs={{0,1},{1,0},{2,3},{3,2},{4,5},{5,4},{6,7},{7,6},{8,9},{9,8},{10,11... | collective-permute-start | bytes 43016 | tf_op jit(solution)/shard_map/ppermute | solution.py:33
  40.6 2.2 %collective-permute-start.24 = (bf16[8,192]{1,0:T(8,128)(2,1)S(1)}, bf16[8,192]{1,0:T(8,128)(2,1)S(1)}, u32[]{:S(2)}, u32[]{:S(2)}) collective-permute-start(bf16[8,192]{1,0:T(8,128)(2,1)S(1)} %get-tuple-element.46), channel_id=1, source_target_pairs={{0,1},{1,0},{2,3},{3,2},{4,5},{5,4},{6,7},{7,6},{8,9},{9,8},{10,11... | collective-permute-start | bytes 9224 | tf_op jit(solution)/shard_map/ppermute | solution.py:33
  40.7 3.7 %collective-permute-start.25 = (bf16[8,192]{1,0:T(8,128)(2,1)S(1)}, bf16[8,192]{1,0:T(8,128)(2,1)S(1)}, u32[]{:S(2)}, u32[]{:S(2)}) collective-permute-start(bf16[8,192]{1,0:T(8,128)(2,1)S(1)} %get-tuple-element.47), channel_id=1, source_target_pairs={{0,2},{1,3},{2,0},{3,1},{4,6},{5,7},{6,4},{7,5},{8,10},{9,11},{10,... | collective-permute-start | bytes 9224 | tf_op jit(solution)/shard_map/ppermute | solution.py:33
  41.8 3.0 %collective-permute-start.26 = (bf16[8,192]{1,0:T(8,128)(2,1)S(1)}, bf16[8,192]{1,0:T(8,128)(2,1)S(1)}, u32[]{:S(2)}, u32[]{:S(2)}) collective-permute-start(bf16[8,192]{1,0:T(8,128)(2,1)S(1)} %get-tuple-element.48), channel_id=1, source_target_pairs={{0,3},{1,2},{2,1},{3,0},{4,7},{5,6},{6,5},{7,4},{8,11},{9,10},{10,... | collective-permute-start | bytes 9224 | tf_op jit(solution)/shard_map/ppermute | solution.py:33

commit v2 on v1

--- a/solution.py
+++ b/solution.py
@@ -41,14 +41,15 @@
     size, seq_size = lax.axis_size("fsdp"), lax.axis_size("seq")
     if size % 2 or seq_size & (seq_size - 1) or seq_size < 4:
         return spread(array, "seq")
-    direct = [swap(array, "seq", step) for step in range(3, seq_size)]
     pairs = [
-        (row * size + place, (row ^ (1 + place % 2)) * size + place)
+        (row * size + place, (row ^ (2 + place % 2)) * size + place)
         for row in range(seq_size)
         for place in range(size)
     ]
-    near = lax.ppermute(array, ("seq", "fsdp"), pairs)
-    return [array, near, swap(near, "fsdp", 1), *direct]
+    far = lax.ppermute(array, ("seq", "fsdp"), pairs)
+    steps = [1, *range(4, seq_size)]
+    direct = [swap(array, "seq", step) for step in steps]
+    return [array, far, swap(far, "fsdp", 1), *direct]
 
 
 def deal(arrays, axis):

time: 45.6 us -> 44.8 us (0.982)
  waiting for transfers between devices: 15.1 us -> 14.2 us
    ppermute x26, waiting for transfers between devices: 15.1 us -> 13.8 us  [swap(): lax.ppermute(array, axis, [(i, other(i, step, size)) for i in range(size)])]
    ppermute x1, starting transfers between devices: 1.62 us -> 2.63 us  [rows_of_all(): far = lax.ppermute(array, ('seq', 'fsdp'), pairs)]
    ppermute x26, starting transfers between devices: 19.9 us -> 19 us  [swap(): lax.ppermute(array, axis, [(i, other(i, step, size)) for i in range(size)])]
  transfers between devices with their start and end apart: 27 -> 27, of which waited for: 14 -> 15; matrix products, arithmetic and copies ran while one was open for 3% -> 3% of each run, Pallas kernels for 7% -> 7%
where the time goes in v2:
time: 44.8 us; the launch traced here: 44.7 us
  starting transfers between devices  21.7 us (48%)
  waiting for transfers between devices  14.2 us (32%)
  Pallas kernels  5.88 us (13%)
  other arithmetic  1.97 us (4%)
  between operations  0.87 us (2%)
    ppermute x26, starting transfers between devices, swap(): lax.ppermute(array, axis, [(i, other(i, step, size)) for i in range(size)])  19 us
    ppermute x26, waiting for transfers between devices, swap(): lax.ppermute(array, axis, [(i, other(i, step, size)) for i in range(size)])  13.8 us
    pallas_call x11, Pallas kernels, run(): pl.pallas_call(body, out_shape=outs, in_specs=[smem] + [vmem] * last + [p...  4.92 us
    ppermute x1, starting transfers between devices, rows_of_all(): far = lax.ppermute(array, ('seq', 'fsdp'), pairs)  2.63 us
    pallas_call x1, Pallas kernels, local(): pl.pallas_call(head_kernel, out_shape=jax.ShapeDtypeStruct((tiles, width)...  0.97 us
  transfers between devices with their start and end apart: 27, of which 15 were waited for; matrix products, arithmetic and copies ran while one was open for 3% of the time, Pallas kernels for 7%

profile of v2, /device:TPU:0, one launch (start us, length us, event | category | flops | bytes accessed | tf_op | source)
XLA Modules:
  0.0 44.7 jit_solution(9029382432851108555)
XLA Ops:
  0.0 1.0 %head.1.refs_0_.after = bf16[2,1536]{1,0:T(2,128)(2,1)S(1)} custom-call(bf16[2,256,1536]{2,1,0:T(8,128)(2,1)} %tokens.1), custom_call_target="tpu_custom_call" | custom-call | tf_op jit(solution)/shard_map/head/pallas_call | solution.py:329
  1.0 0.6 %collective-permute-start = (bf16[2,1536]{1,0:T(2,128)(2,1)S(1)}, bf16[2,1536]{1,0:T(2,128)(2,1)S(1)}, u32[]{:S(2)}, u32[]{:S(2)}) collective-permute-start(bf16[2,1536]{1,0:T(2,128)(2,1)S(1)} %head.1.refs_0_.after), channel_id=1, source_target_pairs={{0,1},{1,0},{2,3},{3,2},{4,5},{5,4},{6,7},{7,6},{8,9},{9,8},{10,11... | collective-permute-start | bytes 18440 | tf_op jit(solution)/shard_map/ppermute | solution.py:33
  1.5 2.6 %collective-permute-start.1 = (bf16[2,1536]{1,0:T(2,128)(2,1)S(1)}, bf16[2,1536]{1,0:T(2,128)(2,1)S(1)}, u32[]{:S(2)}, u32[]{:S(2)}) collective-permute-start(bf16[2,1536]{1,0:T(2,128)(2,1)S(1)} %head.1.refs_0_.after), channel_id=1, source_target_pairs={{0,2},{1,3},{2,0},{3,1},{4,6},{5,7},{6,4},{7,5},{8,10},{9,11},{10,... | collective-permute-start | bytes 18440 | tf_op jit(solution)/shard_map/ppermute | solution.py:33
  4.1 0.0 collective-permute-start.2
  4.1 0.1 shard_map.140
  4.3 0.2 collective-permute-start.15
  4.5 1.9 %collective-permute-start.16 = (bf16[192,384]{1,0:T(8,128)(2,1)S(1)}, bf16[192,384]{1,0:T(8,128)(2,1)S(1)}, u32[]{:S(2)}, u32[]{:S(2)}) collective-permute-start(bf16[192,384]{1,0:T(8,128)(2,1)S(1)} %get-tuple-element.38), channel_id=1, source_target_pairs={{0,2},{1,3},{2,0},{3,1},{4,6},{5,7},{6,4},{7,5},{8,10},{9,11},{10,... | collective-permute-start | bytes 442376 | tf_op jit(solution)/shard_map/ppermute | solution.py:33
  6.4 0.3 convert_reduce_fusion
  6.8 0.0 collective-permute-done.1.refs_2_
  6.8 0.4 collective-permute-done.2.refs_3_
  7.2 0.4 shard_map.136
  7.5 0.2 collective-permute-start.3
  7.8 0.5 %collective-permute-start.4 = (bf16[8,768]{1,0:T(8,128)(2,1)S(1)}, bf16[8,768]{1,0:T(8,128)(2,1)S(1)}, u32[]{:S(2)}, u32[]{:S(2)}) collective-permute-start(bf16[8,768]{1,0:T(8,128)(2,1)S(1)} %get-tuple-element.27.refs_0_), channel_id=1, source_target_pairs={{0,2},{1,3},{2,0},{3,1},{4,6},{5,7},{6,4},{7,5},{8,10},{9,11},{10,... | collective-permute-start | bytes 36872 | tf_op jit(solution)/shard_map/ppermute | solution.py:33
  8.2 1.2 %collective-permute-start.5 = (bf16[8,768]{1,0:T(8,128)(2,1)S(1)}, bf16[8,768]{1,0:T(8,128)(2,1)S(1)}, u32[]{:S(2)}, u32[]{:S(2)}) collective-permute-start(bf16[8,768]{1,0:T(8,128)(2,1)S(1)} %get-tuple-element.27.refs_0_), channel_id=1, source_target_pairs={{0,3},{1,2},{2,1},{3,0},{4,7},{5,6},{6,5},{7,4},{8,11},{9,10},{10,... | collective-permute-start | bytes 36872 | tf_op jit(solution)/shard_map/ppermute | solution.py:33
  9.4 0.5 %fusion.2 = f32[2,256]{1,0:T(2,128)S(1)} fusion(bf16[2,256,1536]{2,1,0:T(8,128)(2,1)S(1)} %copy-done.10, f32[2,256]{1,0:T(2,128)S(1)} %broadcast_multiply_fusion), kind=kLoop, calls=%fused_computation.4 | loop fusion | flops 3145216 | bytes 1576960 | tf_op jit(solution)/shard_map/reduce_sum | solution.py:62
  10.0 0.6 %collective-permute-start.17 = (bf16[192,384]{1,0:T(8,128)(2,1)S(1)}, bf16[192,384]{1,0:T(8,128)(2,1)S(1)}, u32[]{:S(2)}, u32[]{:S(2)}) collective-permute-start(bf16[192,384]{1,0:T(8,128)(2,1)S(1)} %get-tuple-element.39), channel_id=1, source_target_pairs={{0,3},{1,2},{2,1},{3,0},{4,7},{5,6},{6,5},{7,4},{8,11},{9,10},{10,... | collective-permute-start | bytes 442376 | tf_op jit(solution)/shard_map/ppermute | solution.py:33
  10.6 0.9 %collective-permute-done.4.refs_2_ = bf16[8,768]{1,0:T(8,128)(2,1)S(1)} collective-permute-done((bf16[8,768]{1,0:T(8,128)(2,1)S(1)}, bf16[8,768]{1,0:T(8,128)(2,1)S(1)}, u32[]{:S(2)}, u32[]{:S(2)}) %collective-permute-start.4) | collective-permute-done | bytes 12320 | tf_op jit(solution)/shard_map/ppermute | solution.py:33
  11.5 0.4 shard_map.137
  11.9 0.2 collective-permute-start.6
  12.1 1.4 %collective-permute-start.7 = (bf16[24,384]{1,0:T(8,128)(2,1)S(1)}, bf16[24,384]{1,0:T(8,128)(2,1)S(1)}, u32[]{:S(2)}, u32[]{:S(2)}) collective-permute-start(bf16[24,384]{1,0:T(8,128)(2,1)S(1)} %get-tuple-element.30), channel_id=1, source_target_pairs={{0,2},{1,3},{2,0},{3,1},{4,6},{5,7},{6,4},{7,5},{8,10},{9,11},{10,... | collective-permute-start | bytes 55304 | tf_op jit(solution)/shard_map/ppermute | solution.py:33
  13.5 0.8 %collective-permute-start.8 = (bf16[24,384]{1,0:T(8,128)(2,1)S(1)}, bf16[24,384]{1,0:T(8,128)(2,1)S(1)}, u32[]{:S(2)}, u32[]{:S(2)}) collective-permute-start(bf16[24,384]{1,0:T(8,128)(2,1)S(1)} %get-tuple-element.31), channel_id=1, source_target_pairs={{0,3},{1,2},{2,1},{3,0},{4,7},{5,6},{6,5},{7,4},{8,11},{9,10},{10,... | collective-permute-start | bytes 55304 | tf_op jit(solution)/shard_map/ppermute | solution.py:33
  14.3 0.5 %fusion.4.refs_4_ = bf16[2,256,1536]{2,1,0:T(8,128)(2,1)S(1)} fusion(bf16[2,256,1536]{2,1,0:T(8,128)(2,1)S(1)} %copy-done.10, f32[1536]{0:T(1024)S(1)} %copy-done.11, f32[2,256]{1,0:T(2,128)S(1)} %add_rsqrt_fusion, f32[2,256]{1,0:T(2,128)S(1)} %broadcast_multiply_fusion), kind=kLoop, calls=%fused_computation.6 | loop fusion | flops 3932160 | bytes 3155968 | tf_op jit(solution)/shard_map/convert_element_type | solution.py:63
  14.9 0.0 copy-start.3
  14.9 0.0 copy-start.9
  14.9 0.0 copy-start.4
  14.9 1.8 %collective-permute-done.7.refs_2_ = bf16[24,384]{1,0:T(8,128)(2,1)S(1)} collective-permute-done((bf16[24,384]{1,0:T(8,128)(2,1)S(1)}, bf16[24,384]{1,0:T(8,128)(2,1)S(1)}, u32[]{:S(2)}, u32[]{:S(2)}) %collective-permute-start.7) | collective-permute-done | bytes 18464 | tf_op jit(solution)/shard_map/ppermute | solution.py:33
  16.7 0.1 collective-permute-done.8.refs_3_
  16.8 1.0 %shard_map.138 = (bf16[24,384]{1,0:T(8,128)(2,1)S(1)}, bf16[24,384]{1,0:T(8,128)(2,1)S(1)}, bf16[24,384]{1,0:T(8,128)(2,1)S(1)}, bf16[24,384]{1,0:T(8,128)(2,1)S(1)}) custom-call(s32[1]{0:T(128)} %bitcast.place.refs_0_, bf16[24,384]{1,0:T(8,128)(2,1)S(1)} %get-tuple-element.28.refs_0_, bf16[24,384]{1,0:T(8,128)(2,1)S(1)} %collective-permute-done.6.refs_1_, ...), custom_call_target="tpu_custom_call" | custom-call | tf_op jit(solution)/shard_map/pallas_call | solution.py:81
  17.8 0.0 copy-start.6
  17.8 0.0 copy-start.7
  17.8 0.0 copy-start.8
  17.8 1.0 %collective-permute-start.10 = (bf16[24,384]{1,0:T(8,128)(2,1)S(1)}, bf16[24,384]{1,0:T(8,128)(2,1)S(1)}, u32[]{:S(2)}, u32[]{:S(2)}) collective-permute-start(bf16[24,384]{1,0:T(8,128)(2,1)S(1)} %get-tuple-element.34), channel_id=1, source_target_pairs={{0,2},{1,3},{2,0},{3,1},{4,6},{5,7},{6,4},{7,5},{8,10},{9,11},{10,... | collective-permute-start | bytes 55304 | tf_op jit(solution)/shard_map/ppermute | solution.py:33
  18.9 0.5 %collective-permute-start.11 = (bf16[24,384]{1,0:T(8,128)(2,1)S(1)}, bf16[24,384]{1,0:T(8,128)(2,1)S(1)}, u32[]{:S(2)}, u32[]{:S(2)}) collective-permute-start(bf16[24,384]{1,0:T(8,128)(2,1)S(1)} %get-tuple-element.35), channel_id=1, source_target_pairs={{0,3},{1,2},{2,1},{3,0},{4,7},{5,6},{6,5},{7,4},{8,11},{9,10},{10,... | collective-permute-start | bytes 55304 | tf_op jit(solution)/shard_map/ppermute | solution.py:33
  19.4 2.3 %collective-permute-done.10.refs_2_ = bf16[24,384]{1,0:T(8,128)(2,1)S(1)} collective-permute-done((bf16[24,384]{1,0:T(8,128)(2,1)S(1)}, bf16[24,384]{1,0:T(8,128)(2,1)S(1)}, u32[]{:S(2)}, u32[]{:S(2)}) %collective-permute-start.10) | collective-permute-done | bytes 18464 | tf_op jit(solution)/shard_map/ppermute | solution.py:33
  21.7 0.5 %collective-permute-done.11.refs_3_ = bf16[24,384]{1,0:T(8,128)(2,1)S(1)} collective-permute-done((bf16[24,384]{1,0:T(8,128)(2,1)S(1)}, bf16[24,384]{1,0:T(8,128)(2,1)S(1)}, u32[]{:S(2)}, u32[]{:S(2)}) %collective-permute-start.11) | collective-permute-done | bytes 18464 | tf_op jit(solution)/shard_map/ppermute | solution.py:33
  22.2 0.7 %collective-permute-done.9.refs_1_ = bf16[24,384]{1,0:T(8,128)(2,1)S(1)} collective-permute-done((bf16[24,384]{1,0:T(8,128)(2,1)S(1)}, bf16[24,384]{1,0:T(8,128)(2,1)S(1)}, u32[]{:S(2)}, u32[]{:S(2)}) %collective-permute-start.9) | collective-permute-done | bytes 18464 | tf_op jit(solution)/shard_map/ppermute | solution.py:33
  22.9 0.3 shard_map.139.refs_0_.after
  23.2 0.2 collective-permute-start.12
  23.4 1.0 %collective-permute-start.13 = (bf16[8,768]{1,0:T(8,128)(2,1)S(1)}, bf16[8,768]{1,0:T(8,128)(2,1)S(1)}, u32[]{:S(2)}, u32[]{:S(2)}) collective-permute-start(bf16[8,768]{1,0:T(8,128)(2,1)S(1)} %shard_map.139.refs_0_.after), channel_id=1, source_target_pairs={{0,2},{1,3},{2,0},{3,1},{4,6},{5,7},{6,4},{7,5},{8,10},{9,11},{10,... | collective-permute-start | bytes 36872 | tf_op jit(solution)/shard_map/ppermute | solution.py:33
  24.4 0.0 collective-permute-done.12.refs_1_
  24.4 0.7 %collective-permute-start.14 = (bf16[8,768]{1,0:T(8,128)(2,1)S(1)}, bf16[8,768]{1,0:T(8,128)(2,1)S(1)}, u32[]{:S(2)}, u32[]{:S(2)}) collective-permute-start(bf16[8,768]{1,0:T(8,128)(2,1)S(1)} %shard_map.139.refs_0_.after), channel_id=1, source_target_pairs={{0,3},{1,2},{2,1},{3,0},{4,7},{5,6},{6,5},{7,4},{8,11},{9,10},{10,... | collective-permute-start | bytes 36872 | tf_op jit(solution)/shard_map/ppermute | solution.py:33
  25.8 0.6 %shard_map.141.refs_10_ = bf16[8,128]{1,0:T(8,128)(2,1)S(1)} custom-call(s32[1]{0:T(128)} %bitcast.place.refs_0_, s32[2]{0:T(128)S(1)} %copy-done.9, s32[1]{0:T(128)S(6)} %copy.15.counts, bf16[2,1536]{1,0:T(2,128)(2,1)S(1)} %head.1.refs_0_.after), custom_call_target="tpu_custom_call" | custom-call | tf_op jit(solution)/shard_map/pallas_call | solution.py:81
  26.4 0.7 %collective-permute-done.13.refs_2_ = bf16[8,768]{1,0:T(8,128)(2,1)S(1)} collective-permute-done((bf16[8,768]{1,0:T(8,128)(2,1)S(1)}, bf16[8,768]{1,0:T(8,128)(2,1)S(1)}, u32[]{:S(2)}, u32[]{:S(2)}) %collective-permute-start.13) | collective-permute-done | bytes 12320 | tf_op jit(solution)/shard_map/ppermute | solution.py:33
  27.1 0.4 collective-permute-done.14.refs_3_
  27.5 0.4 shard_map.142.refs_1_
  28.0 0.2 collective-permute-start.18
  28.2 1.0 %collective-permute-start.19 = (bf16[8,896]{1,0:T(8,128)(2,1)S(1)}, bf16[8,896]{1,0:T(8,128)(2,1)S(1)}, u32[]{:S(2)}, u32[]{:S(2)}) collective-permute-start(bf16[8,896]{1,0:T(8,128)(2,1)S(1)} %shard_map.142.refs_1_), channel_id=1, source_target_pairs={{0,2},{1,3},{2,0},{3,1},{4,6},{5,7},{6,4},{7,5},{8,10},{9,11},{10,... | collective-permute-start | bytes 43016 | tf_op jit(solution)/shard_map/ppermute | solution.py:33
  29.1 0.7 %collective-permute-start.20 = (bf16[8,896]{1,0:T(8,128)(2,1)S(1)}, bf16[8,896]{1,0:T(8,128)(2,1)S(1)}, u32[]{:S(2)}, u32[]{:S(2)}) collective-permute-start(bf16[8,896]{1,0:T(8,128)(2,1)S(1)} %shard_map.142.refs_1_), channel_id=1, source_target_pairs={{0,3},{1,2},{2,1},{3,0},{4,7},{5,6},{6,5},{7,4},{8,11},{9,10},{10,... | collective-permute-start | bytes 43016 | tf_op jit(solution)/shard_map/ppermute | solution.py:33
  29.9 2.0 %collective-permute-done.19.refs_3_ = bf16[8,896]{1,0:T(8,128)(2,1)S(1)} collective-permute-done((bf16[8,896]{1,0:T(8,128)(2,1)S(1)}, bf16[8,896]{1,0:T(8,128)(2,1)S(1)}, u32[]{:S(2)}, u32[]{:S(2)}) %collective-permute-start.19) | collective-permute-done | bytes 14368 | tf_op jit(solution)/shard_map/ppermute | solution.py:33
  31.9 0.4 collective-permute-done.20.refs_4_
  32.3 0.1 shard_map.143.refs_0_
  32.3 2.6 %collective-permute-start.21 = (bf16[8,896]{1,0:T(8,128)(2,1)S(1)}, bf16[8,896]{1,0:T(8,128)(2,1)S(1)}, u32[]{:S(2)}, u32[]{:S(2)}) collective-permute-start(bf16[8,896]{1,0:T(8,128)(2,1)S(1)} %shard_map.143.refs_0_), channel_id=1, source_target_pairs={{0,8},{1,13},{2,10},{3,15},{4,12},{5,9},{6,14},{7,11},{8,0},{9,5},... | collective-permute-start | bytes 43016 | tf_op jit(solution)/shard_map/ppermute | solution.py:49
  35.0 1.6 %collective-permute-start.23 = (bf16[8,896]{1,0:T(8,128)(2,1)S(1)}, bf16[8,896]{1,0:T(8,128)(2,1)S(1)}, u32[]{:S(2)}, u32[]{:S(2)}) collective-permute-start(bf16[8,896]{1,0:T(8,128)(2,1)S(1)} %shard_map.143.refs_0_), channel_id=1, source_target_pairs={{0,4},{4,0},{8,12},{12,8},{1,5},{5,1},{9,13},{13,9},{2,6},{6,2},{1... | collective-permute-start | bytes 43016 | tf_op jit(solution)/shard_map/ppermute | solution.py:33
  36.6 0.4 collective-permute-done.21.refs_1_
  37.0 0.1 shard_map.144
  37.1 1.6 %collective-permute-done.23.refs_3_ = bf16[8,896]{1,0:T(8,128)(2,1)S(1)} collective-permute-done((bf16[8,896]{1,0:T(8,128)(2,1)S(1)}, bf16[8,896]{1,0:T(8,128)(2,1)S(1)}, u32[]{:S(2)}, u32[]{:S(2)}) %collective-permute-start.23) | collective-permute-done | bytes 14368 | tf_op jit(solution)/shard_map/ppermute | solution.py:33
  38.7 1.1 %shard_map.145 = (bf16[8,192]{1,0:T(8,128)(2,1)S(1)}, bf16[8,192]{1,0:T(8,128)(2,1)S(1)}, bf16[8,192]{1,0:T(8,128)(2,1)S(1)}, bf16[8,192]{1,0:T(8,128)(2,1)S(1)}) custom-call(s32[1]{0:T(128)} %bitcast.place.refs_0_, bf16[8,896]{1,0:T(8,128)(2,1)S(1)} %shard_map.143.refs_0_, bf16[8,896]{1,0:T(8,128)(2,1)S(1)} %collective-permute-done.21.refs_1_, ...), custom_call_target="tpu_custom_call" | custom-call | tf_op jit(solution)/shard_map/pallas_call | solution.py:81
  39.9 0.0 collective-permute-start.24
  39.9 1.1 %collective-permute-start.25 = (bf16[8,192]{1,0:T(8,128)(2,1)S(1)}, bf16[8,192]{1,0:T(8,128)(2,1)S(1)}, u32[]{:S(2)}, u32[]{:S(2)}) collective-permute-start(bf16[8,192]{1,0:T(8,128)(2,1)S(1)} %get-tuple-element.47), channel_id=1, source_target_pairs={{0,2},{1,3},{2,0},{3,1},{4,6},{5,7},{6,4},{7,5},{8,10},{9,11},{10,... | collective-permute-start | bytes 9224 | tf_op jit(solution)/shard_map/ppermute | solution.py:33
  41.0 0.7 %collective-permute-start.26 = (bf16[8,192]{1,0:T(8,128)(2,1)S(1)}, bf16[8,192]{1,0:T(8,128)(2,1)S(1)}, u32[]{:S(2)}, u32[]{:S(2)}) collective-permute-start(bf16[8,192]{1,0:T(8,128)(2,1)S(1)} %get-tuple-element.48), channel_id=1, source_target_pairs={{0,3},{1,2},{2,1},{3,0},{4,7},{5,6},{6,5},{7,4},{8,11},{9,10},{10,... | collective-permute-start | bytes 9224 | tf_op jit(solution)/shard_map/ppermute | solution.py:33
  41.8 0.3 shard_map.146
  42.1 1.5 %collective-permute-done.25 = bf16[8,192]{1,0:T(8,128)(2,1)S(1)} collective-permute-done((bf16[8,192]{1,0:T(8,128)(2,1)S(1)}, bf16[8,192]{1,0:T(8,128)(2,1)S(1)}, u32[]{:S(2)}, u32[]{:S(2)}) %collective-permute-start.25) | collective-permute-done | bytes 3104 | tf_op jit(solution)/shard_map/ppermute | solution.py:33
  43.6 0.5 %collective-permute-done.26 = bf16[8,192]{1,0:T(8,128)(2,1)S(1)} collective-permute-done((bf16[8,192]{1,0:T(8,128)(2,1)S(1)}, bf16[8,192]{1,0:T(8,128)(2,1)S(1)}, u32[]{:S(2)}, u32[]{:S(2)}) %collective-permute-start.26) | collective-permute-done | bytes 3104 | tf_op jit(solution)/shard_map/ppermute | solution.py:33
  44.1 0.6 %add_convert_fusion = bf16[8,192]{1,0:T(8,128)(2,1)} fusion(f32[8,192]{1,0:T(8,128)S(1)} %shard_map.146, bf16[8,192]{1,0:T(8,128)(2,1)S(1)} %collective-permute-done.26, bf16[8,192]{1,0:T(8,128)(2,1)S(1)} %collective-permute-done.25, bf16[8,192]{1,0:T(8,128)(2,1)S(1)} %collective-permute-done.24, bf16[8,192]{1,0:T(8,128)(2,1)S(1)} %get-tuple-element.45.refs_4_), kind=kLoop, calls=%fused_computation.7 | loop fusion | flops 13824 | bytes 21504 | tf_op jit(solution)/shard_map/convert_element_type | solution.py:426
  (36 shorter events, 0.1 us)
Async XLA Ops:
  0.0 4.1 %copy-start = (bf16[192,1536]{1,0:T(8,128)(2,1)S(1)}, bf16[192,1536]{1,0:T(8,128)(2,1)}, u32[]{:S(2)}) copy-start(bf16[192,1536]{1,0:T(8,128)(2,1)} %weight.2) | copy-start | bytes 1769476
  0.0 6.4 %copy-start.10 = (bf16[2,256,1536]{2,1,0:T(8,128)(2,1)S(1)}, bf16[2,256,1536]{2,1,0:T(8,128)(2,1)}, u32[]{:S(2)}) copy-start(bf16[2,256,1536]{2,1,0:T(8,128)(2,1)} %tokens.1) | copy-start | bytes 4718596
  0.0 6.7 %copy-start.11 = (f32[1536]{0:T(1024)S(1)}, f32[1536]{0:T(1024)}, u32[]{:S(2)}) copy-start(f32[1536]{0:T(1024)} %param.15) | copy-start | bytes 18436
  0.0 7.2 %copy-start.1 = (bf16[384,768]{1,0:T(8,128)(2,1)S(1)}, bf16[384,768]{1,0:T(8,128)(2,1)}, u32[]{:S(2)}) copy-start(bf16[384,768]{1,0:T(8,128)(2,1)} %refs_5_.1) | copy-start | bytes 1769476
  1.0 5.8 %collective-permute-start = (bf16[2,1536]{1,0:T(2,128)(2,1)S(1)}, bf16[2,1536]{1,0:T(2,128)(2,1)S(1)}, u32[]{:S(2)}, u32[]{:S(2)}) collective-permute-start(bf16[2,1536]{1,0:T(2,128)(2,1)S(1)} %head.1.refs_0_.after), channel_id=1, source_target_pairs={{0,1},{1,0},{2,3},{3,2},{4,5},{5,4},{6,7},{7,6},{8,9},{9,8},{10,11... | collective-permute-start | bytes 18440 | tf_op jit(solution)/shard_map/ppermute | solution.py:33
  1.5 5.2 %collective-permute-start.1 = (bf16[2,1536]{1,0:T(2,128)(2,1)S(1)}, bf16[2,1536]{1,0:T(2,128)(2,1)S(1)}, u32[]{:S(2)}, u32[]{:S(2)}) collective-permute-start(bf16[2,1536]{1,0:T(2,128)(2,1)S(1)} %head.1.refs_0_.after), channel_id=1, source_target_pairs={{0,2},{1,3},{2,0},{3,1},{4,6},{5,7},{6,4},{7,5},{8,10},{9,11},{10,... | collective-permute-start | bytes 18440 | tf_op jit(solution)/shard_map/ppermute | solution.py:33
  4.1 3.1 %collective-permute-start.2 = (bf16[2,1536]{1,0:T(2,128)(2,1)S(1)}, bf16[2,1536]{1,0:T(2,128)(2,1)S(1)}, u32[]{:S(2)}, u32[]{:S(2)}) collective-permute-start(bf16[2,1536]{1,0:T(2,128)(2,1)S(1)} %head.1.refs_0_.after), channel_id=1, source_target_pairs={{0,3},{1,2},{2,1},{3,0},{4,7},{5,6},{6,5},{7,4},{8,11},{9,10},{10,... | collective-permute-start | bytes 18440 | tf_op jit(solution)/shard_map/ppermute | solution.py:33
  4.3 23.3 %collective-permute-start.15 = (bf16[192,384]{1,0:T(8,128)(2,1)S(1)}, bf16[192,384]{1,0:T(8,128)(2,1)S(1)}, u32[]{:S(2)}, u32[]{:S(2)}) collective-permute-start(bf16[192,384]{1,0:T(8,128)(2,1)S(1)} %get-tuple-element.37), channel_id=1, source_target_pairs={{0,1},{1,0},{2,3},{3,2},{4,5},{5,4},{6,7},{7,6},{8,9},{9,8},{10,11... | collective-permute-start | bytes 442376 | tf_op jit(solution)/shard_map/ppermute | solution.py:33
  4.5 7.0 %copy-start.2 = (bf16[384,768]{1,0:T(8,128)(2,1)S(1)}, bf16[384,768]{1,0:T(8,128)(2,1)}, u32[]{:S(2)}) copy-start(bf16[384,768]{1,0:T(8,128)(2,1)} %refs_4_.2) | copy-start | bytes 1769476
  4.5 23.0 %collective-permute-start.16 = (bf16[192,384]{1,0:T(8,128)(2,1)S(1)}, bf16[192,384]{1,0:T(8,128)(2,1)S(1)}, u32[]{:S(2)}, u32[]{:S(2)}) collective-permute-start(bf16[192,384]{1,0:T(8,128)(2,1)S(1)} %get-tuple-element.38), channel_id=1, source_target_pairs={{0,2},{1,3},{2,0},{3,1},{4,6},{5,7},{6,4},{7,5},{8,10},{9,11},{10,... | collective-permute-start | bytes 442376 | tf_op jit(solution)/shard_map/ppermute | solution.py:33
  7.5 2.4 %collective-permute-start.3 = (bf16[8,768]{1,0:T(8,128)(2,1)S(1)}, bf16[8,768]{1,0:T(8,128)(2,1)S(1)}, u32[]{:S(2)}, u32[]{:S(2)}) collective-permute-start(bf16[8,768]{1,0:T(8,128)(2,1)S(1)} %get-tuple-element.27.refs_0_), channel_id=1, source_target_pairs={{0,1},{1,0},{2,3},{3,2},{4,5},{5,4},{6,7},{7,6},{8,9},{9,8},{10,11... | collective-permute-start | bytes 36872 | tf_op jit(solution)/shard_map/ppermute | solution.py:33
  7.8 3.7 %collective-permute-start.4 = (bf16[8,768]{1,0:T(8,128)(2,1)S(1)}, bf16[8,768]{1,0:T(8,128)(2,1)S(1)}, u32[]{:S(2)}, u32[]{:S(2)}) collective-permute-start(bf16[8,768]{1,0:T(8,128)(2,1)S(1)} %get-tuple-element.27.refs_0_), channel_id=1, source_target_pairs={{0,2},{1,3},{2,0},{3,1},{4,6},{5,7},{6,4},{7,5},{8,10},{9,11},{10,... | collective-permute-start | bytes 36872 | tf_op jit(solution)/shard_map/ppermute | solution.py:33
  8.2 3.3 %collective-permute-start.5 = (bf16[8,768]{1,0:T(8,128)(2,1)S(1)}, bf16[8,768]{1,0:T(8,128)(2,1)S(1)}, u32[]{:S(2)}, u32[]{:S(2)}) collective-permute-start(bf16[8,768]{1,0:T(8,128)(2,1)S(1)} %get-tuple-element.27.refs_0_), channel_id=1, source_target_pairs={{0,3},{1,2},{2,1},{3,0},{4,7},{5,6},{6,5},{7,4},{8,11},{9,10},{10,... | collective-permute-start | bytes 36872 | tf_op jit(solution)/shard_map/ppermute | solution.py:33
  10.0 17.5 %collective-permute-start.17 = (bf16[192,384]{1,0:T(8,128)(2,1)S(1)}, bf16[192,384]{1,0:T(8,128)(2,1)S(1)}, u32[]{:S(2)}, u32[]{:S(2)}) collective-permute-start(bf16[192,384]{1,0:T(8,128)(2,1)S(1)} %get-tuple-element.39), channel_id=1, source_target_pairs={{0,3},{1,2},{2,1},{3,0},{4,7},{5,6},{6,5},{7,4},{8,11},{9,10},{10,... | collective-permute-start | bytes 442376 | tf_op jit(solution)/shard_map/ppermute | solution.py:33
  11.9 1.6 %collective-permute-start.6 = (bf16[24,384]{1,0:T(8,128)(2,1)S(1)}, bf16[24,384]{1,0:T(8,128)(2,1)S(1)}, u32[]{:S(2)}, u32[]{:S(2)}) collective-permute-start(bf16[24,384]{1,0:T(8,128)(2,1)S(1)} %get-tuple-element.29), channel_id=1, source_target_pairs={{0,1},{1,0},{2,3},{3,2},{4,5},{5,4},{6,7},{7,6},{8,9},{9,8},{10,11... | collective-permute-start | bytes 55304 | tf_op jit(solution)/shard_map/ppermute | solution.py:33
  12.1 4.6 %collective-permute-start.7 = (bf16[24,384]{1,0:T(8,128)(2,1)S(1)}, bf16[24,384]{1,0:T(8,128)(2,1)S(1)}, u32[]{:S(2)}, u32[]{:S(2)}) collective-permute-start(bf16[24,384]{1,0:T(8,128)(2,1)S(1)} %get-tuple-element.30), channel_id=1, source_target_pairs={{0,2},{1,3},{2,0},{3,1},{4,6},{5,7},{6,4},{7,5},{8,10},{9,11},{10,... | collective-permute-start | bytes 55304 | tf_op jit(solution)/shard_map/ppermute | solution.py:33
  13.5 3.3 %collective-permute-start.8 = (bf16[24,384]{1,0:T(8,128)(2,1)S(1)}, bf16[24,384]{1,0:T(8,128)(2,1)S(1)}, u32[]{:S(2)}, u32[]{:S(2)}) collective-permute-start(bf16[24,384]{1,0:T(8,128)(2,1)S(1)} %get-tuple-element.31), channel_id=1, source_target_pairs={{0,3},{1,2},{2,1},{3,0},{4,7},{5,6},{6,5},{7,4},{8,11},{9,10},{10,... | collective-permute-start | bytes 55304 | tf_op jit(solution)/shard_map/ppermute | solution.py:33
  14.9 8.0 %copy-start.3 = (bf16[384,768]{1,0:T(8,128)(2,1)S(1)}, bf16[384,768]{1,0:T(8,128)(2,1)}, u32[]{:S(2)}) copy-start(bf16[384,768]{1,0:T(8,128)(2,1)} %refs_4_.3) | copy-start | bytes 1769476
  14.9 10.9 %copy-start.9 = (s32[2]{0:T(128)S(1)}, s32[2]{0:T(128)}, u32[]{:S(2)}) copy-start(s32[2]{0:T(128)} %order.1) | copy-start | bytes 28
  14.9 12.6 %copy-start.4 = (bf16[384,768]{1,0:T(8,128)(2,1)S(1)}, bf16[384,768]{1,0:T(8,128)(2,1)}, u32[]{:S(2)}) copy-start(bf16[384,768]{1,0:T(8,128)(2,1)} %refs_9_.1) | copy-start | bytes 1769476
  16.8 20.2 %copy-start.12 = (f32[768]{0:T(1024)S(1)}, f32[768]{0:T(1024)}, u32[]{:S(2)}) copy-start(f32[768]{0:T(1024)} %param.21) | copy-start | bytes 9220
  16.8 20.2 %copy-start.5 = (bf16[192,768]{1,0:T(8,128)(2,1)S(1)}, bf16[192,768]{1,0:T(8,128)(2,1)}, u32[]{:S(2)}) copy-start(bf16[192,768]{1,0:T(8,128)(2,1)} %weight.3) | copy-start | bytes 884740
  17.8 20.9 %copy-start.6 = (bf16[768,192]{0,1:T(8,128)(2,1)S(1)}, bf16[768,192]{0,1:T(8,128)(2,1)}, u32[]{:S(2)}) copy-start(bf16[768,192]{0,1:T(8,128)(2,1)} %param.22) | copy-start | bytes 884740
  17.8 20.9 %copy-start.7 = (bf16[768,192]{0,1:T(8,128)(2,1)S(1)}, bf16[768,192]{0,1:T(8,128)(2,1)}, u32[]{:S(2)}) copy-start(bf16[768,192]{0,1:T(8,128)(2,1)} %param.23) | copy-start | bytes 884740
  17.8 20.9 %copy-start.8 = (bf16[768,192]{0,1:T(8,128)(2,1)S(1)}, bf16[768,192]{0,1:T(8,128)(2,1)}, u32[]{:S(2)}) copy-start(bf16[768,192]{0,1:T(8,128)(2,1)} %param.24) | copy-start | bytes 884740
  17.8 3.8 %collective-permute-start.10 = (bf16[24,384]{1,0:T(8,128)(2,1)S(1)}, bf16[24,384]{1,0:T(8,128)(2,1)S(1)}, u32[]{:S(2)}, u32[]{:S(2)}) collective-permute-start(bf16[24,384]{1,0:T(8,128)(2,1)S(1)} %get-tuple-element.34), channel_id=1, source_target_pairs={{0,2},{1,3},{2,0},{3,1},{4,6},{5,7},{6,4},{7,5},{8,10},{9,11},{10,... | collective-permute-start | bytes 55304 | tf_op jit(solution)/shard_map/ppermute | solution.py:33
  18.9 3.3 %collective-permute-start.11 = (bf16[24,384]{1,0:T(8,128)(2,1)S(1)}, bf16[24,384]{1,0:T(8,128)(2,1)S(1)}, u32[]{:S(2)}, u32[]{:S(2)}) collective-permute-start(bf16[24,384]{1,0:T(8,128)(2,1)S(1)} %get-tuple-element.35), channel_id=1, source_target_pairs={{0,3},{1,2},{2,1},{3,0},{4,7},{5,6},{6,5},{7,4},{8,11},{9,10},{10,... | collective-permute-start | bytes 55304 | tf_op jit(solution)/shard_map/ppermute | solution.py:33
  21.7 1.2 %collective-permute-start.9 = (bf16[24,384]{1,0:T(8,128)(2,1)S(1)}, bf16[24,384]{1,0:T(8,128)(2,1)S(1)}, u32[]{:S(2)}, u32[]{:S(2)}) collective-permute-start(bf16[24,384]{1,0:T(8,128)(2,1)S(1)} %get-tuple-element.33), channel_id=1, source_target_pairs={{0,1},{1,0},{2,3},{3,2},{4,5},{5,4},{6,7},{7,6},{8,9},{9,8},{10,11... | collective-permute-start | bytes 55304 | tf_op jit(solution)/shard_map/ppermute | solution.py:33
  23.2 1.2 %collective-permute-start.12 = (bf16[8,768]{1,0:T(8,128)(2,1)S(1)}, bf16[8,768]{1,0:T(8,128)(2,1)S(1)}, u32[]{:S(2)}, u32[]{:S(2)}) collective-permute-start(bf16[8,768]{1,0:T(8,128)(2,1)S(1)} %shard_map.139.refs_0_.after), channel_id=1, source_target_pairs={{0,1},{1,0},{2,3},{3,2},{4,5},{5,4},{6,7},{7,6},{8,9},{9,8},{10,11... | collective-permute-start | bytes 36872 | tf_op jit(solution)/shard_map/ppermute | solution.py:33
  23.4 3.7 %collective-permute-start.13 = (bf16[8,768]{1,0:T(8,128)(2,1)S(1)}, bf16[8,768]{1,0:T(8,128)(2,1)S(1)}, u32[]{:S(2)}, u32[]{:S(2)}) collective-permute-start(bf16[8,768]{1,0:T(8,128)(2,1)S(1)} %shard_map.139.refs_0_.after), channel_id=1, source_target_pairs={{0,2},{1,3},{2,0},{3,1},{4,6},{5,7},{6,4},{7,5},{8,10},{9,11},{10,... | collective-permute-start | bytes 36872 | tf_op jit(solution)/shard_map/ppermute | solution.py:33
  24.4 3.1 %collective-permute-start.14 = (bf16[8,768]{1,0:T(8,128)(2,1)S(1)}, bf16[8,768]{1,0:T(8,128)(2,1)S(1)}, u32[]{:S(2)}, u32[]{:S(2)}) collective-permute-start(bf16[8,768]{1,0:T(8,128)(2,1)S(1)} %shard_map.139.refs_0_.after), channel_id=1, source_target_pairs={{0,3},{1,2},{2,1},{3,0},{4,7},{5,6},{6,5},{7,4},{8,11},{9,10},{10,... | collective-permute-start | bytes 36872 | tf_op jit(solution)/shard_map/ppermute | solution.py:33
  28.0 1.9 %collective-permute-start.18 = (bf16[8,896]{1,0:T(8,128)(2,1)S(1)}, bf16[8,896]{1,0:T(8,128)(2,1)S(1)}, u32[]{:S(2)}, u32[]{:S(2)}) collective-permute-start(bf16[8,896]{1,0:T(8,128)(2,1)S(1)} %shard_map.142.refs_1_), channel_id=1, source_target_pairs={{0,1},{1,0},{2,3},{3,2},{4,5},{5,4},{6,7},{7,6},{8,9},{9,8},{10,11... | collective-permute-start | bytes 43016 | tf_op jit(solution)/shard_map/ppermute | solution.py:33
  28.2 3.7 %collective-permute-start.19 = (bf16[8,896]{1,0:T(8,128)(2,1)S(1)}, bf16[8,896]{1,0:T(8,128)(2,1)S(1)}, u32[]{:S(2)}, u32[]{:S(2)}) collective-permute-start(bf16[8,896]{1,0:T(8,128)(2,1)S(1)} %shard_map.142.refs_1_), channel_id=1, source_target_pairs={{0,2},{1,3},{2,0},{3,1},{4,6},{5,7},{6,4},{7,5},{8,10},{9,11},{10,... | collective-permute-start | bytes 43016 | tf_op jit(solution)/shard_map/ppermute | solution.py:33
  29.1 3.1 %collective-permute-start.20 = (bf16[8,896]{1,0:T(8,128)(2,1)S(1)}, bf16[8,896]{1,0:T(8,128)(2,1)S(1)}, u32[]{:S(2)}, u32[]{:S(2)}) collective-permute-start(bf16[8,896]{1,0:T(8,128)(2,1)S(1)} %shard_map.142.refs_1_), channel_id=1, source_target_pairs={{0,3},{1,2},{2,1},{3,0},{4,7},{5,6},{6,5},{7,4},{8,11},{9,10},{10,... | collective-permute-start | bytes 43016 | tf_op jit(solution)/shard_map/ppermute | solution.py:33
  32.3 4.6 %collective-permute-start.21 = (bf16[8,896]{1,0:T(8,128)(2,1)S(1)}, bf16[8,896]{1,0:T(8,128)(2,1)S(1)}, u32[]{:S(2)}, u32[]{:S(2)}) collective-permute-start(bf16[8,896]{1,0:T(8,128)(2,1)S(1)} %shard_map.143.refs_0_), channel_id=1, source_target_pairs={{0,8},{1,13},{2,10},{3,15},{4,12},{5,9},{6,14},{7,11},{8,0},{9,5},... | collective-permute-start | bytes 43016 | tf_op jit(solution)/shard_map/ppermute | solution.py:49
  35.0 3.8 %collective-permute-start.23 = (bf16[8,896]{1,0:T(8,128)(2,1)S(1)}, bf16[8,896]{1,0:T(8,128)(2,1)S(1)}, u32[]{:S(2)}, u32[]{:S(2)}) collective-permute-start(bf16[8,896]{1,0:T(8,128)(2,1)S(1)} %shard_map.143.refs_0_), channel_id=1, source_target_pairs={{0,4},{4,0},{8,12},{12,8},{1,5},{5,1},{9,13},{13,9},{2,6},{6,2},{1... | collective-permute-start | bytes 43016 | tf_op jit(solution)/shard_map/ppermute | solution.py:33
  37.0 1.8 %collective-permute-start.22 = (bf16[8,896]{1,0:T(8,128)(2,1)S(1)}, bf16[8,896]{1,0:T(8,128)(2,1)S(1)}, u32[]{:S(2)}, u32[]{:S(2)}) collective-permute-start(bf16[8,896]{1,0:T(8,128)(2,1)S(1)} %collective-permute-done.21.refs_1_), channel_id=1, source_target_pairs={{0,1},{1,0},{2,3},{3,2},{4,5},{5,4},{6,7},{7,6},{8,9},{9,8},{10,11... | collective-permute-start | bytes 43016 | tf_op jit(solution)/shard_map/ppermute | solution.py:33
  39.9 2.2 %collective-permute-start.24 = (bf16[8,192]{1,0:T(8,128)(2,1)S(1)}, bf16[8,192]{1,0:T(8,128)(2,1)S(1)}, u32[]{:S(2)}, u32[]{:S(2)}) collective-permute-start(bf16[8,192]{1,0:T(8,128)(2,1)S(1)} %get-tuple-element.46), channel_id=1, source_target_pairs={{0,1},{1,0},{2,3},{3,2},{4,5},{5,4},{6,7},{7,6},{8,9},{9,8},{10,11... | collective-permute-start | bytes 9224 | tf_op jit(solution)/shard_map/ppermute | solution.py:33
  39.9 3.7 %collective-permute-start.25 = (bf16[8,192]{1,0:T(8,128)(2,1)S(1)}, bf16[8,192]{1,0:T(8,128)(2,1)S(1)}, u32[]{:S(2)}, u32[]{:S(2)}) collective-permute-start(bf16[8,192]{1,0:T(8,128)(2,1)S(1)} %get-tuple-element.47), channel_id=1, source_target_pairs={{0,2},{1,3},{2,0},{3,1},{4,6},{5,7},{6,4},{7,5},{8,10},{9,11},{10,... | collective-permute-start | bytes 9224 | tf_op jit(solution)/shard_map/ppermute | solution.py:33
  41.0 3.0 %collective-permute-start.26 = (bf16[8,192]{1,0:T(8,128)(2,1)S(1)}, bf16[8,192]{1,0:T(8,128)(2,1)S(1)}, u32[]{:S(2)}, u32[]{:S(2)}) collective-permute-start(bf16[8,192]{1,0:T(8,128)(2,1)S(1)} %get-tuple-element.48), channel_id=1, source_target_pairs={{0,3},{1,2},{2,1},{3,0},{4,7},{5,6},{6,5},{7,4},{8,11},{9,10},{10,... | collective-permute-start | bytes 9224 | tf_op jit(solution)/shard_map/ppermute | solution.py:33

commit v3 on v2

--- a/solution.py
+++ b/solution.py
@@ -110,11 +110,20 @@
     out[...] = rows[...].reshape(size * tiles, LANES).astype(BF16)
 
 
+def halve_kernel(place, weight, after, kept, sent, halves):
+    mine = place[0] % 2
+    half = kept.shape[1]
+    for block in range(2):
+        halves[block] = weight[:, block * half : (block + 1) * half]
+    kept[...] = halves[mine]
+    sent[...] = halves[1 - mine]
+
+
 def query_kernel(size, place, *refs):
-    heads_in, (gain, weight, out, first, rows, blocks) = refs[:size], refs[size:]
+    heads_in, (gain, kept, fetched, out, first, rows, blocks) = refs[:size], refs[size:]
     me = place[0] % size
     tiles, width = heads_in[0].shape
-    mine = weight.shape[0]
+    mine = kept.shape[0]
     for step in range(size):
         rows[source(me, step, size)] = heads_in[step][...].astype(F32)
     full = rows[...].reshape(size * tiles, width)
@@ -124,32 +133,46 @@
     normed = normalise(full, gain[...]).astype(F32)
     for block in range(size):
         blocks[block] = normed[:, block * mine : (block + 1) * mine]
-    out[...] = contract(blocks[me].astype(BF16), weight[...], 1, 0).astype(BF16)
+    part = contract(blocks[me].astype(BF16), kept[...], 1, 0)
+    part = part + contract(blocks[me ^ 1].astype(BF16), fetched[...], 1, 0)
+    out[...] = part.astype(BF16)
 
 
 def grouped(shape, axis, span):
     return lax.broadcasted_iota(jnp.int32, shape, axis) // span
 
 
-def own_head(shape, heads):
-    row = lax.broadcasted_iota(jnp.int32, shape, 0) % heads
-    return row == grouped(shape, 1, VHD)
-
-
-def fold_kernel(size, heads, place, *refs):
-    parts, weight, outs, folded = refs[:size], refs[size], refs[size + 1 : -1], refs[-1]
+def own_head(shape, tiles, half):
+    row = lax.broadcasted_iota(jnp.int32, shape, 0)
+    return row // (tiles * half) % 2 * half + row % half == grouped(shape, 1, VHD)
+
+
+def own_tile(row, tiles, half):
+    return row // (2 * tiles * half) * tiles + row % (tiles * half) // half
+
+
+def fold_kernel(size, half, place, *refs):
+    parts, (kept, fetched) = refs[: size // 2], refs[size // 2 : size // 2 + 2]
+    outs, folded = refs[size // 2 + 2 : -1], refs[-1]
     me = place[0] % size
     total = parts[0][...].astype(F32)
-    for step in range(1, size):
-        total = total + parts[step][...].astype(F32)
+    for part in parts[1:]:
+        total = total + part[...].astype(F32)
     count, _ = total.shape
-    spots = (count * heads, count)
-    repeat = grouped(spots, 0, heads) == lax.broadcasted_iota(jnp.int32, spots, 1)
+    spots = (count * half, count)
+    repeat = grouped(spots, 0, half) == lax.broadcasted_iota(jnp.int32, spots, 1)
     repeated = contract(repeat.astype(F32).astype(BF16), total.astype(BF16), 1, 0)
-    blocked = jnp.where(own_head(repeated.shape, heads), repeated, 0.0).astype(BF16)
-    folded[...] = contract(blocked, weight[...], 1, 1).astype(BF16).reshape(folded.shape)
-    for step in range(size):
-        outs[step][...] = folded[other(me, step, size)]
+    shape = repeated.shape
+    own = lax.broadcasted_iota(jnp.int32, shape, 0) % half == grouped(shape, 1, VHD)
+    blocked = jnp.where(own, repeated, 0.0).astype(BF16)
+    for at, weight in ((me % 2, kept), (1 - me % 2, fetched)):
+        product = contract(blocked, weight[...], 1, 1)
+        product = product.reshape(size, product.shape[0] // size, product.shape[1])
+        for owner in range(size):
+            folded[owner, at] = product[owner]
+    for step in range(size):
+        piece = folded[other(me, step, size)]
+        outs[step][...] = piece.reshape(outs[step].shape).astype(BF16)
 
 
 def cut_kernel(size, place, weight, after, *refs):
@@ -162,23 +185,29 @@
         outs[step][...] = blocks[other(me, step, size)]
 
 
-def token_kernel(size, heads, place, *refs):
-    parts, normed, outs, (blocks, folded) = (
+def token_kernel(size, half, place, *refs):
+    parts, normed, outs, (pieces, blocks, folded) = (
         refs[:size],
         refs[size],
-        refs[size + 1 : -2],
-        refs[-2:],
+        refs[size + 1 : -3],
+        refs[-3:],
     )
     me = place[0] % size
     rows = parts[0].shape[1]
-    for step in range(size):
-        blocks[source(me, step, size)] = parts[step][...]
-    for block in range(size):
-        folded[:, block * rows : (block + 1) * rows] = blocks[block]
     tiles, patches, width = normed.shape
+    for step in range(size):
+        sender = source(me, step, size)
+        at = sender % 2
+        part = parts[step][...].astype(F32).reshape(2, tiles * half, rows)
+        for block in range(2):
+            pieces[sender - at + block, at] = part[block]
+    for block in range(size):
+        piece = pieces[block].reshape(folded.shape[0], rows).astype(BF16)
+        folded[:, block * rows : (block + 1) * rows] = piece
     tokens = normed[...].reshape(tiles * patches, width)
     scores = contract(folded[...], tokens, 1, 1) / math.sqrt(VHD)
-    same = grouped(scores.shape, 0, heads) == grouped(scores.shape, 1, patches)
+    row = lax.broadcasted_iota(jnp.int32, scores.shape, 0)
+    same = own_tile(row, tiles, half) == grouped(scores.shape, 1, patches)
     lifted = jnp.where(same, jnp.exp(scores), 0.0)
     probs = (lifted / jnp.sum(lifted, axis=-1, keepdims=True)).astype(BF16)
     mixed = contract(probs, tokens, 1, 0).astype(BF16)
@@ -188,16 +217,17 @@
         outs[step][...] = blocks[other(me, step, size)]
 
 
-def value_kernel(size, heads, place, *refs):
+def value_kernel(size, tiles, half, place, *refs):
     parts, (weight, out, mixed) = refs[:size], refs[size:]
     me = place[0] % size
     for step in range(size):
         mixed[source(me, step, size)] = parts[step][...]
     rows = mixed[...].reshape(size * parts[0].shape[0], parts[0].shape[1])
     product = contract(rows, weight[...], 1, 0)
-    kept = jnp.where(own_head(product.shape, heads), product, 0.0).astype(BF16)
+    kept = jnp.where(own_head(product.shape, tiles, half), product, 0.0).astype(BF16)
     spots = (out.shape[0], product.shape[0])
-    collect = lax.broadcasted_iota(jnp.int32, spots, 0) == grouped(spots, 1, heads)
+    row = lax.broadcasted_iota(jnp.int32, spots, 1)
+    collect = lax.broadcasted_iota(jnp.int32, spots, 0) == own_tile(row, tiles, half)
     out[...] = contract(collect.astype(F32).astype(BF16), kept, 1, 0).astype(BF16)
 
 
@@ -357,33 +387,50 @@
     normed = normalise(tile_patches.astype(F32), vit_gain)
 
     gain_row = vit_gain[None, :]
+
+    def halve(weight, after):
+        shape = jax.ShapeDtypeStruct((rows, vit_width // 2), BF16)
+        kept, sent = call(
+            halve_kernel,
+            [shape, shape],
+            [pltpu.VMEM((2, rows, vit_width // 2), BF16)],
+            specs=[pl.ANY],
+        )(place, weight, after)
+        return kept, swap(sent, "fsdp", 1)
+
     query_part, first = call(
         functools.partial(query_kernel, size),
         [
-            jax.ShapeDtypeStruct((count, vit_width), BF16),
+            jax.ShapeDtypeStruct((count, vit_width // 2), BF16),
             jax.ShapeDtypeStruct((count, rows), F32),
         ],
         [pltpu.VMEM((size, tiles, width), F32), pltpu.VMEM((size, count, rows), F32)],
-    )(place, *head_rows, gain_row, w_query)
-    query_parts = spread(query_part, "fsdp")
-
+    )(place, *head_rows, gain_row, *halve(w_query, head_row))
+    query_parts = [query_part]
+    query_parts += [swap(query_part, "fsdp", step) for step in range(2, size, 2)]
+
+    half = heads // 2
     block = jax.ShapeDtypeStruct((tiles * heads, rows), BF16)
     folded = call(
-        functools.partial(fold_kernel, size, heads),
+        functools.partial(fold_kernel, size, half),
         [block] * size,
-        [pltpu.VMEM((size, tiles * heads, rows), BF16)],
-    )(place, *query_parts, w_key)
+        [pltpu.VMEM((size, 2, tiles * half, rows), F32)],
+    )(place, *query_parts, *halve(w_key, query_part))
     folded = deal(folded, "fsdp")
 
     mixed = call(
-        functools.partial(token_kernel, size, heads),
+        functools.partial(token_kernel, size, half),
         [block] * size,
-        [pltpu.VMEM((size, tiles * heads, rows), BF16), pltpu.VMEM((tiles * heads, width), BF16)],
+        [
+            pltpu.VMEM((size, 2, tiles * half, rows), F32),
+            pltpu.VMEM((size, tiles * heads, rows), BF16),
+            pltpu.VMEM((tiles * heads, width), BF16),
+        ],
     )(place, *folded, normed)
     mixed = deal(mixed, "fsdp")
 
     pooled_part = call(
-        functools.partial(value_kernel, size, heads),
+        functools.partial(value_kernel, size, tiles, half),
         jax.ShapeDtypeStruct((count, vit_width), BF16),
         [pltpu.VMEM((size, tiles * heads, rows), BF16)],
     )(place, *mixed, w_value)

time: 44.8 us -> 48.3 us (1.078)
  waiting for transfers between devices: 14.2 us -> 17.3 us
    ppermute x26, waiting for transfers between devices: 13.8 us -> 16.8 us  [swap(): lax.ppermute(array, axis, [(i, other(i, step, size)) for i in range(size)])]
    pallas_call x11 -> x13, Pallas kernels: 4.92 us -> 5.18 us  [run(): pl.pallas_call(body, out_shape=outs, in_specs=[smem] + [vmem] * last + [p...]
where the time goes in v3:
time: 48.3 us; the launch traced here: 48.1 us
  starting transfers between devices  21.6 us (45%)
  waiting for transfers between devices  17.3 us (36%)
  Pallas kernels  6.14 us (13%)
  other arithmetic  1.97 us (4%)
  between operations  0.9 us (2%)
    ppermute x26, starting transfers between devices, swap(): lax.ppermute(array, axis, [(i, other(i, step, size)) for i in range(size)])  19.1 us
    ppermute x26, waiting for transfers between devices, swap(): lax.ppermute(array, axis, [(i, other(i, step, size)) for i in range(size)])  16.8 us
    pallas_call x13, Pallas kernels, run(): pl.pallas_call(body, out_shape=outs, in_specs=[smem] + [vmem] * last + [p...  5.18 us
    ppermute x1, starting transfers between devices, rows_of_all(): far = lax.ppermute(array, ('seq', 'fsdp'), pairs)  2.59 us
    pallas_call x1, Pallas kernels, local(): pl.pallas_call(head_kernel, out_shape=jax.ShapeDtypeStruct((tiles, width)...  0.97 us
  transfers between devices with their start and end apart: 27, of which 15 were waited for; matrix products, arithmetic and copies ran while one was open for 3% of the time, Pallas kernels for 7%

profile of v3, /device:TPU:0, one launch (start us, length us, event | category | flops | bytes accessed | tf_op | source)
XLA Modules:
  0.0 48.1 jit_solution(14376046381892862078)
XLA Ops:
  0.0 1.0 %head.1.after.refs_0_ = bf16[2,1536]{1,0:T(2,128)(2,1)S(1)} custom-call(bf16[2,256,1536]{2,1,0:T(8,128)(2,1)} %tokens.1), custom_call_target="tpu_custom_call" | custom-call | tf_op jit(solution)/shard_map/head/pallas_call | solution.py:359
  1.0 0.0 copy-start.11
  1.0 0.1 copy-done
  1.1 0.1 shard_map.136
  1.2 0.6 %collective-permute-start.3 = (bf16[384,384]{1,0:T(8,128)(2,1)S(1)}, bf16[384,384]{1,0:T(8,128)(2,1)S(1)}, u32[]{:S(2)}, u32[]{:S(2)}) collective-permute-start(bf16[384,384]{1,0:T(8,128)(2,1)S(1)} %get-tuple-element.32), channel_id=1, source_target_pairs={{0,1},{1,0},{2,3},{3,2},{4,5},{5,4},{6,7},{7,6},{8,9},{9,8},{10,11... | collective-permute-start | bytes 884744 | tf_op jit(solution)/shard_map/ppermute | solution.py:33
  1.8 0.1 collective-permute-start
  1.8 2.9 %collective-permute-start.1 = (bf16[2,1536]{1,0:T(2,128)(2,1)S(1)}, bf16[2,1536]{1,0:T(2,128)(2,1)S(1)}, u32[]{:S(2)}, u32[]{:S(2)}) collective-permute-start(bf16[2,1536]{1,0:T(2,128)(2,1)S(1)} %head.1.after.refs_0_), channel_id=1, source_target_pairs={{0,2},{1,3},{2,0},{3,1},{4,6},{5,7},{6,4},{7,5},{8,10},{9,11},{10,... | collective-permute-start | bytes 18440 | tf_op jit(solution)/shard_map/ppermute | solution.py:33
  4.7 0.1 shard_map.142
  4.9 0.2 collective-permute-start.15
  5.0 0.3 convert_reduce_fusion
  5.4 2.1 %collective-permute-start.16 = (bf16[192,384]{1,0:T(8,128)(2,1)S(1)}, bf16[192,384]{1,0:T(8,128)(2,1)S(1)}, u32[]{:S(2)}, u32[]{:S(2)}) collective-permute-start(bf16[192,384]{1,0:T(8,128)(2,1)S(1)} %get-tuple-element.46), channel_id=1, source_target_pairs={{0,2},{1,3},{2,0},{3,1},{4,6},{5,7},{6,4},{7,5},{8,10},{9,11},{10,... | collective-permute-start | bytes 442376 | tf_op jit(solution)/shard_map/ppermute | solution.py:33
  7.5 0.4 collective-permute-done.2.refs_3_
  7.8 0.4 shard_map.137
  8.2 0.1 shard_map.138
  8.4 0.7 %collective-permute-start.5 = (bf16[384,384]{1,0:T(8,128)(2,1)S(1)}, bf16[384,384]{1,0:T(8,128)(2,1)S(1)}, u32[]{:S(2)}, u32[]{:S(2)}) collective-permute-start(bf16[384,384]{1,0:T(8,128)(2,1)S(1)} %get-tuple-element.35), channel_id=1, source_target_pairs={{0,1},{1,0},{2,3},{3,2},{4,5},{5,4},{6,7},{7,6},{8,9},{9,8},{10,11... | collective-permute-start | bytes 884744 | tf_op jit(solution)/shard_map/ppermute | solution.py:33
  9.1 1.1 %collective-permute-start.4 = (bf16[8,384]{1,0:T(8,128)(2,1)S(1)}, bf16[8,384]{1,0:T(8,128)(2,1)S(1)}, u32[]{:S(2)}, u32[]{:S(2)}) collective-permute-start(bf16[8,384]{1,0:T(8,128)(2,1)S(1)} %get-tuple-element.33.after.refs_0_), channel_id=1, source_target_pairs={{0,2},{1,3},{2,0},{3,1},{4,6},{5,7},{6,4},{7,5},{8,10},{9,11},{10,... | collective-permute-start | bytes 18440 | tf_op jit(solution)/shard_map/ppermute | solution.py:33
  10.2 0.5 %fusion.2 = f32[2,256]{1,0:T(2,128)S(1)} fusion(bf16[2,256,1536]{2,1,0:T(8,128)(2,1)S(1)} %copy-done.10, f32[2,256]{1,0:T(2,128)S(1)} %broadcast_multiply_fusion), kind=kLoop, calls=%fused_computation.4 | loop fusion | flops 3145216 | bytes 1576960 | tf_op jit(solution)/shard_map/reduce_sum | solution.py:62
  10.7 4.1 %collective-permute-done.4.refs_1_ = bf16[8,384]{1,0:T(8,128)(2,1)S(1)} collective-permute-done((bf16[8,384]{1,0:T(8,128)(2,1)S(1)}, bf16[8,384]{1,0:T(8,128)(2,1)S(1)}, u32[]{:S(2)}, u32[]{:S(2)}) %collective-permute-start.4) | collective-permute-done | bytes 6176 | tf_op jit(solution)/shard_map/ppermute | solution.py:33
  14.9 0.4 shard_map.139
  15.3 0.1 collective-permute-start.6
  15.4 1.7 %collective-permute-start.7 = (bf16[24,384]{1,0:T(8,128)(2,1)S(1)}, bf16[24,384]{1,0:T(8,128)(2,1)S(1)}, u32[]{:S(2)}, u32[]{:S(2)}) collective-permute-start(bf16[24,384]{1,0:T(8,128)(2,1)S(1)} %get-tuple-element.38), channel_id=1, source_target_pairs={{0,2},{1,3},{2,0},{3,1},{4,6},{5,7},{6,4},{7,5},{8,10},{9,11},{10,... | collective-permute-start | bytes 55304 | tf_op jit(solution)/shard_map/ppermute | solution.py:33
  17.1 0.9 %collective-permute-start.8 = (bf16[24,384]{1,0:T(8,128)(2,1)S(1)}, bf16[24,384]{1,0:T(8,128)(2,1)S(1)}, u32[]{:S(2)}, u32[]{:S(2)}) collective-permute-start(bf16[24,384]{1,0:T(8,128)(2,1)S(1)} %get-tuple-element.39), channel_id=1, source_target_pairs={{0,3},{1,2},{2,1},{3,0},{4,7},{5,6},{6,5},{7,4},{8,11},{9,10},{10,... | collective-permute-start | bytes 55304 | tf_op jit(solution)/shard_map/ppermute | solution.py:33
  18.0 0.5 %fusion.4.refs_4_ = bf16[2,256,1536]{2,1,0:T(8,128)(2,1)S(1)} fusion(bf16[2,256,1536]{2,1,0:T(8,128)(2,1)S(1)} %copy-done.10, f32[1536]{0:T(1024)S(1)} %copy-done.11, f32[2,256]{1,0:T(2,128)S(1)} %add_rsqrt_fusion, f32[2,256]{1,0:T(2,128)S(1)} %broadcast_multiply_fusion), kind=kLoop, calls=%fused_computation.6 | loop fusion | flops 3932160 | bytes 3155968 | tf_op jit(solution)/shard_map/convert_element_type | solution.py:63
  18.5 0.0 copy-start.3
  18.5 0.0 copy-start.9
  18.5 0.0 copy-start.4
  18.5 0.7 %collective-permute-done.7.refs_2_ = bf16[24,384]{1,0:T(8,128)(2,1)S(1)} collective-permute-done((bf16[24,384]{1,0:T(8,128)(2,1)S(1)}, bf16[24,384]{1,0:T(8,128)(2,1)S(1)}, u32[]{:S(2)}, u32[]{:S(2)}) %collective-permute-start.7) | collective-permute-done | bytes 18464 | tf_op jit(solution)/shard_map/ppermute | solution.py:33
  19.2 1.1 %collective-permute-done.8.refs_3_ = bf16[24,384]{1,0:T(8,128)(2,1)S(1)} collective-permute-done((bf16[24,384]{1,0:T(8,128)(2,1)S(1)}, bf16[24,384]{1,0:T(8,128)(2,1)S(1)}, u32[]{:S(2)}, u32[]{:S(2)}) %collective-permute-start.8) | collective-permute-done | bytes 18464 | tf_op jit(solution)/shard_map/ppermute | solution.py:33
  20.3 1.0 %shard_map.140 = (bf16[24,384]{1,0:T(8,128)(2,1)S(1)}, bf16[24,384]{1,0:T(8,128)(2,1)S(1)}, bf16[24,384]{1,0:T(8,128)(2,1)S(1)}, bf16[24,384]{1,0:T(8,128)(2,1)S(1)}) custom-call(s32[1]{0:T(128)} %bitcast.place.refs_0_, bf16[24,384]{1,0:T(8,128)(2,1)S(1)} %get-tuple-element.36.refs_0_, bf16[24,384]{1,0:T(8,128)(2,1)S(1)} %collective-permute-done.6.refs_1_, ...), custom_call_target="tpu_custom_call" | custom-call | tf_op jit(solution)/shard_map/pallas_call | solution.py:81
  21.3 0.0 copy-start.6
  21.3 0.0 copy-start.7
  21.3 0.0 copy-start.8
  21.4 1.2 %collective-permute-start.10 = (bf16[24,384]{1,0:T(8,128)(2,1)S(1)}, bf16[24,384]{1,0:T(8,128)(2,1)S(1)}, u32[]{:S(2)}, u32[]{:S(2)}) collective-permute-start(bf16[24,384]{1,0:T(8,128)(2,1)S(1)} %get-tuple-element.42), channel_id=1, source_target_pairs={{0,2},{1,3},{2,0},{3,1},{4,6},{5,7},{6,4},{7,5},{8,10},{9,11},{10,... | collective-permute-start | bytes 55304 | tf_op jit(solution)/shard_map/ppermute | solution.py:33
  22.5 0.4 collective-permute-start.11
  22.9 2.3 %collective-permute-done.10.refs_2_ = bf16[24,384]{1,0:T(8,128)(2,1)S(1)} collective-permute-done((bf16[24,384]{1,0:T(8,128)(2,1)S(1)}, bf16[24,384]{1,0:T(8,128)(2,1)S(1)}, u32[]{:S(2)}, u32[]{:S(2)}) %collective-permute-start.10) | collective-permute-done | bytes 18464 | tf_op jit(solution)/shard_map/ppermute | solution.py:33
  25.2 0.6 %collective-permute-done.11.refs_3_ = bf16[24,384]{1,0:T(8,128)(2,1)S(1)} collective-permute-done((bf16[24,384]{1,0:T(8,128)(2,1)S(1)}, bf16[24,384]{1,0:T(8,128)(2,1)S(1)}, u32[]{:S(2)}, u32[]{:S(2)}) %collective-permute-start.11) | collective-permute-done | bytes 18464 | tf_op jit(solution)/shard_map/ppermute | solution.py:33
  25.8 0.5 %collective-permute-done.9.refs_1_ = bf16[24,384]{1,0:T(8,128)(2,1)S(1)} collective-permute-done((bf16[24,384]{1,0:T(8,128)(2,1)S(1)}, bf16[24,384]{1,0:T(8,128)(2,1)S(1)}, u32[]{:S(2)}, u32[]{:S(2)}) %collective-permute-start.9) | collective-permute-done | bytes 18464 | tf_op jit(solution)/shard_map/ppermute | solution.py:33
  26.4 0.3 shard_map.141.refs_0_.after
  26.7 0.2 collective-permute-start.12
  26.9 1.1 %collective-permute-start.13 = (bf16[8,768]{1,0:T(8,128)(2,1)S(1)}, bf16[8,768]{1,0:T(8,128)(2,1)S(1)}, u32[]{:S(2)}, u32[]{:S(2)}) collective-permute-start(bf16[8,768]{1,0:T(8,128)(2,1)S(1)} %shard_map.141.refs_0_.after), channel_id=1, source_target_pairs={{0,2},{1,3},{2,0},{3,1},{4,6},{5,7},{6,4},{7,5},{8,10},{9,11},{10,... | collective-permute-start | bytes 36872 | tf_op jit(solution)/shard_map/ppermute | solution.py:33
  28.0 0.6 %collective-permute-start.14 = (bf16[8,768]{1,0:T(8,128)(2,1)S(1)}, bf16[8,768]{1,0:T(8,128)(2,1)S(1)}, u32[]{:S(2)}, u32[]{:S(2)}) collective-permute-start(bf16[8,768]{1,0:T(8,128)(2,1)S(1)} %shard_map.141.refs_0_.after), channel_id=1, source_target_pairs={{0,3},{1,2},{2,1},{3,0},{4,7},{5,6},{6,5},{7,4},{8,11},{9,10},{10,... | collective-permute-start | bytes 36872 | tf_op jit(solution)/shard_map/ppermute | solution.py:33
  29.3 0.6 %shard_map.143.refs_10_ = bf16[8,128]{1,0:T(8,128)(2,1)S(1)} custom-call(s32[1]{0:T(128)} %bitcast.place.refs_0_, s32[2]{0:T(128)S(1)} %copy-done.9, s32[1]{0:T(128)S(6)} %copy.15.counts, bf16[2,1536]{1,0:T(2,128)(2,1)S(1)} %head.1.after.refs_0_), custom_call_target="tpu_custom_call" | custom-call | tf_op jit(solution)/shard_map/pallas_call | solution.py:81
  29.9 0.7 %collective-permute-done.13.refs_2_ = bf16[8,768]{1,0:T(8,128)(2,1)S(1)} collective-permute-done((bf16[8,768]{1,0:T(8,128)(2,1)S(1)}, bf16[8,768]{1,0:T(8,128)(2,1)S(1)}, u32[]{:S(2)}, u32[]{:S(2)}) %collective-permute-start.13) | collective-permute-done | bytes 12320 | tf_op jit(solution)/shard_map/ppermute | solution.py:33
  30.6 0.5 %collective-permute-done.14.refs_3_ = bf16[8,768]{1,0:T(8,128)(2,1)S(1)} collective-permute-done((bf16[8,768]{1,0:T(8,128)(2,1)S(1)}, bf16[8,768]{1,0:T(8,128)(2,1)S(1)}, u32[]{:S(2)}, u32[]{:S(2)}) %collective-permute-start.14) | collective-permute-done | bytes 12320 | tf_op jit(solution)/shard_map/ppermute | solution.py:33
  31.1 0.4 shard_map.144.refs_1_
  31.5 0.1 collective-permute-start.18
  31.7 0.9 %collective-permute-start.19 = (bf16[8,896]{1,0:T(8,128)(2,1)S(1)}, bf16[8,896]{1,0:T(8,128)(2,1)S(1)}, u32[]{:S(2)}, u32[]{:S(2)}) collective-permute-start(bf16[8,896]{1,0:T(8,128)(2,1)S(1)} %shard_map.144.refs_1_), channel_id=1, source_target_pairs={{0,2},{1,3},{2,0},{3,1},{4,6},{5,7},{6,4},{7,5},{8,10},{9,11},{10,... | collective-permute-start | bytes 43016 | tf_op jit(solution)/shard_map/ppermute | solution.py:33
  32.6 0.8 %collective-permute-start.20 = (bf16[8,896]{1,0:T(8,128)(2,1)S(1)}, bf16[8,896]{1,0:T(8,128)(2,1)S(1)}, u32[]{:S(2)}, u32[]{:S(2)}) collective-permute-start(bf16[8,896]{1,0:T(8,128)(2,1)S(1)} %shard_map.144.refs_1_), channel_id=1, source_target_pairs={{0,3},{1,2},{2,1},{3,0},{4,7},{5,6},{6,5},{7,4},{8,11},{9,10},{10,... | collective-permute-start | bytes 43016 | tf_op jit(solution)/shard_map/ppermute | solution.py:33
  33.4 2.0 %collective-permute-done.19.refs_3_ = bf16[8,896]{1,0:T(8,128)(2,1)S(1)} collective-permute-done((bf16[8,896]{1,0:T(8,128)(2,1)S(1)}, bf16[8,896]{1,0:T(8,128)(2,1)S(1)}, u32[]{:S(2)}, u32[]{:S(2)}) %collective-permute-start.19) | collective-permute-done | bytes 14368 | tf_op jit(solution)/shard_map/ppermute | solution.py:33
  35.4 0.4 collective-permute-done.20.refs_4_
  35.7 0.1 shard_map.145.refs_0_
  35.8 2.6 %collective-permute-start.21 = (bf16[8,896]{1,0:T(8,128)(2,1)S(1)}, bf16[8,896]{1,0:T(8,128)(2,1)S(1)}, u32[]{:S(2)}, u32[]{:S(2)}) collective-permute-start(bf16[8,896]{1,0:T(8,128)(2,1)S(1)} %shard_map.145.refs_0_), channel_id=1, source_target_pairs={{0,8},{1,13},{2,10},{3,15},{4,12},{5,9},{6,14},{7,11},{8,0},{9,5},... | collective-permute-start | bytes 43016 | tf_op jit(solution)/shard_map/ppermute | solution.py:49
  38.4 1.6 %collective-permute-start.23 = (bf16[8,896]{1,0:T(8,128)(2,1)S(1)}, bf16[8,896]{1,0:T(8,128)(2,1)S(1)}, u32[]{:S(2)}, u32[]{:S(2)}) collective-permute-start(bf16[8,896]{1,0:T(8,128)(2,1)S(1)} %shard_map.145.refs_0_), channel_id=1, source_target_pairs={{0,4},{4,0},{8,12},{12,8},{1,5},{5,1},{9,13},{13,9},{2,6},{6,2},{1... | collective-permute-start | bytes 43016 | tf_op jit(solution)/shard_map/ppermute | solution.py:33
  40.0 0.5 collective-permute-done.21.refs_1_
  40.5 0.1 shard_map.146
  40.6 1.5 %collective-permute-done.23.refs_3_ = bf16[8,896]{1,0:T(8,128)(2,1)S(1)} collective-permute-done((bf16[8,896]{1,0:T(8,128)(2,1)S(1)}, bf16[8,896]{1,0:T(8,128)(2,1)S(1)}, u32[]{:S(2)}, u32[]{:S(2)}) %collective-permute-start.23) | collective-permute-done | bytes 14368 | tf_op jit(solution)/shard_map/ppermute | solution.py:33
  42.2 1.1 %shard_map.147 = (bf16[8,192]{1,0:T(8,128)(2,1)S(1)}, bf16[8,192]{1,0:T(8,128)(2,1)S(1)}, bf16[8,192]{1,0:T(8,128)(2,1)S(1)}, bf16[8,192]{1,0:T(8,128)(2,1)S(1)}) custom-call(s32[1]{0:T(128)} %bitcast.place.refs_0_, bf16[8,896]{1,0:T(8,128)(2,1)S(1)} %shard_map.145.refs_0_, bf16[8,896]{1,0:T(8,128)(2,1)S(1)} %collective-permute-done.21.refs_1_, ...), custom_call_target="tpu_custom_call" | custom-call | tf_op jit(solution)/shard_map/pallas_call | solution.py:81
  43.3 0.0 collective-permute-start.24
  43.3 1.2 %collective-permute-start.25 = (bf16[8,192]{1,0:T(8,128)(2,1)S(1)}, bf16[8,192]{1,0:T(8,128)(2,1)S(1)}, u32[]{:S(2)}, u32[]{:S(2)}) collective-permute-start(bf16[8,192]{1,0:T(8,128)(2,1)S(1)} %get-tuple-element.55), channel_id=1, source_target_pairs={{0,2},{1,3},{2,0},{3,1},{4,6},{5,7},{6,4},{7,5},{8,10},{9,11},{10,... | collective-permute-start | bytes 9224 | tf_op jit(solution)/shard_map/ppermute | solution.py:33
  44.5 0.7 %collective-permute-start.26 = (bf16[8,192]{1,0:T(8,128)(2,1)S(1)}, bf16[8,192]{1,0:T(8,128)(2,1)S(1)}, u32[]{:S(2)}, u32[]{:S(2)}) collective-permute-start(bf16[8,192]{1,0:T(8,128)(2,1)S(1)} %get-tuple-element.56), channel_id=1, source_target_pairs={{0,3},{1,2},{2,1},{3,0},{4,7},{5,6},{6,5},{7,4},{8,11},{9,10},{10,... | collective-permute-start | bytes 9224 | tf_op jit(solution)/shard_map/ppermute | solution.py:33
  45.2 0.3 shard_map.148
  45.5 1.5 %collective-permute-done.25 = bf16[8,192]{1,0:T(8,128)(2,1)S(1)} collective-permute-done((bf16[8,192]{1,0:T(8,128)(2,1)S(1)}, bf16[8,192]{1,0:T(8,128)(2,1)S(1)}, u32[]{:S(2)}, u32[]{:S(2)}) %collective-permute-start.25) | collective-permute-done | bytes 3104 | tf_op jit(solution)/shard_map/ppermute | solution.py:33
  47.0 0.5 %collective-permute-done.26 = bf16[8,192]{1,0:T(8,128)(2,1)S(1)} collective-permute-done((bf16[8,192]{1,0:T(8,128)(2,1)S(1)}, bf16[8,192]{1,0:T(8,128)(2,1)S(1)}, u32[]{:S(2)}, u32[]{:S(2)}) %collective-permute-start.26) | collective-permute-done | bytes 3104 | tf_op jit(solution)/shard_map/ppermute | solution.py:33
  47.5 0.6 %add_convert_fusion = bf16[8,192]{1,0:T(8,128)(2,1)} fusion(f32[8,192]{1,0:T(8,128)S(1)} %shard_map.148, bf16[8,192]{1,0:T(8,128)(2,1)S(1)} %collective-permute-done.26, bf16[8,192]{1,0:T(8,128)(2,1)S(1)} %collective-permute-done.25, bf16[8,192]{1,0:T(8,128)(2,1)S(1)} %collective-permute-done.24, bf16[8,192]{1,0:T(8,128)(2,1)S(1)} %get-tuple-element.53.refs_4_), kind=kLoop, calls=%fused_computation.7 | loop fusion | flops 13824 | bytes 21504 | tf_op jit(solution)/shard_map/convert_element_type | solution.py:473
  (38 shorter events, 0.1 us)
Async XLA Ops:
  0.0 1.1 %copy-start = (bf16[384,768]{1,0:T(8,128)(2,1)S(1)}, bf16[384,768]{1,0:T(8,128)(2,1)}, u32[]{:S(2)}) copy-start(bf16[384,768]{1,0:T(8,128)(2,1)} %weight.4) | copy-start | bytes 1769476
  0.0 4.7 %copy-start.1 = (bf16[192,1536]{1,0:T(8,128)(2,1)S(1)}, bf16[192,1536]{1,0:T(8,128)(2,1)}, u32[]{:S(2)}) copy-start(bf16[192,1536]{1,0:T(8,128)(2,1)} %weight.6) | copy-start | bytes 1769476
  0.0 5.0 %copy-start.10 = (bf16[2,256,1536]{2,1,0:T(8,128)(2,1)S(1)}, bf16[2,256,1536]{2,1,0:T(8,128)(2,1)}, u32[]{:S(2)}) copy-start(bf16[2,256,1536]{2,1,0:T(8,128)(2,1)} %tokens.1) | copy-start | bytes 4718596
  1.0 4.3 %copy-start.11 = (f32[1536]{0:T(1024)S(1)}, f32[1536]{0:T(1024)}, u32[]{:S(2)}) copy-start(f32[1536]{0:T(1024)} %param.15) | copy-start | bytes 18436
  1.1 7.2 %copy-start.2 = (bf16[384,768]{1,0:T(8,128)(2,1)S(1)}, bf16[384,768]{1,0:T(8,128)(2,1)}, u32[]{:S(2)}) copy-start(bf16[384,768]{1,0:T(8,128)(2,1)} %weight.5) | copy-start | bytes 1769476
  1.2 6.6 %collective-permute-start.3 = (bf16[384,384]{1,0:T(8,128)(2,1)S(1)}, bf16[384,384]{1,0:T(8,128)(2,1)S(1)}, u32[]{:S(2)}, u32[]{:S(2)}) collective-permute-start(bf16[384,384]{1,0:T(8,128)(2,1)S(1)} %get-tuple-element.32), channel_id=1, source_target_pairs={{0,1},{1,0},{2,3},{3,2},{4,5},{5,4},{6,7},{7,6},{8,9},{9,8},{10,11... | collective-permute-start | bytes 884744 | tf_op jit(solution)/shard_map/ppermute | solution.py:33
  1.8 3.6 %collective-permute-start = (bf16[2,1536]{1,0:T(2,128)(2,1)S(1)}, bf16[2,1536]{1,0:T(2,128)(2,1)S(1)}, u32[]{:S(2)}, u32[]{:S(2)}) collective-permute-start(bf16[2,1536]{1,0:T(2,128)(2,1)S(1)} %head.1.after.refs_0_), channel_id=1, source_target_pairs={{0,1},{1,0},{2,3},{3,2},{4,5},{5,4},{6,7},{7,6},{8,9},{9,8},{10,11... | collective-permute-start | bytes 18440 | tf_op jit(solution)/shard_map/ppermute | solution.py:33
  1.8 5.6 %collective-permute-start.1 = (bf16[2,1536]{1,0:T(2,128)(2,1)S(1)}, bf16[2,1536]{1,0:T(2,128)(2,1)S(1)}, u32[]{:S(2)}, u32[]{:S(2)}) collective-permute-start(bf16[2,1536]{1,0:T(2,128)(2,1)S(1)} %head.1.after.refs_0_), channel_id=1, source_target_pairs={{0,2},{1,3},{2,0},{3,1},{4,6},{5,7},{6,4},{7,5},{8,10},{9,11},{10,... | collective-permute-start | bytes 18440 | tf_op jit(solution)/shard_map/ppermute | solution.py:33
  4.7 3.1 %collective-permute-start.2 = (bf16[2,1536]{1,0:T(2,128)(2,1)S(1)}, bf16[2,1536]{1,0:T(2,128)(2,1)S(1)}, u32[]{:S(2)}, u32[]{:S(2)}) collective-permute-start(bf16[2,1536]{1,0:T(2,128)(2,1)S(1)} %head.1.after.refs_0_), channel_id=1, source_target_pairs={{0,3},{1,2},{2,1},{3,0},{4,7},{5,6},{6,5},{7,4},{8,11},{9,10},{10,... | collective-permute-start | bytes 18440 | tf_op jit(solution)/shard_map/ppermute | solution.py:33
  4.9 23.1 %collective-permute-start.15 = (bf16[192,384]{1,0:T(8,128)(2,1)S(1)}, bf16[192,384]{1,0:T(8,128)(2,1)S(1)}, u32[]{:S(2)}, u32[]{:S(2)}) collective-permute-start(bf16[192,384]{1,0:T(8,128)(2,1)S(1)} %get-tuple-element.45), channel_id=1, source_target_pairs={{0,1},{1,0},{2,3},{3,2},{4,5},{5,4},{6,7},{7,6},{8,9},{9,8},{10,11... | collective-permute-start | bytes 442376 | tf_op jit(solution)/shard_map/ppermute | solution.py:33
  5.4 24.5 %collective-permute-start.16 = (bf16[192,384]{1,0:T(8,128)(2,1)S(1)}, bf16[192,384]{1,0:T(8,128)(2,1)S(1)}, u32[]{:S(2)}, u32[]{:S(2)}) collective-permute-start(bf16[192,384]{1,0:T(8,128)(2,1)S(1)} %get-tuple-element.46), channel_id=1, source_target_pairs={{0,2},{1,3},{2,0},{3,1},{4,6},{5,7},{6,4},{7,5},{8,10},{9,11},{10,... | collective-permute-start | bytes 442376 | tf_op jit(solution)/shard_map/ppermute | solution.py:33
  7.4 22.4 %collective-permute-start.17 = (bf16[192,384]{1,0:T(8,128)(2,1)S(1)}, bf16[192,384]{1,0:T(8,128)(2,1)S(1)}, u32[]{:S(2)}, u32[]{:S(2)}) collective-permute-start(bf16[192,384]{1,0:T(8,128)(2,1)S(1)} %get-tuple-element.47), channel_id=1, source_target_pairs={{0,3},{1,2},{2,1},{3,0},{4,7},{5,6},{6,5},{7,4},{8,11},{9,10},{10,... | collective-permute-start | bytes 442376 | tf_op jit(solution)/shard_map/ppermute | solution.py:33
  8.4 6.5 %collective-permute-start.5 = (bf16[384,384]{1,0:T(8,128)(2,1)S(1)}, bf16[384,384]{1,0:T(8,128)(2,1)S(1)}, u32[]{:S(2)}, u32[]{:S(2)}) collective-permute-start(bf16[384,384]{1,0:T(8,128)(2,1)S(1)} %get-tuple-element.35), channel_id=1, source_target_pairs={{0,1},{1,0},{2,3},{3,2},{4,5},{5,4},{6,7},{7,6},{8,9},{9,8},{10,11... | collective-permute-start | bytes 884744 | tf_op jit(solution)/shard_map/ppermute | solution.py:33
  9.1 5.8 %collective-permute-start.4 = (bf16[8,384]{1,0:T(8,128)(2,1)S(1)}, bf16[8,384]{1,0:T(8,128)(2,1)S(1)}, u32[]{:S(2)}, u32[]{:S(2)}) collective-permute-start(bf16[8,384]{1,0:T(8,128)(2,1)S(1)} %get-tuple-element.33.after.refs_0_), channel_id=1, source_target_pairs={{0,2},{1,3},{2,0},{3,1},{4,6},{5,7},{6,4},{7,5},{8,10},{9,11},{10,... | collective-permute-start | bytes 18440 | tf_op jit(solution)/shard_map/ppermute | solution.py:33
  15.3 1.8 %collective-permute-start.6 = (bf16[24,384]{1,0:T(8,128)(2,1)S(1)}, bf16[24,384]{1,0:T(8,128)(2,1)S(1)}, u32[]{:S(2)}, u32[]{:S(2)}) collective-permute-start(bf16[24,384]{1,0:T(8,128)(2,1)S(1)} %get-tuple-element.37), channel_id=1, source_target_pairs={{0,1},{1,0},{2,3},{3,2},{4,5},{5,4},{6,7},{7,6},{8,9},{9,8},{10,11... | collective-permute-start | bytes 55304 | tf_op jit(solution)/shard_map/ppermute | solution.py:33
  15.4 3.8 %collective-permute-start.7 = (bf16[24,384]{1,0:T(8,128)(2,1)S(1)}, bf16[24,384]{1,0:T(8,128)(2,1)S(1)}, u32[]{:S(2)}, u32[]{:S(2)}) collective-permute-start(bf16[24,384]{1,0:T(8,128)(2,1)S(1)} %get-tuple-element.38), channel_id=1, source_target_pairs={{0,2},{1,3},{2,0},{3,1},{4,6},{5,7},{6,4},{7,5},{8,10},{9,11},{10,... | collective-permute-start | bytes 55304 | tf_op jit(solution)/shard_map/ppermute | solution.py:33
  17.1 3.2 %collective-permute-start.8 = (bf16[24,384]{1,0:T(8,128)(2,1)S(1)}, bf16[24,384]{1,0:T(8,128)(2,1)S(1)}, u32[]{:S(2)}, u32[]{:S(2)}) collective-permute-start(bf16[24,384]{1,0:T(8,128)(2,1)S(1)} %get-tuple-element.39), channel_id=1, source_target_pairs={{0,3},{1,2},{2,1},{3,0},{4,7},{5,6},{6,5},{7,4},{8,11},{9,10},{10,... | collective-permute-start | bytes 55304 | tf_op jit(solution)/shard_map/ppermute | solution.py:33
  18.5 7.9 %copy-start.3 = (bf16[384,768]{1,0:T(8,128)(2,1)S(1)}, bf16[384,768]{1,0:T(8,128)(2,1)}, u32[]{:S(2)}) copy-start(bf16[384,768]{1,0:T(8,128)(2,1)} %refs_4_.1) | copy-start | bytes 1769476
  18.5 10.7 %copy-start.9 = (s32[2]{0:T(128)S(1)}, s32[2]{0:T(128)}, u32[]{:S(2)}) copy-start(s32[2]{0:T(128)} %order.1) | copy-start | bytes 28
  18.5 12.6 %copy-start.4 = (bf16[384,768]{1,0:T(8,128)(2,1)S(1)}, bf16[384,768]{1,0:T(8,128)(2,1)}, u32[]{:S(2)}) copy-start(bf16[384,768]{1,0:T(8,128)(2,1)} %refs_9_.1) | copy-start | bytes 1769476
  20.3 20.2 %copy-start.12 = (f32[768]{0:T(1024)S(1)}, f32[768]{0:T(1024)}, u32[]{:S(2)}) copy-start(f32[768]{0:T(1024)} %param.21) | copy-start | bytes 9220
  20.3 20.2 %copy-start.5 = (bf16[192,768]{1,0:T(8,128)(2,1)S(1)}, bf16[192,768]{1,0:T(8,128)(2,1)}, u32[]{:S(2)}) copy-start(bf16[192,768]{1,0:T(8,128)(2,1)} %weight.7) | copy-start | bytes 884740
  21.3 20.9 %copy-start.6 = (bf16[768,192]{0,1:T(8,128)(2,1)S(1)}, bf16[768,192]{0,1:T(8,128)(2,1)}, u32[]{:S(2)}) copy-start(bf16[768,192]{0,1:T(8,128)(2,1)} %param.22) | copy-start | bytes 884740
  21.3 20.9 %copy-start.7 = (bf16[768,192]{0,1:T(8,128)(2,1)S(1)}, bf16[768,192]{0,1:T(8,128)(2,1)}, u32[]{:S(2)}) copy-start(bf16[768,192]{0,1:T(8,128)(2,1)} %param.23) | copy-start | bytes 884740
  21.3 20.8 %copy-start.8 = (bf16[768,192]{0,1:T(8,128)(2,1)S(1)}, bf16[768,192]{0,1:T(8,128)(2,1)}, u32[]{:S(2)}) copy-start(bf16[768,192]{0,1:T(8,128)(2,1)} %param.24) | copy-start | bytes 884740
  21.4 3.8 %collective-permute-start.10 = (bf16[24,384]{1,0:T(8,128)(2,1)S(1)}, bf16[24,384]{1,0:T(8,128)(2,1)S(1)}, u32[]{:S(2)}, u32[]{:S(2)}) collective-permute-start(bf16[24,384]{1,0:T(8,128)(2,1)S(1)} %get-tuple-element.42), channel_id=1, source_target_pairs={{0,2},{1,3},{2,0},{3,1},{4,6},{5,7},{6,4},{7,5},{8,10},{9,11},{10,... | collective-permute-start | bytes 55304 | tf_op jit(solution)/shard_map/ppermute | solution.py:33
  22.5 3.3 %collective-permute-start.11 = (bf16[24,384]{1,0:T(8,128)(2,1)S(1)}, bf16[24,384]{1,0:T(8,128)(2,1)S(1)}, u32[]{:S(2)}, u32[]{:S(2)}) collective-permute-start(bf16[24,384]{1,0:T(8,128)(2,1)S(1)} %get-tuple-element.43), channel_id=1, source_target_pairs={{0,3},{1,2},{2,1},{3,0},{4,7},{5,6},{6,5},{7,4},{8,11},{9,10},{10,... | collective-permute-start | bytes 55304 | tf_op jit(solution)/shard_map/ppermute | solution.py:33
  25.2 1.2 %collective-permute-start.9 = (bf16[24,384]{1,0:T(8,128)(2,1)S(1)}, bf16[24,384]{1,0:T(8,128)(2,1)S(1)}, u32[]{:S(2)}, u32[]{:S(2)}) collective-permute-start(bf16[24,384]{1,0:T(8,128)(2,1)S(1)} %get-tuple-element.41), channel_id=1, source_target_pairs={{0,1},{1,0},{2,3},{3,2},{4,5},{5,4},{6,7},{7,6},{8,9},{9,8},{10,11... | collective-permute-start | bytes 55304 | tf_op jit(solution)/shard_map/ppermute | solution.py:33
  26.7 3.1 %collective-permute-start.12 = (bf16[8,768]{1,0:T(8,128)(2,1)S(1)}, bf16[8,768]{1,0:T(8,128)(2,1)S(1)}, u32[]{:S(2)}, u32[]{:S(2)}) collective-permute-start(bf16[8,768]{1,0:T(8,128)(2,1)S(1)} %shard_map.141.refs_0_.after), channel_id=1, source_target_pairs={{0,1},{1,0},{2,3},{3,2},{4,5},{5,4},{6,7},{7,6},{8,9},{9,8},{10,11... | collective-permute-start | bytes 36872 | tf_op jit(solution)/shard_map/ppermute | solution.py:33
  26.9 3.7 %collective-permute-start.13 = (bf16[8,768]{1,0:T(8,128)(2,1)S(1)}, bf16[8,768]{1,0:T(8,128)(2,1)S(1)}, u32[]{:S(2)}, u32[]{:S(2)}) collective-permute-start(bf16[8,768]{1,0:T(8,128)(2,1)S(1)} %shard_map.141.refs_0_.after), channel_id=1, source_target_pairs={{0,2},{1,3},{2,0},{3,1},{4,6},{5,7},{6,4},{7,5},{8,10},{9,11},{10,... | collective-permute-start | bytes 36872 | tf_op jit(solution)/shard_map/ppermute | solution.py:33
  28.0 3.1 %collective-permute-start.14 = (bf16[8,768]{1,0:T(8,128)(2,1)S(1)}, bf16[8,768]{1,0:T(8,128)(2,1)S(1)}, u32[]{:S(2)}, u32[]{:S(2)}) collective-permute-start(bf16[8,768]{1,0:T(8,128)(2,1)S(1)} %shard_map.141.refs_0_.after), channel_id=1, source_target_pairs={{0,3},{1,2},{2,1},{3,0},{4,7},{5,6},{6,5},{7,4},{8,11},{9,10},{10,... | collective-permute-start | bytes 36872 | tf_op jit(solution)/shard_map/ppermute | solution.py:33
  31.5 1.9 %collective-permute-start.18 = (bf16[8,896]{1,0:T(8,128)(2,1)S(1)}, bf16[8,896]{1,0:T(8,128)(2,1)S(1)}, u32[]{:S(2)}, u32[]{:S(2)}) collective-permute-start(bf16[8,896]{1,0:T(8,128)(2,1)S(1)} %shard_map.144.refs_1_), channel_id=1, source_target_pairs={{0,1},{1,0},{2,3},{3,2},{4,5},{5,4},{6,7},{7,6},{8,9},{9,8},{10,11... | collective-permute-start | bytes 43016 | tf_op jit(solution)/shard_map/ppermute | solution.py:33
  31.7 3.7 %collective-permute-start.19 = (bf16[8,896]{1,0:T(8,128)(2,1)S(1)}, bf16[8,896]{1,0:T(8,128)(2,1)S(1)}, u32[]{:S(2)}, u32[]{:S(2)}) collective-permute-start(bf16[8,896]{1,0:T(8,128)(2,1)S(1)} %shard_map.144.refs_1_), channel_id=1, source_target_pairs={{0,2},{1,3},{2,0},{3,1},{4,6},{5,7},{6,4},{7,5},{8,10},{9,11},{10,... | collective-permute-start | bytes 43016 | tf_op jit(solution)/shard_map/ppermute | solution.py:33
  32.6 3.1 %collective-permute-start.20 = (bf16[8,896]{1,0:T(8,128)(2,1)S(1)}, bf16[8,896]{1,0:T(8,128)(2,1)S(1)}, u32[]{:S(2)}, u32[]{:S(2)}) collective-permute-start(bf16[8,896]{1,0:T(8,128)(2,1)S(1)} %shard_map.144.refs_1_), channel_id=1, source_target_pairs={{0,3},{1,2},{2,1},{3,0},{4,7},{5,6},{6,5},{7,4},{8,11},{9,10},{10,... | collective-permute-start | bytes 43016 | tf_op jit(solution)/shard_map/ppermute | solution.py:33
  35.8 4.6 %collective-permute-start.21 = (bf16[8,896]{1,0:T(8,128)(2,1)S(1)}, bf16[8,896]{1,0:T(8,128)(2,1)S(1)}, u32[]{:S(2)}, u32[]{:S(2)}) collective-permute-start(bf16[8,896]{1,0:T(8,128)(2,1)S(1)} %shard_map.145.refs_0_), channel_id=1, source_target_pairs={{0,8},{1,13},{2,10},{3,15},{4,12},{5,9},{6,14},{7,11},{8,0},{9,5},... | collective-permute-start | bytes 43016 | tf_op jit(solution)/shard_map/ppermute | solution.py:49
  38.4 3.8 %collective-permute-start.23 = (bf16[8,896]{1,0:T(8,128)(2,1)S(1)}, bf16[8,896]{1,0:T(8,128)(2,1)S(1)}, u32[]{:S(2)}, u32[]{:S(2)}) collective-permute-start(bf16[8,896]{1,0:T(8,128)(2,1)S(1)} %shard_map.145.refs_0_), channel_id=1, source_target_pairs={{0,4},{4,0},{8,12},{12,8},{1,5},{5,1},{9,13},{13,9},{2,6},{6,2},{1... | collective-permute-start | bytes 43016 | tf_op jit(solution)/shard_map/ppermute | solution.py:33
  40.5 1.7 %collective-permute-start.22 = (bf16[8,896]{1,0:T(8,128)(2,1)S(1)}, bf16[8,896]{1,0:T(8,128)(2,1)S(1)}, u32[]{:S(2)}, u32[]{:S(2)}) collective-permute-start(bf16[8,896]{1,0:T(8,128)(2,1)S(1)} %collective-permute-done.21.refs_1_), channel_id=1, source_target_pairs={{0,1},{1,0},{2,3},{3,2},{4,5},{5,4},{6,7},{7,6},{8,9},{9,8},{10,11... | collective-permute-start | bytes 43016 | tf_op jit(solution)/shard_map/ppermute | solution.py:33
  43.3 2.2 %collective-permute-start.24 = (bf16[8,192]{1,0:T(8,128)(2,1)S(1)}, bf16[8,192]{1,0:T(8,128)(2,1)S(1)}, u32[]{:S(2)}, u32[]{:S(2)}) collective-permute-start(bf16[8,192]{1,0:T(8,128)(2,1)S(1)} %get-tuple-element.54), channel_id=1, source_target_pairs={{0,1},{1,0},{2,3},{3,2},{4,5},{5,4},{6,7},{7,6},{8,9},{9,8},{10,11... | collective-permute-start | bytes 9224 | tf_op jit(solution)/shard_map/ppermute | solution.py:33
  43.3 3.7 %collective-permute-start.25 = (bf16[8,192]{1,0:T(8,128)(2,1)S(1)}, bf16[8,192]{1,0:T(8,128)(2,1)S(1)}, u32[]{:S(2)}, u32[]{:S(2)}) collective-permute-start(bf16[8,192]{1,0:T(8,128)(2,1)S(1)} %get-tuple-element.55), channel_id=1, source_target_pairs={{0,2},{1,3},{2,0},{3,1},{4,6},{5,7},{6,4},{7,5},{8,10},{9,11},{10,... | collective-permute-start | bytes 9224 | tf_op jit(solution)/shard_map/ppermute | solution.py:33
  44.5 3.0 %collective-permute-start.26 = (bf16[8,192]{1,0:T(8,128)(2,1)S(1)}, bf16[8,192]{1,0:T(8,128)(2,1)S(1)}, u32[]{:S(2)}, u32[]{:S(2)}) collective-permute-start(bf16[8,192]{1,0:T(8,128)(2,1)S(1)} %get-tuple-element.56), channel_id=1, source_target_pairs={{0,3},{1,2},{2,1},{3,0},{4,7},{5,6},{6,5},{7,4},{8,11},{9,10},{10,... | collective-permute-start | bytes 9224 | tf_op jit(solution)/shard_map/ppermute | solution.py:33

commit v4 on v3

--- a/solution.py
+++ b/solution.py
@@ -135,7 +135,7 @@
         blocks[block] = normed[:, block * mine : (block + 1) * mine]
     part = contract(blocks[me].astype(BF16), kept[...], 1, 0)
     part = part + contract(blocks[me ^ 1].astype(BF16), fetched[...], 1, 0)
-    out[...] = part.astype(BF16)
+    out[...] = part
 
 
 def grouped(shape, axis, span):
@@ -329,6 +329,14 @@
     out[...] = blocks[me]
 
 
+def final_kernel(place, residual, *refs):
+    terms, out = refs[:-1], refs[-1]
+    total = terms[0][...].astype(F32)
+    for term in terms[1:]:
+        total = total + term[...].astype(F32)
+    out[...] = (residual[...] + total).astype(BF16)
+
+
 def local(
     tile_patches,
     vit_gain,
@@ -401,7 +409,7 @@
     query_part, first = call(
         functools.partial(query_kernel, size),
         [
-            jax.ShapeDtypeStruct((count, vit_width // 2), BF16),
+            jax.ShapeDtypeStruct((count, vit_width // 2), F32),
             jax.ShapeDtypeStruct((count, rows), F32),
         ],
         [pltpu.VMEM((size, tiles, width), F32), pltpu.VMEM((size, count, rows), F32)],
@@ -467,10 +475,9 @@
         specs=[pl.ANY],
     )(place, *all_tiles, terms[0])
     terms = deal(terms, "fsdp")
-    summed = terms[0].astype(F32)
-    for step in range(1, size):
-        summed = summed + terms[step].astype(F32)
-    return (residual + summed).astype(BF16)
+    return call(
+        final_kernel, jax.ShapeDtypeStruct((count, head_width), BF16)
+    )(place, residual, *terms)
 
 
 def solution(mesh):

time: 48.3 us -> 48.4 us (level)
  Pallas kernels: 6.14 us -> 6.75 us
  other arithmetic: 1.97 us -> 1.37 us
    pallas_call x13 -> x14, Pallas kernels: 5.18 us -> 5.78 us  [run(): pl.pallas_call(body, out_shape=outs, in_specs=[smem] + [vmem] * last + [p...]
    convert_element_type x1 -> x0, other arithmetic: 0.6 us -> none  [local(): return (residual + summed).astype(BF16)]
where the time goes in v4:
time: 48.4 us; the launch traced here: 48.3 us
  starting transfers between devices  21.6 us (45%)
  waiting for transfers between devices  17.4 us (36%)
  Pallas kernels  6.75 us (14%)
  other arithmetic  1.37 us (3%)
  between operations  0.9 us (2%)
    ppermute x26, starting transfers between devices, swap(): lax.ppermute(array, axis, [(i, other(i, step, size)) for i in range(size)])  19.1 us
    ppermute x26, waiting for transfers between devices, swap(): lax.ppermute(array, axis, [(i, other(i, step, size)) for i in range(size)])  17 us
    pallas_call x14, Pallas kernels, run(): pl.pallas_call(body, out_shape=outs, in_specs=[smem] + [vmem] * last + [p...  5.78 us
    ppermute x1, starting transfers between devices, rows_of_all(): far = lax.ppermute(array, ('seq', 'fsdp'), pairs)  2.59 us
  transfers between devices with their start and end apart: 27, of which 15 were waited for; matrix products, arithmetic and copies ran while one was open for 3% of the time, Pallas kernels for 7%

profile of v4, /device:TPU:0, one launch (start us, length us, event | category | flops | bytes accessed | tf_op | source)
XLA Modules:
  0.0 48.3 jit_solution(4708967669025816184)
XLA Ops:
  0.0 1.0 %head.1.after.refs_0_ = bf16[2,1536]{1,0:T(2,128)(2,1)S(1)} custom-call(bf16[2,256,1536]{2,1,0:T(8,128)(2,1)} %tokens.1), custom_call_target="tpu_custom_call" | custom-call | tf_op jit(solution)/shard_map/head/pallas_call | solution.py:367
  1.0 0.0 copy-start.11
  1.0 0.1 copy-done
  1.1 0.1 shard_map.136
  1.2 0.6 %collective-permute-start.3 = (bf16[384,384]{1,0:T(8,128)(2,1)S(1)}, bf16[384,384]{1,0:T(8,128)(2,1)S(1)}, u32[]{:S(2)}, u32[]{:S(2)}) collective-permute-start(bf16[384,384]{1,0:T(8,128)(2,1)S(1)} %get-tuple-element.32), channel_id=1, source_target_pairs={{0,1},{1,0},{2,3},{3,2},{4,5},{5,4},{6,7},{7,6},{8,9},{9,8},{10,11... | collective-permute-start | bytes 884744 | tf_op jit(solution)/shard_map/ppermute | solution.py:33
  1.8 0.1 collective-permute-start
  1.8 2.9 %collective-permute-start.1 = (bf16[2,1536]{1,0:T(2,128)(2,1)S(1)}, bf16[2,1536]{1,0:T(2,128)(2,1)S(1)}, u32[]{:S(2)}, u32[]{:S(2)}) collective-permute-start(bf16[2,1536]{1,0:T(2,128)(2,1)S(1)} %head.1.after.refs_0_), channel_id=1, source_target_pairs={{0,2},{1,3},{2,0},{3,1},{4,6},{5,7},{6,4},{7,5},{8,10},{9,11},{10,... | collective-permute-start | bytes 18440 | tf_op jit(solution)/shard_map/ppermute | solution.py:33
  4.7 0.1 shard_map.142
  4.9 0.2 collective-permute-start.15
  5.0 0.3 convert_reduce_fusion
  5.4 2.1 %collective-permute-start.16 = (bf16[192,384]{1,0:T(8,128)(2,1)S(1)}, bf16[192,384]{1,0:T(8,128)(2,1)S(1)}, u32[]{:S(2)}, u32[]{:S(2)}) collective-permute-start(bf16[192,384]{1,0:T(8,128)(2,1)S(1)} %get-tuple-element.46), channel_id=1, source_target_pairs={{0,2},{1,3},{2,0},{3,1},{4,6},{5,7},{6,4},{7,5},{8,10},{9,11},{10,... | collective-permute-start | bytes 442376 | tf_op jit(solution)/shard_map/ppermute | solution.py:33
  7.5 0.4 collective-permute-done.2.refs_3_
  7.8 0.4 shard_map.137
  8.2 0.1 shard_map.138
  8.4 0.7 %collective-permute-start.5 = (bf16[384,384]{1,0:T(8,128)(2,1)S(1)}, bf16[384,384]{1,0:T(8,128)(2,1)S(1)}, u32[]{:S(2)}, u32[]{:S(2)}) collective-permute-start(bf16[384,384]{1,0:T(8,128)(2,1)S(1)} %get-tuple-element.35), channel_id=1, source_target_pairs={{0,1},{1,0},{2,3},{3,2},{4,5},{5,4},{6,7},{7,6},{8,9},{9,8},{10,11... | collective-permute-start | bytes 884744 | tf_op jit(solution)/shard_map/ppermute | solution.py:33
  9.1 1.1 %collective-permute-start.4 = (f32[8,384]{1,0:T(8,128)S(1)}, f32[8,384]{1,0:T(8,128)S(1)}, u32[]{:S(2)}, u32[]{:S(2)}) collective-permute-start(f32[8,384]{1,0:T(8,128)S(1)} %get-tuple-element.33.after.refs_0_), channel_id=1, source_target_pairs={{0,2},{1,3},{2,0},{3,1},{4,6},{5,7},{6,4},{7,5},{8,10},{9,11},{10,... | collective-permute-start | bytes 36872 | tf_op jit(solution)/shard_map/ppermute | solution.py:33
  10.2 0.5 %fusion.2 = f32[2,256]{1,0:T(2,128)S(1)} fusion(bf16[2,256,1536]{2,1,0:T(8,128)(2,1)S(1)} %copy-done.10, f32[2,256]{1,0:T(2,128)S(1)} %broadcast_multiply_fusion), kind=kLoop, calls=%fused_computation.4 | loop fusion | flops 3145216 | bytes 1576960 | tf_op jit(solution)/shard_map/reduce_sum | solution.py:62
  10.7 4.2 %collective-permute-done.4.refs_1_ = f32[8,384]{1,0:T(8,128)S(1)} collective-permute-done((f32[8,384]{1,0:T(8,128)S(1)}, f32[8,384]{1,0:T(8,128)S(1)}, u32[]{:S(2)}, u32[]{:S(2)}) %collective-permute-start.4) | collective-permute-done | bytes 12320 | tf_op jit(solution)/shard_map/ppermute | solution.py:33
  15.0 0.4 shard_map.139
  15.4 0.1 collective-permute-start.6
  15.5 1.7 %collective-permute-start.7 = (bf16[24,384]{1,0:T(8,128)(2,1)S(1)}, bf16[24,384]{1,0:T(8,128)(2,1)S(1)}, u32[]{:S(2)}, u32[]{:S(2)}) collective-permute-start(bf16[24,384]{1,0:T(8,128)(2,1)S(1)} %get-tuple-element.38), channel_id=1, source_target_pairs={{0,2},{1,3},{2,0},{3,1},{4,6},{5,7},{6,4},{7,5},{8,10},{9,11},{10,... | collective-permute-start | bytes 55304 | tf_op jit(solution)/shard_map/ppermute | solution.py:33
  17.2 0.9 %collective-permute-start.8 = (bf16[24,384]{1,0:T(8,128)(2,1)S(1)}, bf16[24,384]{1,0:T(8,128)(2,1)S(1)}, u32[]{:S(2)}, u32[]{:S(2)}) collective-permute-start(bf16[24,384]{1,0:T(8,128)(2,1)S(1)} %get-tuple-element.39), channel_id=1, source_target_pairs={{0,3},{1,2},{2,1},{3,0},{4,7},{5,6},{6,5},{7,4},{8,11},{9,10},{10,... | collective-permute-start | bytes 55304 | tf_op jit(solution)/shard_map/ppermute | solution.py:33
  18.1 0.5 %fusion.4.refs_4_ = bf16[2,256,1536]{2,1,0:T(8,128)(2,1)S(1)} fusion(bf16[2,256,1536]{2,1,0:T(8,128)(2,1)S(1)} %copy-done.10, f32[1536]{0:T(1024)S(1)} %copy-done.11, f32[2,256]{1,0:T(2,128)S(1)} %add_rsqrt_fusion, f32[2,256]{1,0:T(2,128)S(1)} %broadcast_multiply_fusion), kind=kLoop, calls=%fused_computation.6 | loop fusion | flops 3932160 | bytes 3155968 | tf_op jit(solution)/shard_map/convert_element_type | solution.py:63
  18.6 0.0 copy-start.3
  18.7 0.0 copy-start.9
  18.7 0.0 copy-start.4
  18.7 0.7 %collective-permute-done.7.refs_2_ = bf16[24,384]{1,0:T(8,128)(2,1)S(1)} collective-permute-done((bf16[24,384]{1,0:T(8,128)(2,1)S(1)}, bf16[24,384]{1,0:T(8,128)(2,1)S(1)}, u32[]{:S(2)}, u32[]{:S(2)}) %collective-permute-start.7) | collective-permute-done | bytes 18464 | tf_op jit(solution)/shard_map/ppermute | solution.py:33
  19.3 1.1 %collective-permute-done.8.refs_3_ = bf16[24,384]{1,0:T(8,128)(2,1)S(1)} collective-permute-done((bf16[24,384]{1,0:T(8,128)(2,1)S(1)}, bf16[24,384]{1,0:T(8,128)(2,1)S(1)}, u32[]{:S(2)}, u32[]{:S(2)}) %collective-permute-start.8) | collective-permute-done | bytes 18464 | tf_op jit(solution)/shard_map/ppermute | solution.py:33
  20.4 1.0 %shard_map.140 = (bf16[24,384]{1,0:T(8,128)(2,1)S(1)}, bf16[24,384]{1,0:T(8,128)(2,1)S(1)}, bf16[24,384]{1,0:T(8,128)(2,1)S(1)}, bf16[24,384]{1,0:T(8,128)(2,1)S(1)}) custom-call(s32[1]{0:T(128)} %bitcast.place.refs_0_, bf16[24,384]{1,0:T(8,128)(2,1)S(1)} %get-tuple-element.36.refs_0_, bf16[24,384]{1,0:T(8,128)(2,1)S(1)} %collective-permute-done.6.refs_1_, ...), custom_call_target="tpu_custom_call" | custom-call | tf_op jit(solution)/shard_map/pallas_call | solution.py:81
  21.4 0.0 copy-start.6
  21.5 0.0 copy-start.7
  21.5 0.0 copy-start.8
  21.5 1.2 %collective-permute-start.10 = (bf16[24,384]{1,0:T(8,128)(2,1)S(1)}, bf16[24,384]{1,0:T(8,128)(2,1)S(1)}, u32[]{:S(2)}, u32[]{:S(2)}) collective-permute-start(bf16[24,384]{1,0:T(8,128)(2,1)S(1)} %get-tuple-element.42), channel_id=1, source_target_pairs={{0,2},{1,3},{2,0},{3,1},{4,6},{5,7},{6,4},{7,5},{8,10},{9,11},{10,... | collective-permute-start | bytes 55304 | tf_op jit(solution)/shard_map/ppermute | solution.py:33
  22.6 0.4 collective-permute-start.11
  23.1 2.3 %collective-permute-done.10.refs_2_ = bf16[24,384]{1,0:T(8,128)(2,1)S(1)} collective-permute-done((bf16[24,384]{1,0:T(8,128)(2,1)S(1)}, bf16[24,384]{1,0:T(8,128)(2,1)S(1)}, u32[]{:S(2)}, u32[]{:S(2)}) %collective-permute-start.10) | collective-permute-done | bytes 18464 | tf_op jit(solution)/shard_map/ppermute | solution.py:33
  25.3 0.6 %collective-permute-done.11.refs_3_ = bf16[24,384]{1,0:T(8,128)(2,1)S(1)} collective-permute-done((bf16[24,384]{1,0:T(8,128)(2,1)S(1)}, bf16[24,384]{1,0:T(8,128)(2,1)S(1)}, u32[]{:S(2)}, u32[]{:S(2)}) %collective-permute-start.11) | collective-permute-done | bytes 18464 | tf_op jit(solution)/shard_map/ppermute | solution.py:33
  26.0 0.5 %collective-permute-done.9.refs_1_ = bf16[24,384]{1,0:T(8,128)(2,1)S(1)} collective-permute-done((bf16[24,384]{1,0:T(8,128)(2,1)S(1)}, bf16[24,384]{1,0:T(8,128)(2,1)S(1)}, u32[]{:S(2)}, u32[]{:S(2)}) %collective-permute-start.9) | collective-permute-done | bytes 18464 | tf_op jit(solution)/shard_map/ppermute | solution.py:33
  26.5 0.3 shard_map.141.refs_0_.after
  26.8 0.2 collective-permute-start.12
  27.0 1.1 %collective-permute-start.13 = (bf16[8,768]{1,0:T(8,128)(2,1)S(1)}, bf16[8,768]{1,0:T(8,128)(2,1)S(1)}, u32[]{:S(2)}, u32[]{:S(2)}) collective-permute-start(bf16[8,768]{1,0:T(8,128)(2,1)S(1)} %shard_map.141.refs_0_.after), channel_id=1, source_target_pairs={{0,2},{1,3},{2,0},{3,1},{4,6},{5,7},{6,4},{7,5},{8,10},{9,11},{10,... | collective-permute-start | bytes 36872 | tf_op jit(solution)/shard_map/ppermute | solution.py:33
  28.1 0.6 %collective-permute-start.14 = (bf16[8,768]{1,0:T(8,128)(2,1)S(1)}, bf16[8,768]{1,0:T(8,128)(2,1)S(1)}, u32[]{:S(2)}, u32[]{:S(2)}) collective-permute-start(bf16[8,768]{1,0:T(8,128)(2,1)S(1)} %shard_map.141.refs_0_.after), channel_id=1, source_target_pairs={{0,3},{1,2},{2,1},{3,0},{4,7},{5,6},{6,5},{7,4},{8,11},{9,10},{10,... | collective-permute-start | bytes 36872 | tf_op jit(solution)/shard_map/ppermute | solution.py:33
  29.4 0.6 %shard_map.143.refs_10_ = bf16[8,128]{1,0:T(8,128)(2,1)S(1)} custom-call(s32[1]{0:T(128)} %bitcast.place.refs_0_, s32[2]{0:T(128)S(1)} %copy-done.9, s32[1]{0:T(128)S(6)} %copy.15.counts, bf16[2,1536]{1,0:T(2,128)(2,1)S(1)} %head.1.after.refs_0_), custom_call_target="tpu_custom_call" | custom-call | tf_op jit(solution)/shard_map/pallas_call | solution.py:81
  30.0 0.7 %collective-permute-done.13.refs_2_ = bf16[8,768]{1,0:T(8,128)(2,1)S(1)} collective-permute-done((bf16[8,768]{1,0:T(8,128)(2,1)S(1)}, bf16[8,768]{1,0:T(8,128)(2,1)S(1)}, u32[]{:S(2)}, u32[]{:S(2)}) %collective-permute-start.13) | collective-permute-done | bytes 12320 | tf_op jit(solution)/shard_map/ppermute | solution.py:33
  30.7 0.5 %collective-permute-done.14.refs_3_ = bf16[8,768]{1,0:T(8,128)(2,1)S(1)} collective-permute-done((bf16[8,768]{1,0:T(8,128)(2,1)S(1)}, bf16[8,768]{1,0:T(8,128)(2,1)S(1)}, u32[]{:S(2)}, u32[]{:S(2)}) %collective-permute-start.14) | collective-permute-done | bytes 12320 | tf_op jit(solution)/shard_map/ppermute | solution.py:33
  31.2 0.4 shard_map.144.refs_1_
  31.7 0.1 collective-permute-start.18
  31.8 0.9 %collective-permute-start.19 = (bf16[8,896]{1,0:T(8,128)(2,1)S(1)}, bf16[8,896]{1,0:T(8,128)(2,1)S(1)}, u32[]{:S(2)}, u32[]{:S(2)}) collective-permute-start(bf16[8,896]{1,0:T(8,128)(2,1)S(1)} %shard_map.144.refs_1_), channel_id=1, source_target_pairs={{0,2},{1,3},{2,0},{3,1},{4,6},{5,7},{6,4},{7,5},{8,10},{9,11},{10,... | collective-permute-start | bytes 43016 | tf_op jit(solution)/shard_map/ppermute | solution.py:33
  32.7 0.8 %collective-permute-start.20 = (bf16[8,896]{1,0:T(8,128)(2,1)S(1)}, bf16[8,896]{1,0:T(8,128)(2,1)S(1)}, u32[]{:S(2)}, u32[]{:S(2)}) collective-permute-start(bf16[8,896]{1,0:T(8,128)(2,1)S(1)} %shard_map.144.refs_1_), channel_id=1, source_target_pairs={{0,3},{1,2},{2,1},{3,0},{4,7},{5,6},{6,5},{7,4},{8,11},{9,10},{10,... | collective-permute-start | bytes 43016 | tf_op jit(solution)/shard_map/ppermute | solution.py:33
  33.6 2.0 %collective-permute-done.19.refs_3_ = bf16[8,896]{1,0:T(8,128)(2,1)S(1)} collective-permute-done((bf16[8,896]{1,0:T(8,128)(2,1)S(1)}, bf16[8,896]{1,0:T(8,128)(2,1)S(1)}, u32[]{:S(2)}, u32[]{:S(2)}) %collective-permute-start.19) | collective-permute-done | bytes 14368 | tf_op jit(solution)/shard_map/ppermute | solution.py:33
  35.5 0.4 collective-permute-done.20.refs_4_
  35.9 0.1 shard_map.145.refs_0_
  36.0 2.6 %collective-permute-start.21 = (bf16[8,896]{1,0:T(8,128)(2,1)S(1)}, bf16[8,896]{1,0:T(8,128)(2,1)S(1)}, u32[]{:S(2)}, u32[]{:S(2)}) collective-permute-start(bf16[8,896]{1,0:T(8,128)(2,1)S(1)} %shard_map.145.refs_0_), channel_id=1, source_target_pairs={{0,8},{1,13},{2,10},{3,15},{4,12},{5,9},{6,14},{7,11},{8,0},{9,5},... | collective-permute-start | bytes 43016 | tf_op jit(solution)/shard_map/ppermute | solution.py:49
  38.6 1.6 %collective-permute-start.23 = (bf16[8,896]{1,0:T(8,128)(2,1)S(1)}, bf16[8,896]{1,0:T(8,128)(2,1)S(1)}, u32[]{:S(2)}, u32[]{:S(2)}) collective-permute-start(bf16[8,896]{1,0:T(8,128)(2,1)S(1)} %shard_map.145.refs_0_), channel_id=1, source_target_pairs={{0,4},{4,0},{8,12},{12,8},{1,5},{5,1},{9,13},{13,9},{2,6},{6,2},{1... | collective-permute-start | bytes 43016 | tf_op jit(solution)/shard_map/ppermute | solution.py:33
  40.1 0.5 collective-permute-done.21.refs_1_
  40.6 0.1 shard_map.146
  40.8 1.5 %collective-permute-done.23.refs_3_ = bf16[8,896]{1,0:T(8,128)(2,1)S(1)} collective-permute-done((bf16[8,896]{1,0:T(8,128)(2,1)S(1)}, bf16[8,896]{1,0:T(8,128)(2,1)S(1)}, u32[]{:S(2)}, u32[]{:S(2)}) %collective-permute-start.23) | collective-permute-done | bytes 14368 | tf_op jit(solution)/shard_map/ppermute | solution.py:33
  42.3 1.1 %shard_map.147 = (bf16[8,192]{1,0:T(8,128)(2,1)S(1)}, bf16[8,192]{1,0:T(8,128)(2,1)S(1)}, bf16[8,192]{1,0:T(8,128)(2,1)S(1)}, bf16[8,192]{1,0:T(8,128)(2,1)S(1)}) custom-call(s32[1]{0:T(128)} %bitcast.place.refs_0_, bf16[8,896]{1,0:T(8,128)(2,1)S(1)} %shard_map.145.refs_0_, bf16[8,896]{1,0:T(8,128)(2,1)S(1)} %collective-permute-done.21.refs_1_, ...), custom_call_target="tpu_custom_call" | custom-call | tf_op jit(solution)/shard_map/pallas_call | solution.py:81
  43.4 0.0 collective-permute-start.24
  43.5 1.2 %collective-permute-start.25 = (bf16[8,192]{1,0:T(8,128)(2,1)S(1)}, bf16[8,192]{1,0:T(8,128)(2,1)S(1)}, u32[]{:S(2)}, u32[]{:S(2)}) collective-permute-start(bf16[8,192]{1,0:T(8,128)(2,1)S(1)} %get-tuple-element.55), channel_id=1, source_target_pairs={{0,2},{1,3},{2,0},{3,1},{4,6},{5,7},{6,4},{7,5},{8,10},{9,11},{10,... | collective-permute-start | bytes 9224 | tf_op jit(solution)/shard_map/ppermute | solution.py:33
  44.6 0.7 %collective-permute-start.26 = (bf16[8,192]{1,0:T(8,128)(2,1)S(1)}, bf16[8,192]{1,0:T(8,128)(2,1)S(1)}, u32[]{:S(2)}, u32[]{:S(2)}) collective-permute-start(bf16[8,192]{1,0:T(8,128)(2,1)S(1)} %get-tuple-element.56), channel_id=1, source_target_pairs={{0,3},{1,2},{2,1},{3,0},{4,7},{5,6},{6,5},{7,4},{8,11},{9,10},{10,... | collective-permute-start | bytes 9224 | tf_op jit(solution)/shard_map/ppermute | solution.py:33
  45.3 0.3 shard_map.148.residual
  45.7 1.5 %collective-permute-done.25.refs_2_ = bf16[8,192]{1,0:T(8,128)(2,1)S(1)} collective-permute-done((bf16[8,192]{1,0:T(8,128)(2,1)S(1)}, bf16[8,192]{1,0:T(8,128)(2,1)S(1)}, u32[]{:S(2)}, u32[]{:S(2)}) %collective-permute-start.25) | collective-permute-done | bytes 3104 | tf_op jit(solution)/shard_map/ppermute | solution.py:33
  47.2 0.5 %collective-permute-done.26.refs_3_ = bf16[8,192]{1,0:T(8,128)(2,1)S(1)} collective-permute-done((bf16[8,192]{1,0:T(8,128)(2,1)S(1)}, bf16[8,192]{1,0:T(8,128)(2,1)S(1)}, u32[]{:S(2)}, u32[]{:S(2)}) %collective-permute-start.26) | collective-permute-done | bytes 3104 | tf_op jit(solution)/shard_map/ppermute | solution.py:33
  47.7 0.6 %shard_map.149 = bf16[8,192]{1,0:T(8,128)(2,1)} custom-call(s32[1]{0:T(128)} %bitcast.place.refs_0_, f32[8,192]{1,0:T(8,128)S(1)} %shard_map.148.residual, bf16[8,192]{1,0:T(8,128)(2,1)S(1)} %get-tuple-element.53.refs_4_.refs_0_, bf16[8,192]{1,0:T(8,128)(2,1)S(1)} %collective-permute-done.24.refs_1_, bf16[8,192]{1,0:T(8,128)(2,1)S(1)} %collective-permute-done.25.refs_2_, ...), custom_call_target="tpu_custom_call" | custom-call | tf_op jit(solution)/shard_map/pallas_call | solution.py:81
  (38 shorter events, 0.1 us)
Async XLA Ops:
  0.0 1.1 %copy-start = (bf16[384,768]{1,0:T(8,128)(2,1)S(1)}, bf16[384,768]{1,0:T(8,128)(2,1)}, u32[]{:S(2)}) copy-start(bf16[384,768]{1,0:T(8,128)(2,1)} %weight.4) | copy-start | bytes 1769476
  0.0 4.7 %copy-start.1 = (bf16[192,1536]{1,0:T(8,128)(2,1)S(1)}, bf16[192,1536]{1,0:T(8,128)(2,1)}, u32[]{:S(2)}) copy-start(bf16[192,1536]{1,0:T(8,128)(2,1)} %weight.6) | copy-start | bytes 1769476
  0.0 5.0 %copy-start.10 = (bf16[2,256,1536]{2,1,0:T(8,128)(2,1)S(1)}, bf16[2,256,1536]{2,1,0:T(8,128)(2,1)}, u32[]{:S(2)}) copy-start(bf16[2,256,1536]{2,1,0:T(8,128)(2,1)} %tokens.1) | copy-start | bytes 4718596
  1.0 4.3 %copy-start.11 = (f32[1536]{0:T(1024)S(1)}, f32[1536]{0:T(1024)}, u32[]{:S(2)}) copy-start(f32[1536]{0:T(1024)} %param.15) | copy-start | bytes 18436
  1.1 7.2 %copy-start.2 = (bf16[384,768]{1,0:T(8,128)(2,1)S(1)}, bf16[384,768]{1,0:T(8,128)(2,1)}, u32[]{:S(2)}) copy-start(bf16[384,768]{1,0:T(8,128)(2,1)} %weight.5) | copy-start | bytes 1769476
  1.2 6.6 %collective-permute-start.3 = (bf16[384,384]{1,0:T(8,128)(2,1)S(1)}, bf16[384,384]{1,0:T(8,128)(2,1)S(1)}, u32[]{:S(2)}, u32[]{:S(2)}) collective-permute-start(bf16[384,384]{1,0:T(8,128)(2,1)S(1)} %get-tuple-element.32), channel_id=1, source_target_pairs={{0,1},{1,0},{2,3},{3,2},{4,5},{5,4},{6,7},{7,6},{8,9},{9,8},{10,11... | collective-permute-start | bytes 884744 | tf_op jit(solution)/shard_map/ppermute | solution.py:33
  1.8 3.6 %collective-permute-start = (bf16[2,1536]{1,0:T(2,128)(2,1)S(1)}, bf16[2,1536]{1,0:T(2,128)(2,1)S(1)}, u32[]{:S(2)}, u32[]{:S(2)}) collective-permute-start(bf16[2,1536]{1,0:T(2,128)(2,1)S(1)} %head.1.after.refs_0_), channel_id=1, source_target_pairs={{0,1},{1,0},{2,3},{3,2},{4,5},{5,4},{6,7},{7,6},{8,9},{9,8},{10,11... | collective-permute-start | bytes 18440 | tf_op jit(solution)/shard_map/ppermute | solution.py:33
  1.8 5.6 %collective-permute-start.1 = (bf16[2,1536]{1,0:T(2,128)(2,1)S(1)}, bf16[2,1536]{1,0:T(2,128)(2,1)S(1)}, u32[]{:S(2)}, u32[]{:S(2)}) collective-permute-start(bf16[2,1536]{1,0:T(2,128)(2,1)S(1)} %head.1.after.refs_0_), channel_id=1, source_target_pairs={{0,2},{1,3},{2,0},{3,1},{4,6},{5,7},{6,4},{7,5},{8,10},{9,11},{10,... | collective-permute-start | bytes 18440 | tf_op jit(solution)/shard_map/ppermute | solution.py:33
  4.7 3.1 %collective-permute-start.2 = (bf16[2,1536]{1,0:T(2,128)(2,1)S(1)}, bf16[2,1536]{1,0:T(2,128)(2,1)S(1)}, u32[]{:S(2)}, u32[]{:S(2)}) collective-permute-start(bf16[2,1536]{1,0:T(2,128)(2,1)S(1)} %head.1.after.refs_0_), channel_id=1, source_target_pairs={{0,3},{1,2},{2,1},{3,0},{4,7},{5,6},{6,5},{7,4},{8,11},{9,10},{10,... | collective-permute-start | bytes 18440 | tf_op jit(solution)/shard_map/ppermute | solution.py:33
  4.9 23.3 %collective-permute-start.15 = (bf16[192,384]{1,0:T(8,128)(2,1)S(1)}, bf16[192,384]{1,0:T(8,128)(2,1)S(1)}, u32[]{:S(2)}, u32[]{:S(2)}) collective-permute-start(bf16[192,384]{1,0:T(8,128)(2,1)S(1)} %get-tuple-element.45), channel_id=1, source_target_pairs={{0,1},{1,0},{2,3},{3,2},{4,5},{5,4},{6,7},{7,6},{8,9},{9,8},{10,11... | collective-permute-start | bytes 442376 | tf_op jit(solution)/shard_map/ppermute | solution.py:33
  5.4 24.6 %collective-permute-start.16 = (bf16[192,384]{1,0:T(8,128)(2,1)S(1)}, bf16[192,384]{1,0:T(8,128)(2,1)S(1)}, u32[]{:S(2)}, u32[]{:S(2)}) collective-permute-start(bf16[192,384]{1,0:T(8,128)(2,1)S(1)} %get-tuple-element.46), channel_id=1, source_target_pairs={{0,2},{1,3},{2,0},{3,1},{4,6},{5,7},{6,4},{7,5},{8,10},{9,11},{10,... | collective-permute-start | bytes 442376 | tf_op jit(solution)/shard_map/ppermute | solution.py:33
  7.4 22.5 %collective-permute-start.17 = (bf16[192,384]{1,0:T(8,128)(2,1)S(1)}, bf16[192,384]{1,0:T(8,128)(2,1)S(1)}, u32[]{:S(2)}, u32[]{:S(2)}) collective-permute-start(bf16[192,384]{1,0:T(8,128)(2,1)S(1)} %get-tuple-element.47), channel_id=1, source_target_pairs={{0,3},{1,2},{2,1},{3,0},{4,7},{5,6},{6,5},{7,4},{8,11},{9,10},{10,... | collective-permute-start | bytes 442376 | tf_op jit(solution)/shard_map/ppermute | solution.py:33
  8.4 6.6 %collective-permute-start.5 = (bf16[384,384]{1,0:T(8,128)(2,1)S(1)}, bf16[384,384]{1,0:T(8,128)(2,1)S(1)}, u32[]{:S(2)}, u32[]{:S(2)}) collective-permute-start(bf16[384,384]{1,0:T(8,128)(2,1)S(1)} %get-tuple-element.35), channel_id=1, source_target_pairs={{0,1},{1,0},{2,3},{3,2},{4,5},{5,4},{6,7},{7,6},{8,9},{9,8},{10,11... | collective-permute-start | bytes 884744 | tf_op jit(solution)/shard_map/ppermute | solution.py:33
  9.1 5.9 %collective-permute-start.4 = (f32[8,384]{1,0:T(8,128)S(1)}, f32[8,384]{1,0:T(8,128)S(1)}, u32[]{:S(2)}, u32[]{:S(2)}) collective-permute-start(f32[8,384]{1,0:T(8,128)S(1)} %get-tuple-element.33.after.refs_0_), channel_id=1, source_target_pairs={{0,2},{1,3},{2,0},{3,1},{4,6},{5,7},{6,4},{7,5},{8,10},{9,11},{10,... | collective-permute-start | bytes 36872 | tf_op jit(solution)/shard_map/ppermute | solution.py:33
  15.4 1.8 %collective-permute-start.6 = (bf16[24,384]{1,0:T(8,128)(2,1)S(1)}, bf16[24,384]{1,0:T(8,128)(2,1)S(1)}, u32[]{:S(2)}, u32[]{:S(2)}) collective-permute-start(bf16[24,384]{1,0:T(8,128)(2,1)S(1)} %get-tuple-element.37), channel_id=1, source_target_pairs={{0,1},{1,0},{2,3},{3,2},{4,5},{5,4},{6,7},{7,6},{8,9},{9,8},{10,11... | collective-permute-start | bytes 55304 | tf_op jit(solution)/shard_map/ppermute | solution.py:33
  15.5 3.8 %collective-permute-start.7 = (bf16[24,384]{1,0:T(8,128)(2,1)S(1)}, bf16[24,384]{1,0:T(8,128)(2,1)S(1)}, u32[]{:S(2)}, u32[]{:S(2)}) collective-permute-start(bf16[24,384]{1,0:T(8,128)(2,1)S(1)} %get-tuple-element.38), channel_id=1, source_target_pairs={{0,2},{1,3},{2,0},{3,1},{4,6},{5,7},{6,4},{7,5},{8,10},{9,11},{10,... | collective-permute-start | bytes 55304 | tf_op jit(solution)/shard_map/ppermute | solution.py:33
  17.2 3.2 %collective-permute-start.8 = (bf16[24,384]{1,0:T(8,128)(2,1)S(1)}, bf16[24,384]{1,0:T(8,128)(2,1)S(1)}, u32[]{:S(2)}, u32[]{:S(2)}) collective-permute-start(bf16[24,384]{1,0:T(8,128)(2,1)S(1)} %get-tuple-element.39), channel_id=1, source_target_pairs={{0,3},{1,2},{2,1},{3,0},{4,7},{5,6},{6,5},{7,4},{8,11},{9,10},{10,... | collective-permute-start | bytes 55304 | tf_op jit(solution)/shard_map/ppermute | solution.py:33
  18.6 7.9 %copy-start.3 = (bf16[384,768]{1,0:T(8,128)(2,1)S(1)}, bf16[384,768]{1,0:T(8,128)(2,1)}, u32[]{:S(2)}) copy-start(bf16[384,768]{1,0:T(8,128)(2,1)} %refs_4_.1) | copy-start | bytes 1769476
  18.7 10.7 %copy-start.9 = (s32[2]{0:T(128)S(1)}, s32[2]{0:T(128)}, u32[]{:S(2)}) copy-start(s32[2]{0:T(128)} %order.1) | copy-start | bytes 28
  18.7 12.6 %copy-start.4 = (bf16[384,768]{1,0:T(8,128)(2,1)S(1)}, bf16[384,768]{1,0:T(8,128)(2,1)}, u32[]{:S(2)}) copy-start(bf16[384,768]{1,0:T(8,128)(2,1)} %refs_9_.1) | copy-start | bytes 1769476
  20.4 20.2 %copy-start.12 = (f32[768]{0:T(1024)S(1)}, f32[768]{0:T(1024)}, u32[]{:S(2)}) copy-start(f32[768]{0:T(1024)} %param.21) | copy-start | bytes 9220
  20.4 20.2 %copy-start.5 = (bf16[192,768]{1,0:T(8,128)(2,1)S(1)}, bf16[192,768]{1,0:T(8,128)(2,1)}, u32[]{:S(2)}) copy-start(bf16[192,768]{1,0:T(8,128)(2,1)} %weight.7) | copy-start | bytes 884740
  21.4 20.9 %copy-start.6 = (bf16[768,192]{0,1:T(8,128)(2,1)S(1)}, bf16[768,192]{0,1:T(8,128)(2,1)}, u32[]{:S(2)}) copy-start(bf16[768,192]{0,1:T(8,128)(2,1)} %param.22) | copy-start | bytes 884740
  21.5 20.9 %copy-start.7 = (bf16[768,192]{0,1:T(8,128)(2,1)S(1)}, bf16[768,192]{0,1:T(8,128)(2,1)}, u32[]{:S(2)}) copy-start(bf16[768,192]{0,1:T(8,128)(2,1)} %param.23) | copy-start | bytes 884740
  21.5 20.8 %copy-start.8 = (bf16[768,192]{0,1:T(8,128)(2,1)S(1)}, bf16[768,192]{0,1:T(8,128)(2,1)}, u32[]{:S(2)}) copy-start(bf16[768,192]{0,1:T(8,128)(2,1)} %param.24) | copy-start | bytes 884740
  21.5 3.8 %collective-permute-start.10 = (bf16[24,384]{1,0:T(8,128)(2,1)S(1)}, bf16[24,384]{1,0:T(8,128)(2,1)S(1)}, u32[]{:S(2)}, u32[]{:S(2)}) collective-permute-start(bf16[24,384]{1,0:T(8,128)(2,1)S(1)} %get-tuple-element.42), channel_id=1, source_target_pairs={{0,2},{1,3},{2,0},{3,1},{4,6},{5,7},{6,4},{7,5},{8,10},{9,11},{10,... | collective-permute-start | bytes 55304 | tf_op jit(solution)/shard_map/ppermute | solution.py:33
  22.6 3.3 %collective-permute-start.11 = (bf16[24,384]{1,0:T(8,128)(2,1)S(1)}, bf16[24,384]{1,0:T(8,128)(2,1)S(1)}, u32[]{:S(2)}, u32[]{:S(2)}) collective-permute-start(bf16[24,384]{1,0:T(8,128)(2,1)S(1)} %get-tuple-element.43), channel_id=1, source_target_pairs={{0,3},{1,2},{2,1},{3,0},{4,7},{5,6},{6,5},{7,4},{8,11},{9,10},{10,... | collective-permute-start | bytes 55304 | tf_op jit(solution)/shard_map/ppermute | solution.py:33
  25.3 1.2 %collective-permute-start.9 = (bf16[24,384]{1,0:T(8,128)(2,1)S(1)}, bf16[24,384]{1,0:T(8,128)(2,1)S(1)}, u32[]{:S(2)}, u32[]{:S(2)}) collective-permute-start(bf16[24,384]{1,0:T(8,128)(2,1)S(1)} %get-tuple-element.41), channel_id=1, source_target_pairs={{0,1},{1,0},{2,3},{3,2},{4,5},{5,4},{6,7},{7,6},{8,9},{9,8},{10,11... | collective-permute-start | bytes 55304 | tf_op jit(solution)/shard_map/ppermute | solution.py:33
  26.8 3.1 %collective-permute-start.12 = (bf16[8,768]{1,0:T(8,128)(2,1)S(1)}, bf16[8,768]{1,0:T(8,128)(2,1)S(1)}, u32[]{:S(2)}, u32[]{:S(2)}) collective-permute-start(bf16[8,768]{1,0:T(8,128)(2,1)S(1)} %shard_map.141.refs_0_.after), channel_id=1, source_target_pairs={{0,1},{1,0},{2,3},{3,2},{4,5},{5,4},{6,7},{7,6},{8,9},{9,8},{10,11... | collective-permute-start | bytes 36872 | tf_op jit(solution)/shard_map/ppermute | solution.py:33
  27.0 3.7 %collective-permute-start.13 = (bf16[8,768]{1,0:T(8,128)(2,1)S(1)}, bf16[8,768]{1,0:T(8,128)(2,1)S(1)}, u32[]{:S(2)}, u32[]{:S(2)}) collective-permute-start(bf16[8,768]{1,0:T(8,128)(2,1)S(1)} %shard_map.141.refs_0_.after), channel_id=1, source_target_pairs={{0,2},{1,3},{2,0},{3,1},{4,6},{5,7},{6,4},{7,5},{8,10},{9,11},{10,... | collective-permute-start | bytes 36872 | tf_op jit(solution)/shard_map/ppermute | solution.py:33
  28.1 3.1 %collective-permute-start.14 = (bf16[8,768]{1,0:T(8,128)(2,1)S(1)}, bf16[8,768]{1,0:T(8,128)(2,1)S(1)}, u32[]{:S(2)}, u32[]{:S(2)}) collective-permute-start(bf16[8,768]{1,0:T(8,128)(2,1)S(1)} %shard_map.141.refs_0_.after), channel_id=1, source_target_pairs={{0,3},{1,2},{2,1},{3,0},{4,7},{5,6},{6,5},{7,4},{8,11},{9,10},{10,... | collective-permute-start | bytes 36872 | tf_op jit(solution)/shard_map/ppermute | solution.py:33
  31.7 1.9 %collective-permute-start.18 = (bf16[8,896]{1,0:T(8,128)(2,1)S(1)}, bf16[8,896]{1,0:T(8,128)(2,1)S(1)}, u32[]{:S(2)}, u32[]{:S(2)}) collective-permute-start(bf16[8,896]{1,0:T(8,128)(2,1)S(1)} %shard_map.144.refs_1_), channel_id=1, source_target_pairs={{0,1},{1,0},{2,3},{3,2},{4,5},{5,4},{6,7},{7,6},{8,9},{9,8},{10,11... | collective-permute-start | bytes 43016 | tf_op jit(solution)/shard_map/ppermute | solution.py:33
  31.8 3.7 %collective-permute-start.19 = (bf16[8,896]{1,0:T(8,128)(2,1)S(1)}, bf16[8,896]{1,0:T(8,128)(2,1)S(1)}, u32[]{:S(2)}, u32[]{:S(2)}) collective-permute-start(bf16[8,896]{1,0:T(8,128)(2,1)S(1)} %shard_map.144.refs_1_), channel_id=1, source_target_pairs={{0,2},{1,3},{2,0},{3,1},{4,6},{5,7},{6,4},{7,5},{8,10},{9,11},{10,... | collective-permute-start | bytes 43016 | tf_op jit(solution)/shard_map/ppermute | solution.py:33
  32.7 3.1 %collective-permute-start.20 = (bf16[8,896]{1,0:T(8,128)(2,1)S(1)}, bf16[8,896]{1,0:T(8,128)(2,1)S(1)}, u32[]{:S(2)}, u32[]{:S(2)}) collective-permute-start(bf16[8,896]{1,0:T(8,128)(2,1)S(1)} %shard_map.144.refs_1_), channel_id=1, source_target_pairs={{0,3},{1,2},{2,1},{3,0},{4,7},{5,6},{6,5},{7,4},{8,11},{9,10},{10,... | collective-permute-start | bytes 43016 | tf_op jit(solution)/shard_map/ppermute | solution.py:33
  36.0 4.6 %collective-permute-start.21 = (bf16[8,896]{1,0:T(8,128)(2,1)S(1)}, bf16[8,896]{1,0:T(8,128)(2,1)S(1)}, u32[]{:S(2)}, u32[]{:S(2)}) collective-permute-start(bf16[8,896]{1,0:T(8,128)(2,1)S(1)} %shard_map.145.refs_0_), channel_id=1, source_target_pairs={{0,8},{1,13},{2,10},{3,15},{4,12},{5,9},{6,14},{7,11},{8,0},{9,5},... | collective-permute-start | bytes 43016 | tf_op jit(solution)/shard_map/ppermute | solution.py:49
  38.6 3.7 %collective-permute-start.23 = (bf16[8,896]{1,0:T(8,128)(2,1)S(1)}, bf16[8,896]{1,0:T(8,128)(2,1)S(1)}, u32[]{:S(2)}, u32[]{:S(2)}) collective-permute-start(bf16[8,896]{1,0:T(8,128)(2,1)S(1)} %shard_map.145.refs_0_), channel_id=1, source_target_pairs={{0,4},{4,0},{8,12},{12,8},{1,5},{5,1},{9,13},{13,9},{2,6},{6,2},{1... | collective-permute-start | bytes 43016 | tf_op jit(solution)/shard_map/ppermute | solution.py:33
  40.6 1.7 %collective-permute-start.22 = (bf16[8,896]{1,0:T(8,128)(2,1)S(1)}, bf16[8,896]{1,0:T(8,128)(2,1)S(1)}, u32[]{:S(2)}, u32[]{:S(2)}) collective-permute-start(bf16[8,896]{1,0:T(8,128)(2,1)S(1)} %collective-permute-done.21.refs_1_), channel_id=1, source_target_pairs={{0,1},{1,0},{2,3},{3,2},{4,5},{5,4},{6,7},{7,6},{8,9},{9,8},{10,11... | collective-permute-start | bytes 43016 | tf_op jit(solution)/shard_map/ppermute | solution.py:33
  43.4 2.2 %collective-permute-start.24 = (bf16[8,192]{1,0:T(8,128)(2,1)S(1)}, bf16[8,192]{1,0:T(8,128)(2,1)S(1)}, u32[]{:S(2)}, u32[]{:S(2)}) collective-permute-start(bf16[8,192]{1,0:T(8,128)(2,1)S(1)} %get-tuple-element.54), channel_id=1, source_target_pairs={{0,1},{1,0},{2,3},{3,2},{4,5},{5,4},{6,7},{7,6},{8,9},{9,8},{10,11... | collective-permute-start | bytes 9224 | tf_op jit(solution)/shard_map/ppermute | solution.py:33
  43.5 3.7 %collective-permute-start.25 = (bf16[8,192]{1,0:T(8,128)(2,1)S(1)}, bf16[8,192]{1,0:T(8,128)(2,1)S(1)}, u32[]{:S(2)}, u32[]{:S(2)}) collective-permute-start(bf16[8,192]{1,0:T(8,128)(2,1)S(1)} %get-tuple-element.55), channel_id=1, source_target_pairs={{0,2},{1,3},{2,0},{3,1},{4,6},{5,7},{6,4},{7,5},{8,10},{9,11},{10,... | collective-permute-start | bytes 9224 | tf_op jit(solution)/shard_map/ppermute | solution.py:33
  44.6 3.0 %collective-permute-start.26 = (bf16[8,192]{1,0:T(8,128)(2,1)S(1)}, bf16[8,192]{1,0:T(8,128)(2,1)S(1)}, u32[]{:S(2)}, u32[]{:S(2)}) collective-permute-start(bf16[8,192]{1,0:T(8,128)(2,1)S(1)} %get-tuple-element.56), channel_id=1, source_target_pairs={{0,3},{1,2},{2,1},{3,0},{4,7},{5,6},{6,5},{7,4},{8,11},{9,10},{10,... | collective-permute-start | bytes 9224 | tf_op jit(solution)/shard_map/ppermute | solution.py:33

commit v5 on v4

--- a/solution.py
+++ b/solution.py
@@ -231,21 +231,21 @@
     out[...] = contract(collect.astype(F32).astype(BF16), kept, 1, 0).astype(BF16)
 
 
+def join_kernel(size, place, *refs):
+    blocks, out = refs[:size], refs[-1]
+    me = place[0] % size
+    depth = blocks[0].shape[0]
+    for step in range(size):
+        start = pl.multiple_of(source(me, step, size) * depth, 16)
+        out[pl.ds(start, depth), :] = blocks[step][...]
+
+
 def embed_kernel(size, place, *refs):
-    parts, blocks, (first, project, notes, out, weight) = (
-        refs[:size],
-        refs[size : 2 * size],
-        refs[2 * size :],
-    )
-    me = place[0] % size
+    parts, (weight, first, project, notes, out) = refs[:size], refs[size:]
     total = parts[0][...].astype(F32)
     for step in range(1, size):
         total = total + parts[step][...].astype(F32)
     pooled = total.astype(BF16)
-    depth = blocks[0].shape[0]
-    for step in range(size):
-        start = pl.multiple_of(source(me, step, size) * depth, 16)
-        weight[pl.ds(start, depth), :] = blocks[step][...]
     class_row = (first[...] + contract(pooled, weight[...], 1, 0)).astype(BF16)
     width = project.shape[1]
     out[:, :width] = contract(class_row, project[...], 1, 0).astype(BF16)
@@ -444,11 +444,14 @@
     )(place, *mixed, w_value)
     pooled_parts = spread(pooled_part, "fsdp")
 
+    out_weight = call(
+        functools.partial(join_kernel, size),
+        jax.ShapeDtypeStruct((vit_width, width // size), BF16),
+        specs=[pl.ANY],
+    )(place, *out_blocks, pooled_part)
     embed_part = call(
-        functools.partial(embed_kernel, size),
-        jax.ShapeDtypeStruct((count, model + LANES), BF16),
-        [pltpu.VMEM((vit_width, width // size), BF16)],
-    )(place, *pooled_parts, *out_blocks, first, w_proj, notes)
+        functools.partial(embed_kernel, size), jax.ShapeDtypeStruct((count, model + LANES), BF16)
+    )(place, *pooled_parts, out_weight, first, w_proj, notes)
     embed_parts = spread(embed_part, "fsdp")
 
     group_tiles = call(

time: 48.4 us -> 48.4 us (level)
    pallas_call x14 -> x15, Pallas kernels: 5.78 us -> 5.78 us  [run(): pl.pallas_call(body, out_shape=outs, in_specs=[smem] + [vmem] * last + [p...]
where the time goes in v5:
time: 48.4 us; the launch traced here: 48.2 us
  starting transfers between devices  21.7 us (45%)
  waiting for transfers between devices  17.4 us (36%)
  Pallas kernels  6.75 us (14%)
  other arithmetic  1.37 us (3%)
  between operations  0.88 us (2%)
    ppermute x26, starting transfers between devices, swap(): lax.ppermute(array, axis, [(i, other(i, step, size)) for i in range(size)])  19.1 us
    ppermute x26, waiting for transfers between devices, swap(): lax.ppermute(array, axis, [(i, other(i, step, size)) for i in range(size)])  16.9 us
    pallas_call x15, Pallas kernels, run(): pl.pallas_call(body, out_shape=outs, in_specs=[smem] + [vmem] * last + [p...  5.78 us
    ppermute x1, starting transfers between devices, rows_of_all(): far = lax.ppermute(array, ('seq', 'fsdp'), pairs)  2.59 us
  transfers between devices with their start and end apart: 27, of which 15 were waited for; matrix products, arithmetic and copies ran while one was open for 3% of the time, Pallas kernels for 7%

profile of v5, /device:TPU:0, one launch (start us, length us, event | category | flops | bytes accessed | tf_op | source)
XLA Modules:
  0.0 48.2 jit_solution(17689412029431905761)
XLA Ops:
  0.0 1.0 %head.1.after.refs_0_ = bf16[2,1536]{1,0:T(2,128)(2,1)S(1)} custom-call(bf16[2,256,1536]{2,1,0:T(8,128)(2,1)} %tokens.1), custom_call_target="tpu_custom_call" | custom-call | tf_op jit(solution)/shard_map/head/pallas_call | solution.py:367
  1.0 0.0 copy-start.11
  1.0 0.1 copy-done
  1.1 0.1 shard_map.136
  1.2 0.6 %collective-permute-start.3 = (bf16[384,384]{1,0:T(8,128)(2,1)S(1)}, bf16[384,384]{1,0:T(8,128)(2,1)S(1)}, u32[]{:S(2)}, u32[]{:S(2)}) collective-permute-start(bf16[384,384]{1,0:T(8,128)(2,1)S(1)} %get-tuple-element.32), channel_id=1, source_target_pairs={{0,1},{1,0},{2,3},{3,2},{4,5},{5,4},{6,7},{7,6},{8,9},{9,8},{10,11... | collective-permute-start | bytes 884744 | tf_op jit(solution)/shard_map/ppermute | solution.py:33
  1.8 0.1 collective-permute-start
  1.8 2.9 %collective-permute-start.1 = (bf16[2,1536]{1,0:T(2,128)(2,1)S(1)}, bf16[2,1536]{1,0:T(2,128)(2,1)S(1)}, u32[]{:S(2)}, u32[]{:S(2)}) collective-permute-start(bf16[2,1536]{1,0:T(2,128)(2,1)S(1)} %head.1.after.refs_0_), channel_id=1, source_target_pairs={{0,2},{1,3},{2,0},{3,1},{4,6},{5,7},{6,4},{7,5},{8,10},{9,11},{10,... | collective-permute-start | bytes 18440 | tf_op jit(solution)/shard_map/ppermute | solution.py:33
  4.7 0.1 shard_map.142
  4.9 0.2 collective-permute-start.15
  5.0 0.3 convert_reduce_fusion
  5.3 0.0 collective-permute-done.refs_1_
  5.4 2.1 %collective-permute-start.16 = (bf16[192,384]{1,0:T(8,128)(2,1)S(1)}, bf16[192,384]{1,0:T(8,128)(2,1)S(1)}, u32[]{:S(2)}, u32[]{:S(2)}) collective-permute-start(bf16[192,384]{1,0:T(8,128)(2,1)S(1)} %get-tuple-element.46), channel_id=1, source_target_pairs={{0,2},{1,3},{2,0},{3,1},{4,6},{5,7},{6,4},{7,5},{8,10},{9,11},{10,... | collective-permute-start | bytes 442376 | tf_op jit(solution)/shard_map/ppermute | solution.py:33
  7.4 0.0 collective-permute-done.1.refs_2_
  7.5 0.4 collective-permute-done.2.refs_3_
  7.8 0.0 collective-permute-done.3.refs_6_
  7.8 0.4 shard_map.137
  8.2 0.1 shard_map.138
  8.4 0.7 %collective-permute-start.5 = (bf16[384,384]{1,0:T(8,128)(2,1)S(1)}, bf16[384,384]{1,0:T(8,128)(2,1)S(1)}, u32[]{:S(2)}, u32[]{:S(2)}) collective-permute-start(bf16[384,384]{1,0:T(8,128)(2,1)S(1)} %get-tuple-element.35), channel_id=1, source_target_pairs={{0,1},{1,0},{2,3},{3,2},{4,5},{5,4},{6,7},{7,6},{8,9},{9,8},{10,11... | collective-permute-start | bytes 884744 | tf_op jit(solution)/shard_map/ppermute | solution.py:33
  9.1 1.1 %collective-permute-start.4 = (f32[8,384]{1,0:T(8,128)S(1)}, f32[8,384]{1,0:T(8,128)S(1)}, u32[]{:S(2)}, u32[]{:S(2)}) collective-permute-start(f32[8,384]{1,0:T(8,128)S(1)} %get-tuple-element.33.after.refs_0_), channel_id=1, source_target_pairs={{0,2},{1,3},{2,0},{3,1},{4,6},{5,7},{6,4},{7,5},{8,10},{9,11},{10,... | collective-permute-start | bytes 36872 | tf_op jit(solution)/shard_map/ppermute | solution.py:33
  10.2 0.5 %fusion.2 = f32[2,256]{1,0:T(2,128)S(1)} fusion(bf16[2,256,1536]{2,1,0:T(8,128)(2,1)S(1)} %copy-done.10, f32[2,256]{1,0:T(2,128)S(1)} %broadcast_multiply_fusion), kind=kLoop, calls=%fused_computation.4 | loop fusion | flops 3145216 | bytes 1576960 | tf_op jit(solution)/shard_map/reduce_sum | solution.py:62
  10.7 4.2 %collective-permute-done.4.refs_1_ = f32[8,384]{1,0:T(8,128)S(1)} collective-permute-done((f32[8,384]{1,0:T(8,128)S(1)}, f32[8,384]{1,0:T(8,128)S(1)}, u32[]{:S(2)}, u32[]{:S(2)}) %collective-permute-start.4) | collective-permute-done | bytes 12320 | tf_op jit(solution)/shard_map/ppermute | solution.py:33
  15.0 0.4 shard_map.139
  15.4 0.1 collective-permute-start.6
  15.5 1.7 %collective-permute-start.7 = (bf16[24,384]{1,0:T(8,128)(2,1)S(1)}, bf16[24,384]{1,0:T(8,128)(2,1)S(1)}, u32[]{:S(2)}, u32[]{:S(2)}) collective-permute-start(bf16[24,384]{1,0:T(8,128)(2,1)S(1)} %get-tuple-element.38), channel_id=1, source_target_pairs={{0,2},{1,3},{2,0},{3,1},{4,6},{5,7},{6,4},{7,5},{8,10},{9,11},{10,... | collective-permute-start | bytes 55304 | tf_op jit(solution)/shard_map/ppermute | solution.py:33
  17.2 0.9 %collective-permute-start.8 = (bf16[24,384]{1,0:T(8,128)(2,1)S(1)}, bf16[24,384]{1,0:T(8,128)(2,1)S(1)}, u32[]{:S(2)}, u32[]{:S(2)}) collective-permute-start(bf16[24,384]{1,0:T(8,128)(2,1)S(1)} %get-tuple-element.39), channel_id=1, source_target_pairs={{0,3},{1,2},{2,1},{3,0},{4,7},{5,6},{6,5},{7,4},{8,11},{9,10},{10,... | collective-permute-start | bytes 55304 | tf_op jit(solution)/shard_map/ppermute | solution.py:33
  18.1 0.5 %fusion.4.refs_4_ = bf16[2,256,1536]{2,1,0:T(8,128)(2,1)S(1)} fusion(bf16[2,256,1536]{2,1,0:T(8,128)(2,1)S(1)} %copy-done.10, f32[1536]{0:T(1024)S(1)} %copy-done.11, f32[2,256]{1,0:T(2,128)S(1)} %add_rsqrt_fusion, f32[2,256]{1,0:T(2,128)S(1)} %broadcast_multiply_fusion), kind=kLoop, calls=%fused_computation.6 | loop fusion | flops 3932160 | bytes 3155968 | tf_op jit(solution)/shard_map/convert_element_type | solution.py:63
  18.6 0.0 copy-start.3
  18.7 0.0 copy-start.9
  18.7 0.7 %collective-permute-done.7.refs_2_ = bf16[24,384]{1,0:T(8,128)(2,1)S(1)} collective-permute-done((bf16[24,384]{1,0:T(8,128)(2,1)S(1)}, bf16[24,384]{1,0:T(8,128)(2,1)S(1)}, u32[]{:S(2)}, u32[]{:S(2)}) %collective-permute-start.7) | collective-permute-done | bytes 18464 | tf_op jit(solution)/shard_map/ppermute | solution.py:33
  19.3 1.1 %collective-permute-done.8.refs_3_ = bf16[24,384]{1,0:T(8,128)(2,1)S(1)} collective-permute-done((bf16[24,384]{1,0:T(8,128)(2,1)S(1)}, bf16[24,384]{1,0:T(8,128)(2,1)S(1)}, u32[]{:S(2)}, u32[]{:S(2)}) %collective-permute-start.8) | collective-permute-done | bytes 18464 | tf_op jit(solution)/shard_map/ppermute | solution.py:33
  20.4 1.0 %shard_map.140 = (bf16[24,384]{1,0:T(8,128)(2,1)S(1)}, bf16[24,384]{1,0:T(8,128)(2,1)S(1)}, bf16[24,384]{1,0:T(8,128)(2,1)S(1)}, bf16[24,384]{1,0:T(8,128)(2,1)S(1)}) custom-call(s32[1]{0:T(128)} %bitcast.place.refs_0_, bf16[24,384]{1,0:T(8,128)(2,1)S(1)} %get-tuple-element.36.refs_0_, bf16[24,384]{1,0:T(8,128)(2,1)S(1)} %collective-permute-done.6.refs_1_, ...), custom_call_target="tpu_custom_call" | custom-call | tf_op jit(solution)/shard_map/pallas_call | solution.py:81
  21.4 1.2 %collective-permute-start.10 = (bf16[24,384]{1,0:T(8,128)(2,1)S(1)}, bf16[24,384]{1,0:T(8,128)(2,1)S(1)}, u32[]{:S(2)}, u32[]{:S(2)}) collective-permute-start(bf16[24,384]{1,0:T(8,128)(2,1)S(1)} %get-tuple-element.42), channel_id=1, source_target_pairs={{0,2},{1,3},{2,0},{3,1},{4,6},{5,7},{6,4},{7,5},{8,10},{9,11},{10,... | collective-permute-start | bytes 55304 | tf_op jit(solution)/shard_map/ppermute | solution.py:33
  22.6 0.4 collective-permute-start.11
  23.0 2.3 %collective-permute-done.10.refs_2_ = bf16[24,384]{1,0:T(8,128)(2,1)S(1)} collective-permute-done((bf16[24,384]{1,0:T(8,128)(2,1)S(1)}, bf16[24,384]{1,0:T(8,128)(2,1)S(1)}, u32[]{:S(2)}, u32[]{:S(2)}) %collective-permute-start.10) | collective-permute-done | bytes 18464 | tf_op jit(solution)/shard_map/ppermute | solution.py:33
  25.3 0.6 %collective-permute-done.11.refs_3_ = bf16[24,384]{1,0:T(8,128)(2,1)S(1)} collective-permute-done((bf16[24,384]{1,0:T(8,128)(2,1)S(1)}, bf16[24,384]{1,0:T(8,128)(2,1)S(1)}, u32[]{:S(2)}, u32[]{:S(2)}) %collective-permute-start.11) | collective-permute-done | bytes 18464 | tf_op jit(solution)/shard_map/ppermute | solution.py:33
  25.9 0.5 %collective-permute-done.9.refs_1_ = bf16[24,384]{1,0:T(8,128)(2,1)S(1)} collective-permute-done((bf16[24,384]{1,0:T(8,128)(2,1)S(1)}, bf16[24,384]{1,0:T(8,128)(2,1)S(1)}, u32[]{:S(2)}, u32[]{:S(2)}) %collective-permute-start.9) | collective-permute-done | bytes 18464 | tf_op jit(solution)/shard_map/ppermute | solution.py:33
  26.5 0.3 shard_map.141.refs_4_.refs_0_.after
  26.8 0.2 collective-permute-start.12
  27.1 1.1 %collective-permute-start.13 = (bf16[8,768]{1,0:T(8,128)(2,1)S(1)}, bf16[8,768]{1,0:T(8,128)(2,1)S(1)}, u32[]{:S(2)}, u32[]{:S(2)}) collective-permute-start(bf16[8,768]{1,0:T(8,128)(2,1)S(1)} %shard_map.141.refs_4_.refs_0_.after), channel_id=1, source_target_pairs={{0,2},{1,3},{2,0},{3,1},{4,6},{5,7},{6,4},{7,5},{8,10},{9,11},{10,... | collective-permute-start | bytes 36872 | tf_op jit(solution)/shard_map/ppermute | solution.py:33
  28.2 0.6 %collective-permute-start.14 = (bf16[8,768]{1,0:T(8,128)(2,1)S(1)}, bf16[8,768]{1,0:T(8,128)(2,1)S(1)}, u32[]{:S(2)}, u32[]{:S(2)}) collective-permute-start(bf16[8,768]{1,0:T(8,128)(2,1)S(1)} %shard_map.141.refs_4_.refs_0_.after), channel_id=1, source_target_pairs={{0,3},{1,2},{2,1},{3,0},{4,7},{5,6},{6,5},{7,4},{8,11},{9,10},{10,... | collective-permute-start | bytes 36872 | tf_op jit(solution)/shard_map/ppermute | solution.py:33
  29.4 0.6 %shard_map.144.refs_7_ = bf16[8,128]{1,0:T(8,128)(2,1)S(1)} custom-call(s32[1]{0:T(128)} %bitcast.place.refs_0_, s32[2]{0:T(128)S(1)} %copy-done.9, s32[1]{0:T(128)S(6)} %copy.15.counts, bf16[2,1536]{1,0:T(2,128)(2,1)S(1)} %head.1.after.refs_0_), custom_call_target="tpu_custom_call" | custom-call | tf_op jit(solution)/shard_map/pallas_call | solution.py:81
  30.0 0.1 shard_map.143.refs_4_
  30.1 0.7 %collective-permute-done.13.refs_2_ = bf16[8,768]{1,0:T(8,128)(2,1)S(1)} collective-permute-done((bf16[8,768]{1,0:T(8,128)(2,1)S(1)}, bf16[8,768]{1,0:T(8,128)(2,1)S(1)}, u32[]{:S(2)}, u32[]{:S(2)}) %collective-permute-start.13) | collective-permute-done | bytes 12320 | tf_op jit(solution)/shard_map/ppermute | solution.py:33
  30.7 0.5 %collective-permute-done.14.refs_3_ = bf16[8,768]{1,0:T(8,128)(2,1)S(1)} collective-permute-done((bf16[8,768]{1,0:T(8,128)(2,1)S(1)}, bf16[8,768]{1,0:T(8,128)(2,1)S(1)}, u32[]{:S(2)}, u32[]{:S(2)}) %collective-permute-start.14) | collective-permute-done | bytes 12320 | tf_op jit(solution)/shard_map/ppermute | solution.py:33
  31.3 0.4 shard_map.145.refs_1_
  31.6 0.1 collective-permute-start.18
  31.8 0.9 %collective-permute-start.19 = (bf16[8,896]{1,0:T(8,128)(2,1)S(1)}, bf16[8,896]{1,0:T(8,128)(2,1)S(1)}, u32[]{:S(2)}, u32[]{:S(2)}) collective-permute-start(bf16[8,896]{1,0:T(8,128)(2,1)S(1)} %shard_map.145.refs_1_), channel_id=1, source_target_pairs={{0,2},{1,3},{2,0},{3,1},{4,6},{5,7},{6,4},{7,5},{8,10},{9,11},{10,... | collective-permute-start | bytes 43016 | tf_op jit(solution)/shard_map/ppermute | solution.py:33
  32.7 0.8 %collective-permute-start.20 = (bf16[8,896]{1,0:T(8,128)(2,1)S(1)}, bf16[8,896]{1,0:T(8,128)(2,1)S(1)}, u32[]{:S(2)}, u32[]{:S(2)}) collective-permute-start(bf16[8,896]{1,0:T(8,128)(2,1)S(1)} %shard_map.145.refs_1_), channel_id=1, source_target_pairs={{0,3},{1,2},{2,1},{3,0},{4,7},{5,6},{6,5},{7,4},{8,11},{9,10},{10,... | collective-permute-start | bytes 43016 | tf_op jit(solution)/shard_map/ppermute | solution.py:33
  33.5 2.0 %collective-permute-done.19.refs_3_ = bf16[8,896]{1,0:T(8,128)(2,1)S(1)} collective-permute-done((bf16[8,896]{1,0:T(8,128)(2,1)S(1)}, bf16[8,896]{1,0:T(8,128)(2,1)S(1)}, u32[]{:S(2)}, u32[]{:S(2)}) %collective-permute-start.19) | collective-permute-done | bytes 14368 | tf_op jit(solution)/shard_map/ppermute | solution.py:33
  35.5 0.4 collective-permute-done.20.refs_4_
  35.9 0.1 shard_map.146.refs_0_
  35.9 2.6 %collective-permute-start.21 = (bf16[8,896]{1,0:T(8,128)(2,1)S(1)}, bf16[8,896]{1,0:T(8,128)(2,1)S(1)}, u32[]{:S(2)}, u32[]{:S(2)}) collective-permute-start(bf16[8,896]{1,0:T(8,128)(2,1)S(1)} %shard_map.146.refs_0_), channel_id=1, source_target_pairs={{0,8},{1,13},{2,10},{3,15},{4,12},{5,9},{6,14},{7,11},{8,0},{9,5},... | collective-permute-start | bytes 43016 | tf_op jit(solution)/shard_map/ppermute | solution.py:49
  38.5 1.6 %collective-permute-start.23 = (bf16[8,896]{1,0:T(8,128)(2,1)S(1)}, bf16[8,896]{1,0:T(8,128)(2,1)S(1)}, u32[]{:S(2)}, u32[]{:S(2)}) collective-permute-start(bf16[8,896]{1,0:T(8,128)(2,1)S(1)} %shard_map.146.refs_0_), channel_id=1, source_target_pairs={{0,4},{4,0},{8,12},{12,8},{1,5},{5,1},{9,13},{13,9},{2,6},{6,2},{1... | collective-permute-start | bytes 43016 | tf_op jit(solution)/shard_map/ppermute | solution.py:33
  40.1 0.5 collective-permute-done.21.refs_1_
  40.6 0.1 shard_map.147
  40.7 1.5 %collective-permute-done.23.refs_3_ = bf16[8,896]{1,0:T(8,128)(2,1)S(1)} collective-permute-done((bf16[8,896]{1,0:T(8,128)(2,1)S(1)}, bf16[8,896]{1,0:T(8,128)(2,1)S(1)}, u32[]{:S(2)}, u32[]{:S(2)}) %collective-permute-start.23) | collective-permute-done | bytes 14368 | tf_op jit(solution)/shard_map/ppermute | solution.py:33
  42.3 1.1 %shard_map.148 = (bf16[8,192]{1,0:T(8,128)(2,1)S(1)}, bf16[8,192]{1,0:T(8,128)(2,1)S(1)}, bf16[8,192]{1,0:T(8,128)(2,1)S(1)}, bf16[8,192]{1,0:T(8,128)(2,1)S(1)}) custom-call(s32[1]{0:T(128)} %bitcast.place.refs_0_, bf16[8,896]{1,0:T(8,128)(2,1)S(1)} %shard_map.146.refs_0_, bf16[8,896]{1,0:T(8,128)(2,1)S(1)} %collective-permute-done.21.refs_1_, ...), custom_call_target="tpu_custom_call" | custom-call | tf_op jit(solution)/shard_map/pallas_call | solution.py:81
  43.4 0.0 collective-permute-start.24
  43.5 1.2 %collective-permute-start.25 = (bf16[8,192]{1,0:T(8,128)(2,1)S(1)}, bf16[8,192]{1,0:T(8,128)(2,1)S(1)}, u32[]{:S(2)}, u32[]{:S(2)}) collective-permute-start(bf16[8,192]{1,0:T(8,128)(2,1)S(1)} %get-tuple-element.55), channel_id=1, source_target_pairs={{0,2},{1,3},{2,0},{3,1},{4,6},{5,7},{6,4},{7,5},{8,10},{9,11},{10,... | collective-permute-start | bytes 9224 | tf_op jit(solution)/shard_map/ppermute | solution.py:33
  44.6 0.7 %collective-permute-start.26 = (bf16[8,192]{1,0:T(8,128)(2,1)S(1)}, bf16[8,192]{1,0:T(8,128)(2,1)S(1)}, u32[]{:S(2)}, u32[]{:S(2)}) collective-permute-start(bf16[8,192]{1,0:T(8,128)(2,1)S(1)} %get-tuple-element.56), channel_id=1, source_target_pairs={{0,3},{1,2},{2,1},{3,0},{4,7},{5,6},{6,5},{7,4},{8,11},{9,10},{10,... | collective-permute-start | bytes 9224 | tf_op jit(solution)/shard_map/ppermute | solution.py:33
  45.3 0.3 shard_map.149.residual
  45.6 1.5 %collective-permute-done.25.refs_2_ = bf16[8,192]{1,0:T(8,128)(2,1)S(1)} collective-permute-done((bf16[8,192]{1,0:T(8,128)(2,1)S(1)}, bf16[8,192]{1,0:T(8,128)(2,1)S(1)}, u32[]{:S(2)}, u32[]{:S(2)}) %collective-permute-start.25) | collective-permute-done | bytes 3104 | tf_op jit(solution)/shard_map/ppermute | solution.py:33
  47.1 0.5 %collective-permute-done.26.refs_3_ = bf16[8,192]{1,0:T(8,128)(2,1)S(1)} collective-permute-done((bf16[8,192]{1,0:T(8,128)(2,1)S(1)}, bf16[8,192]{1,0:T(8,128)(2,1)S(1)}, u32[]{:S(2)}, u32[]{:S(2)}) %collective-permute-start.26) | collective-permute-done | bytes 3104 | tf_op jit(solution)/shard_map/ppermute | solution.py:33
  47.6 0.6 %shard_map.150 = bf16[8,192]{1,0:T(8,128)(2,1)} custom-call(s32[1]{0:T(128)} %bitcast.place.refs_0_, f32[8,192]{1,0:T(8,128)S(1)} %shard_map.149.residual, bf16[8,192]{1,0:T(8,128)(2,1)S(1)} %get-tuple-element.53.refs_4_.refs_0_, bf16[8,192]{1,0:T(8,128)(2,1)S(1)} %collective-permute-done.24.refs_1_, bf16[8,192]{1,0:T(8,128)(2,1)S(1)} %collective-permute-done.25.refs_2_, ...), custom_call_target="tpu_custom_call" | custom-call | tf_op jit(solution)/shard_map/pallas_call | solution.py:81
  (39 shorter events, 0.1 us)
Async XLA Ops:
  0.0 1.1 %copy-start = (bf16[384,768]{1,0:T(8,128)(2,1)S(1)}, bf16[384,768]{1,0:T(8,128)(2,1)}, u32[]{:S(2)}) copy-start(bf16[384,768]{1,0:T(8,128)(2,1)} %weight.4) | copy-start | bytes 1769476
  0.0 4.7 %copy-start.1 = (bf16[192,1536]{1,0:T(8,128)(2,1)S(1)}, bf16[192,1536]{1,0:T(8,128)(2,1)}, u32[]{:S(2)}) copy-start(bf16[192,1536]{1,0:T(8,128)(2,1)} %weight.6) | copy-start | bytes 1769476
  0.0 5.0 %copy-start.10 = (bf16[2,256,1536]{2,1,0:T(8,128)(2,1)S(1)}, bf16[2,256,1536]{2,1,0:T(8,128)(2,1)}, u32[]{:S(2)}) copy-start(bf16[2,256,1536]{2,1,0:T(8,128)(2,1)} %tokens.1) | copy-start | bytes 4718596
  1.0 4.3 %copy-start.11 = (f32[1536]{0:T(1024)S(1)}, f32[1536]{0:T(1024)}, u32[]{:S(2)}) copy-start(f32[1536]{0:T(1024)} %param.15) | copy-start | bytes 18436
  1.1 7.2 %copy-start.2 = (bf16[384,768]{1,0:T(8,128)(2,1)S(1)}, bf16[384,768]{1,0:T(8,128)(2,1)}, u32[]{:S(2)}) copy-start(bf16[384,768]{1,0:T(8,128)(2,1)} %weight.5) | copy-start | bytes 1769476
  1.2 6.6 %collective-permute-start.3 = (bf16[384,384]{1,0:T(8,128)(2,1)S(1)}, bf16[384,384]{1,0:T(8,128)(2,1)S(1)}, u32[]{:S(2)}, u32[]{:S(2)}) collective-permute-start(bf16[384,384]{1,0:T(8,128)(2,1)S(1)} %get-tuple-element.32), channel_id=1, source_target_pairs={{0,1},{1,0},{2,3},{3,2},{4,5},{5,4},{6,7},{7,6},{8,9},{9,8},{10,11... | collective-permute-start | bytes 884744 | tf_op jit(solution)/shard_map/ppermute | solution.py:33
  1.8 3.6 %collective-permute-start = (bf16[2,1536]{1,0:T(2,128)(2,1)S(1)}, bf16[2,1536]{1,0:T(2,128)(2,1)S(1)}, u32[]{:S(2)}, u32[]{:S(2)}) collective-permute-start(bf16[2,1536]{1,0:T(2,128)(2,1)S(1)} %head.1.after.refs_0_), channel_id=1, source_target_pairs={{0,1},{1,0},{2,3},{3,2},{4,5},{5,4},{6,7},{7,6},{8,9},{9,8},{10,11... | collective-permute-start | bytes 18440 | tf_op jit(solution)/shard_map/ppermute | solution.py:33
  1.8 5.6 %collective-permute-start.1 = (bf16[2,1536]{1,0:T(2,128)(2,1)S(1)}, bf16[2,1536]{1,0:T(2,128)(2,1)S(1)}, u32[]{:S(2)}, u32[]{:S(2)}) collective-permute-start(bf16[2,1536]{1,0:T(2,128)(2,1)S(1)} %head.1.after.refs_0_), channel_id=1, source_target_pairs={{0,2},{1,3},{2,0},{3,1},{4,6},{5,7},{6,4},{7,5},{8,10},{9,11},{10,... | collective-permute-start | bytes 18440 | tf_op jit(solution)/shard_map/ppermute | solution.py:33
  4.7 3.1 %collective-permute-start.2 = (bf16[2,1536]{1,0:T(2,128)(2,1)S(1)}, bf16[2,1536]{1,0:T(2,128)(2,1)S(1)}, u32[]{:S(2)}, u32[]{:S(2)}) collective-permute-start(bf16[2,1536]{1,0:T(2,128)(2,1)S(1)} %head.1.after.refs_0_), channel_id=1, source_target_pairs={{0,3},{1,2},{2,1},{3,0},{4,7},{5,6},{6,5},{7,4},{8,11},{9,10},{10,... | collective-permute-start | bytes 18440 | tf_op jit(solution)/shard_map/ppermute | solution.py:33
  4.9 23.3 %collective-permute-start.15 = (bf16[192,384]{1,0:T(8,128)(2,1)S(1)}, bf16[192,384]{1,0:T(8,128)(2,1)S(1)}, u32[]{:S(2)}, u32[]{:S(2)}) collective-permute-start(bf16[192,384]{1,0:T(8,128)(2,1)S(1)} %get-tuple-element.45), channel_id=1, source_target_pairs={{0,1},{1,0},{2,3},{3,2},{4,5},{5,4},{6,7},{7,6},{8,9},{9,8},{10,11... | collective-permute-start | bytes 442376 | tf_op jit(solution)/shard_map/ppermute | solution.py:33
  5.4 24.6 %collective-permute-start.16 = (bf16[192,384]{1,0:T(8,128)(2,1)S(1)}, bf16[192,384]{1,0:T(8,128)(2,1)S(1)}, u32[]{:S(2)}, u32[]{:S(2)}) collective-permute-start(bf16[192,384]{1,0:T(8,128)(2,1)S(1)} %get-tuple-element.46), channel_id=1, source_target_pairs={{0,2},{1,3},{2,0},{3,1},{4,6},{5,7},{6,4},{7,5},{8,10},{9,11},{10,... | collective-permute-start | bytes 442376 | tf_op jit(solution)/shard_map/ppermute | solution.py:33
  7.4 22.6 %collective-permute-start.17 = (bf16[192,384]{1,0:T(8,128)(2,1)S(1)}, bf16[192,384]{1,0:T(8,128)(2,1)S(1)}, u32[]{:S(2)}, u32[]{:S(2)}) collective-permute-start(bf16[192,384]{1,0:T(8,128)(2,1)S(1)} %get-tuple-element.47), channel_id=1, source_target_pairs={{0,3},{1,2},{2,1},{3,0},{4,7},{5,6},{6,5},{7,4},{8,11},{9,10},{10,... | collective-permute-start | bytes 442376 | tf_op jit(solution)/shard_map/ppermute | solution.py:33
  8.4 6.6 %collective-permute-start.5 = (bf16[384,384]{1,0:T(8,128)(2,1)S(1)}, bf16[384,384]{1,0:T(8,128)(2,1)S(1)}, u32[]{:S(2)}, u32[]{:S(2)}) collective-permute-start(bf16[384,384]{1,0:T(8,128)(2,1)S(1)} %get-tuple-element.35), channel_id=1, source_target_pairs={{0,1},{1,0},{2,3},{3,2},{4,5},{5,4},{6,7},{7,6},{8,9},{9,8},{10,11... | collective-permute-start | bytes 884744 | tf_op jit(solution)/shard_map/ppermute | solution.py:33
  9.1 5.9 %collective-permute-start.4 = (f32[8,384]{1,0:T(8,128)S(1)}, f32[8,384]{1,0:T(8,128)S(1)}, u32[]{:S(2)}, u32[]{:S(2)}) collective-permute-start(f32[8,384]{1,0:T(8,128)S(1)} %get-tuple-element.33.after.refs_0_), channel_id=1, source_target_pairs={{0,2},{1,3},{2,0},{3,1},{4,6},{5,7},{6,4},{7,5},{8,10},{9,11},{10,... | collective-permute-start | bytes 36872 | tf_op jit(solution)/shard_map/ppermute | solution.py:33
  15.4 1.8 %collective-permute-start.6 = (bf16[24,384]{1,0:T(8,128)(2,1)S(1)}, bf16[24,384]{1,0:T(8,128)(2,1)S(1)}, u32[]{:S(2)}, u32[]{:S(2)}) collective-permute-start(bf16[24,384]{1,0:T(8,128)(2,1)S(1)} %get-tuple-element.37), channel_id=1, source_target_pairs={{0,1},{1,0},{2,3},{3,2},{4,5},{5,4},{6,7},{7,6},{8,9},{9,8},{10,11... | collective-permute-start | bytes 55304 | tf_op jit(solution)/shard_map/ppermute | solution.py:33
  15.5 3.8 %collective-permute-start.7 = (bf16[24,384]{1,0:T(8,128)(2,1)S(1)}, bf16[24,384]{1,0:T(8,128)(2,1)S(1)}, u32[]{:S(2)}, u32[]{:S(2)}) collective-permute-start(bf16[24,384]{1,0:T(8,128)(2,1)S(1)} %get-tuple-element.38), channel_id=1, source_target_pairs={{0,2},{1,3},{2,0},{3,1},{4,6},{5,7},{6,4},{7,5},{8,10},{9,11},{10,... | collective-permute-start | bytes 55304 | tf_op jit(solution)/shard_map/ppermute | solution.py:33
  17.2 3.2 %collective-permute-start.8 = (bf16[24,384]{1,0:T(8,128)(2,1)S(1)}, bf16[24,384]{1,0:T(8,128)(2,1)S(1)}, u32[]{:S(2)}, u32[]{:S(2)}) collective-permute-start(bf16[24,384]{1,0:T(8,128)(2,1)S(1)} %get-tuple-element.39), channel_id=1, source_target_pairs={{0,3},{1,2},{2,1},{3,0},{4,7},{5,6},{6,5},{7,4},{8,11},{9,10},{10,... | collective-permute-start | bytes 55304 | tf_op jit(solution)/shard_map/ppermute | solution.py:33
  18.6 7.8 %copy-start.3 = (bf16[384,768]{1,0:T(8,128)(2,1)S(1)}, bf16[384,768]{1,0:T(8,128)(2,1)}, u32[]{:S(2)}) copy-start(bf16[384,768]{1,0:T(8,128)(2,1)} %refs_4_.1) | copy-start | bytes 1769476
  18.7 10.8 %copy-start.9 = (s32[2]{0:T(128)S(1)}, s32[2]{0:T(128)}, u32[]{:S(2)}) copy-start(s32[2]{0:T(128)} %order.1) | copy-start | bytes 28
  20.4 10.9 %copy-start.4 = (bf16[384,768]{1,0:T(8,128)(2,1)S(1)}, bf16[384,768]{1,0:T(8,128)(2,1)}, u32[]{:S(2)}) copy-start(bf16[384,768]{1,0:T(8,128)(2,1)} %refs_6_.1) | copy-start | bytes 1769476
  21.4 3.8 %collective-permute-start.10 = (bf16[24,384]{1,0:T(8,128)(2,1)S(1)}, bf16[24,384]{1,0:T(8,128)(2,1)S(1)}, u32[]{:S(2)}, u32[]{:S(2)}) collective-permute-start(bf16[24,384]{1,0:T(8,128)(2,1)S(1)} %get-tuple-element.42), channel_id=1, source_target_pairs={{0,2},{1,3},{2,0},{3,1},{4,6},{5,7},{6,4},{7,5},{8,10},{9,11},{10,... | collective-permute-start | bytes 55304 | tf_op jit(solution)/shard_map/ppermute | solution.py:33
  22.6 3.3 %collective-permute-start.11 = (bf16[24,384]{1,0:T(8,128)(2,1)S(1)}, bf16[24,384]{1,0:T(8,128)(2,1)S(1)}, u32[]{:S(2)}, u32[]{:S(2)}) collective-permute-start(bf16[24,384]{1,0:T(8,128)(2,1)S(1)} %get-tuple-element.43), channel_id=1, source_target_pairs={{0,3},{1,2},{2,1},{3,0},{4,7},{5,6},{6,5},{7,4},{8,11},{9,10},{10,... | collective-permute-start | bytes 55304 | tf_op jit(solution)/shard_map/ppermute | solution.py:33
  25.3 1.2 %collective-permute-start.9 = (bf16[24,384]{1,0:T(8,128)(2,1)S(1)}, bf16[24,384]{1,0:T(8,128)(2,1)S(1)}, u32[]{:S(2)}, u32[]{:S(2)}) collective-permute-start(bf16[24,384]{1,0:T(8,128)(2,1)S(1)} %get-tuple-element.41), channel_id=1, source_target_pairs={{0,1},{1,0},{2,3},{3,2},{4,5},{5,4},{6,7},{7,6},{8,9},{9,8},{10,11... | collective-permute-start | bytes 55304 | tf_op jit(solution)/shard_map/ppermute | solution.py:33
  26.5 14.1 %copy-start.12 = (f32[768]{0:T(1024)S(1)}, f32[768]{0:T(1024)}, u32[]{:S(2)}) copy-start(f32[768]{0:T(1024)} %param.21) | copy-start | bytes 9220
  26.5 14.1 %copy-start.5 = (bf16[192,768]{1,0:T(8,128)(2,1)S(1)}, bf16[192,768]{1,0:T(8,128)(2,1)}, u32[]{:S(2)}) copy-start(bf16[192,768]{1,0:T(8,128)(2,1)} %weight.7) | copy-start | bytes 884740
  26.8 15.5 %copy-start.6 = (bf16[768,192]{0,1:T(8,128)(2,1)S(1)}, bf16[768,192]{0,1:T(8,128)(2,1)}, u32[]{:S(2)}) copy-start(bf16[768,192]{0,1:T(8,128)(2,1)} %param.22) | copy-start | bytes 884740
  26.8 15.5 %copy-start.7 = (bf16[768,192]{0,1:T(8,128)(2,1)S(1)}, bf16[768,192]{0,1:T(8,128)(2,1)}, u32[]{:S(2)}) copy-start(bf16[768,192]{0,1:T(8,128)(2,1)} %param.23) | copy-start | bytes 884740
  26.8 15.5 %copy-start.8 = (bf16[768,192]{0,1:T(8,128)(2,1)S(1)}, bf16[768,192]{0,1:T(8,128)(2,1)}, u32[]{:S(2)}) copy-start(bf16[768,192]{0,1:T(8,128)(2,1)} %param.24) | copy-start | bytes 884740
  26.8 3.3 %collective-permute-start.12 = (bf16[8,768]{1,0:T(8,128)(2,1)S(1)}, bf16[8,768]{1,0:T(8,128)(2,1)S(1)}, u32[]{:S(2)}, u32[]{:S(2)}) collective-permute-start(bf16[8,768]{1,0:T(8,128)(2,1)S(1)} %shard_map.141.refs_4_.refs_0_.after), channel_id=1, source_target_pairs={{0,1},{1,0},{2,3},{3,2},{4,5},{5,4},{6,7},{7,6},{8,9},{9,8},{10,11... | collective-permute-start | bytes 36872 | tf_op jit(solution)/shard_map/ppermute | solution.py:33
  27.1 3.7 %collective-permute-start.13 = (bf16[8,768]{1,0:T(8,128)(2,1)S(1)}, bf16[8,768]{1,0:T(8,128)(2,1)S(1)}, u32[]{:S(2)}, u32[]{:S(2)}) collective-permute-start(bf16[8,768]{1,0:T(8,128)(2,1)S(1)} %shard_map.141.refs_4_.refs_0_.after), channel_id=1, source_target_pairs={{0,2},{1,3},{2,0},{3,1},{4,6},{5,7},{6,4},{7,5},{8,10},{9,11},{10,... | collective-permute-start | bytes 36872 | tf_op jit(solution)/shard_map/ppermute | solution.py:33
  28.2 3.1 %collective-permute-start.14 = (bf16[8,768]{1,0:T(8,128)(2,1)S(1)}, bf16[8,768]{1,0:T(8,128)(2,1)S(1)}, u32[]{:S(2)}, u32[]{:S(2)}) collective-permute-start(bf16[8,768]{1,0:T(8,128)(2,1)S(1)} %shard_map.141.refs_4_.refs_0_.after), channel_id=1, source_target_pairs={{0,3},{1,2},{2,1},{3,0},{4,7},{5,6},{6,5},{7,4},{8,11},{9,10},{10,... | collective-permute-start | bytes 36872 | tf_op jit(solution)/shard_map/ppermute | solution.py:33
  31.6 1.9 %collective-permute-start.18 = (bf16[8,896]{1,0:T(8,128)(2,1)S(1)}, bf16[8,896]{1,0:T(8,128)(2,1)S(1)}, u32[]{:S(2)}, u32[]{:S(2)}) collective-permute-start(bf16[8,896]{1,0:T(8,128)(2,1)S(1)} %shard_map.145.refs_1_), channel_id=1, source_target_pairs={{0,1},{1,0},{2,3},{3,2},{4,5},{5,4},{6,7},{7,6},{8,9},{9,8},{10,11... | collective-permute-start | bytes 43016 | tf_op jit(solution)/shard_map/ppermute | solution.py:33
  31.8 3.7 %collective-permute-start.19 = (bf16[8,896]{1,0:T(8,128)(2,1)S(1)}, bf16[8,896]{1,0:T(8,128)(2,1)S(1)}, u32[]{:S(2)}, u32[]{:S(2)}) collective-permute-start(bf16[8,896]{1,0:T(8,128)(2,1)S(1)} %shard_map.145.refs_1_), channel_id=1, source_target_pairs={{0,2},{1,3},{2,0},{3,1},{4,6},{5,7},{6,4},{7,5},{8,10},{9,11},{10,... | collective-permute-start | bytes 43016 | tf_op jit(solution)/shard_map/ppermute | solution.py:33
  32.7 3.1 %collective-permute-start.20 = (bf16[8,896]{1,0:T(8,128)(2,1)S(1)}, bf16[8,896]{1,0:T(8,128)(2,1)S(1)}, u32[]{:S(2)}, u32[]{:S(2)}) collective-permute-start(bf16[8,896]{1,0:T(8,128)(2,1)S(1)} %shard_map.145.refs_1_), channel_id=1, source_target_pairs={{0,3},{1,2},{2,1},{3,0},{4,7},{5,6},{6,5},{7,4},{8,11},{9,10},{10,... | collective-permute-start | bytes 43016 | tf_op jit(solution)/shard_map/ppermute | solution.py:33
  35.9 4.6 %collective-permute-start.21 = (bf16[8,896]{1,0:T(8,128)(2,1)S(1)}, bf16[8,896]{1,0:T(8,128)(2,1)S(1)}, u32[]{:S(2)}, u32[]{:S(2)}) collective-permute-start(bf16[8,896]{1,0:T(8,128)(2,1)S(1)} %shard_map.146.refs_0_), channel_id=1, source_target_pairs={{0,8},{1,13},{2,10},{3,15},{4,12},{5,9},{6,14},{7,11},{8,0},{9,5},... | collective-permute-start | bytes 43016 | tf_op jit(solution)/shard_map/ppermute | solution.py:49
  38.5 3.7 %collective-permute-start.23 = (bf16[8,896]{1,0:T(8,128)(2,1)S(1)}, bf16[8,896]{1,0:T(8,128)(2,1)S(1)}, u32[]{:S(2)}, u32[]{:S(2)}) collective-permute-start(bf16[8,896]{1,0:T(8,128)(2,1)S(1)} %shard_map.146.refs_0_), channel_id=1, source_target_pairs={{0,4},{4,0},{8,12},{12,8},{1,5},{5,1},{9,13},{13,9},{2,6},{6,2},{1... | collective-permute-start | bytes 43016 | tf_op jit(solution)/shard_map/ppermute | solution.py:33
  40.6 1.7 %collective-permute-start.22 = (bf16[8,896]{1,0:T(8,128)(2,1)S(1)}, bf16[8,896]{1,0:T(8,128)(2,1)S(1)}, u32[]{:S(2)}, u32[]{:S(2)}) collective-permute-start(bf16[8,896]{1,0:T(8,128)(2,1)S(1)} %collective-permute-done.21.refs_1_), channel_id=1, source_target_pairs={{0,1},{1,0},{2,3},{3,2},{4,5},{5,4},{6,7},{7,6},{8,9},{9,8},{10,11... | collective-permute-start | bytes 43016 | tf_op jit(solution)/shard_map/ppermute | solution.py:33
  43.4 2.2 %collective-permute-start.24 = (bf16[8,192]{1,0:T(8,128)(2,1)S(1)}, bf16[8,192]{1,0:T(8,128)(2,1)S(1)}, u32[]{:S(2)}, u32[]{:S(2)}) collective-permute-start(bf16[8,192]{1,0:T(8,128)(2,1)S(1)} %get-tuple-element.54), channel_id=1, source_target_pairs={{0,1},{1,0},{2,3},{3,2},{4,5},{5,4},{6,7},{7,6},{8,9},{9,8},{10,11... | collective-permute-start | bytes 9224 | tf_op jit(solution)/shard_map/ppermute | solution.py:33
  43.5 3.7 %collective-permute-start.25 = (bf16[8,192]{1,0:T(8,128)(2,1)S(1)}, bf16[8,192]{1,0:T(8,128)(2,1)S(1)}, u32[]{:S(2)}, u32[]{:S(2)}) collective-permute-start(bf16[8,192]{1,0:T(8,128)(2,1)S(1)} %get-tuple-element.55), channel_id=1, source_target_pairs={{0,2},{1,3},{2,0},{3,1},{4,6},{5,7},{6,4},{7,5},{8,10},{9,11},{10,... | collective-permute-start | bytes 9224 | tf_op jit(solution)/shard_map/ppermute | solution.py:33
  44.6 3.0 %collective-permute-start.26 = (bf16[8,192]{1,0:T(8,128)(2,1)S(1)}, bf16[8,192]{1,0:T(8,128)(2,1)S(1)}, u32[]{:S(2)}, u32[]{:S(2)}) collective-permute-start(bf16[8,192]{1,0:T(8,128)(2,1)S(1)} %get-tuple-element.56), channel_id=1, source_target_pairs={{0,3},{1,2},{2,1},{3,0},{4,7},{5,6},{6,5},{7,4},{8,11},{9,10},{10,... | collective-permute-start | bytes 9224 | tf_op jit(solution)/shard_map/ppermute | solution.py:33
